TPU v7x, 32 devices: a whole 2x2x4 slice. The times are simulated.
32 devices in a mesh: batch: 4 (over y, x), seq: 8 (over z, core).
Axes of the slice: x: 2, y: 2, z: 4, core: 2. Of those that a mesh axis runs over, the one named last changes fastest.
Arguments:
- frames: bfloat16 [4, 2048, 768], P('batch', 'seq'), may hold values from -6 to 6
- cotangent: bfloat16 [4, 2048, 768], P('batch', 'seq'), may hold values from -6 to 6
- modulation: float32 [4, 3, 6, 768], P('batch'), may hold values from -3 to 3
- lengths: int32 [4, 3], P('batch'), may hold values from 1 to 1024, 2048 in all within a row
- text: bfloat16 [4, 3, 256, 1024], P('batch'), may hold values from -6 to 6
- text_len: int32 [4, 3], P('batch'), may hold values from 80 to 256
- w_qkv: bfloat16 [768, 2304], replicated, may hold values from -0.21875 to 0.21875
- w_o: bfloat16 [768, 768], replicated, may hold values from -2.5 to 2.5
- w_cq: bfloat16 [768, 768], replicated, may hold values from -0.21875 to 0.21875
- w_ckv: bfloat16 [1024, 1536], replicated, may hold values from -0.1875 to 0.1875
- w_co: bfloat16 [768, 768], replicated, may hold values from -1.25 to 1.25
- w_up: bfloat16 [768, 3072], replicated, may hold values from -0.21875 to 0.21875
- w_down: bfloat16 [3072, 768], replicated, may hold values from -0.109375 to 0.109375
Outputs:
- out: bfloat16 [4, 2048, 768], P('batch', 'seq')
- frames_grad: float32 [4, 2048, 768], P('batch', 'seq')
- modulation_grad: float32 [4, 3, 3, 768], P('batch', None, None, 'seq')
- modulation_mlp_grad: float32 [4, 3, 3, 768], P('batch', None, None, 'seq')
- text_grad: float32 [4, 3, 256, 1024], P('batch', None, 'seq')
- w_qkv_grad: float32 [768, 2304], P('seq', 'batch')
- w_o_grad: float32 [768, 768], P('seq', 'batch')
- w_cq_grad: float32 [768, 768], P('seq', 'batch')
- w_ckv_grad: float32 [1024, 1536], P('seq', 'batch')
- w_co_grad: float32 [768, 768], P('seq', 'batch')
- w_up_grad: float32 [768, 3072], P('seq', 'batch')
- w_down_grad: float32 [3072, 768], P('seq', 'batch')
Inputs may be any that keep to these rules, and one draw needn't show every extreme that they name: The 3 lengths of a group sum to 2048, and the longest is exactly min(1024, 2048). text slots at or beyond text_len are padding.
All inputs are finite; a program needn't handle non-finite values.
Results may differ from a plain program's by a relative error of at most 0.025.
Values may be sent and summed in bfloat16 or wider, within the bound.
No kernel may reach another device: no remote copies, remote signals or barrier semaphores. Data moves between devices by JAX's collectives and lax.ppermute only.
A program may use at most 256 MiB of HBM per device.

v0:
```python
from functools import partial

import jax
import jax.numpy as jnp
from jax import lax
from jax.experimental import pallas as pl
from jax.experimental.pallas import tpu as pltpu
from jax.sharding import PartitionSpec as P

H = 12
LONGEST = 1024

epsilon = 1e-06
far = -1e30
LSE_LANE = 8
DELTA_LANE = 44
MIB = 1 << 20


def layer_norm(values):
    centred = values - jnp.mean(values, axis=-1, keepdims=True)
    inverse = lax.rsqrt(jnp.mean(centred * centred, axis=-1, keepdims=True) + epsilon)
    return (centred * inverse, inverse)


def norm_back(grad_normed, normed, inverse):
    return inverse * (
        grad_normed
        - jnp.mean(grad_normed, axis=-1, keepdims=True)
        - normed * jnp.mean(grad_normed * normed, axis=-1, keepdims=True)
    )


def contract_rows(left, right):
    return lax.dot_general(
        left, right, (((0,), (0,)), ((), ())), preferred_element_type=jnp.float32
    )


def times_transposed(left, right):
    return lax.dot_general(
        left, right, (((1,), (1,)), ((), ())), preferred_element_type=jnp.float32
    )


class Frame:
    def __init__(self, meta, items, count, shards):
        self.position = meta[0]
        self.items = items
        self.count = count
        self.shards = shards
        self.ends = []
        total = jnp.int32(0)
        for item in range(items):
            total = total + meta[1 + item]
            self.ends.append(total)
        self.text_len = [meta[1 + items + item] for item in range(items)]
        self.first = self.item_of(self.position * count)
        self.last = self.item_of(self.position * count + count - 1)
        self.low = jnp.int32(0)
        self.high = jnp.int32(0)
        for item in range(items):
            start = self.ends[item] - meta[1 + item]
            self.low = jnp.where(self.first == item, start, self.low)
            self.high = jnp.where(self.last == item, self.ends[item], self.high)

    def item_of(self, place):
        found = jnp.int32(0)
        for end in self.ends:
            found = found + (place >= end).astype(jnp.int32)
        return found

    def items_of_rows(self, base, rows):
        place = base + lax.broadcasted_iota(jnp.int32, (rows, 1), 0)
        found = jnp.zeros((rows, 1), jnp.int32)
        for end in self.ends:
            found = found + (place >= end).astype(jnp.int32)
        return found

    def base(self, block):
        pair = block // 2
        hop = (pair + 1) // 2
        step = jnp.where(pair % 2 == 1, -hop, hop)
        chip = self.position // 2 + step
        device = chip * 2 + (self.position % 2 + block % 2) % 2
        start = device * self.count
        live = (chip >= 0) & (chip < self.shards // 2)
        return start, live & (start < self.high) & (start + self.count > self.low)


def lanes(rows):
    return lax.broadcasted_iota(jnp.int32, (rows, 128), 1)


def minus_ones(rows, base, head):
    lane = lanes(rows)
    start = base + 3 * head
    return jnp.where((lane >= start) & (lane < start + 3), -1.0, 0.0)


def keep_head(values, half):
    lane = lanes(values.shape[0])
    return jnp.where((lane // 64) == half, values.astype(jnp.float32), 0.0)


def beside(left, right):
    return jnp.concatenate([left.astype(jnp.bfloat16), right.astype(jnp.bfloat16)], axis=1)


def pieces(values):
    high = values.astype(jnp.bfloat16).astype(jnp.float32)
    rest = values - high
    middle = rest.astype(jnp.bfloat16).astype(jnp.float32)
    return high, middle, rest - middle


def dot(left, right):
    return jnp.dot(left, right, preferred_element_type=jnp.float32)


def window_bias(frame, block):
    base, _ = frame.base(block)
    item = frame.items_of_rows(base, frame.count)
    lane = lanes(frame.count)
    return jnp.where((lane != item) & (lane < frame.items), far, 0.0)


def text_bias(frame, block, rows):
    slot = lax.broadcasted_iota(jnp.int32, (rows, 1), 0)
    length = jnp.int32(0)
    for item in range(frame.items):
        length = jnp.where(block == item, frame.text_len[item], length)
    lane = lanes(rows)
    dead = (lane != block) | (slot >= length)
    return jnp.where(dead & (lane < frame.items), far, 0.0)


def block_rule(frame, kind, rows):
    if kind == "frames":
        return (
            lambda block: frame.base(block)[1],
            lambda block: window_bias(frame, block),
        )
    return (
        lambda block: (block >= frame.first) & (block <= frame.last),
        lambda block: text_bias(frame, block, rows),
    )


def project_kernel(items, shards, blocks, columns, meta, mod_ref, w_ref, *refs):
    x_refs, out_ref = refs[:-1], refs[-1]
    count = x_refs[0].shape[0]
    frame = Frame(meta, items, count, shards)
    for number, block in enumerate(blocks):
        base, live = frame.base(jnp.int32(block))

        @pl.when(live)
        def _(number=number, base=base):
            normed, _ = layer_norm(x_refs[number][...].astype(jnp.float32))
            item = frame.items_of_rows(base, count)
            shift = jnp.zeros_like(normed)
            scale = jnp.zeros_like(normed)
            for i in range(items):
                shift = jnp.where(item == i, mod_ref[i, 0:1, :], shift)
                scale = jnp.where(item == i, mod_ref[i, 1:2, :], scale)
            hidden = (normed * (1.0 + scale) + shift).astype(jnp.bfloat16)
            for c in range(columns):
                part = w_ref[:, c * 768 : (c + 1) * 768]
                out_ref[number * count : (number + 1) * count, c * 768 : (c + 1) * 768] = dot(
                    hidden, part
                ).astype(jnp.bfloat16)


def project(meta, modulation, weight, x_blocks, blocks, items, shards, name):
    count, width = x_blocks[0].shape
    columns = weight.shape[1] // width
    return pl.pallas_call(
        partial(project_kernel, items, shards, blocks, columns),
        out_shape=jax.ShapeDtypeStruct((len(blocks) * count, weight.shape[1]), jnp.bfloat16),
        in_specs=[pl.BlockSpec(memory_space=pltpu.SMEM)]
        + [pl.BlockSpec(memory_space=pltpu.VMEM)] * (2 + len(blocks)),
        out_specs=pl.BlockSpec(memory_space=pltpu.VMEM),
        compiler_params=pltpu.CompilerParams(vmem_limit_bytes=40 * MIB),
        cost_estimate=pl.CostEstimate(
            flops=len(blocks) * count * width * weight.shape[1],
            bytes_accessed=2 * len(blocks) * count * (width + weight.shape[1]),
            transcendentals=0,
        ),
        name=name,
    )(meta, modulation, weight, *x_blocks)


def attend_kernel(items, shards, kind, blocks, meta, q_ref, k_ref, v_ref, o_ref, low_ref, f_ref, qa, s, m, l, acc):
    count = q_ref.shape[0]
    rows = k_ref.shape[0] // blocks
    frame = Frame(meta, items, count, shards)
    active, bias = block_rule(frame, kind, rows)
    pair = pl.program_id(0)
    lane = lanes(count)
    own = frame.items_of_rows(frame.position * count, count)
    q = q_ref[...]
    for h in range(2):
        qa[h] = beside(keep_head(q, h) * 0.125, (lane == own).astype(jnp.float32))
        m[h] = jnp.full((count, 128), far, jnp.float32)
        l[h] = jnp.zeros((count, 128), jnp.float32)
        acc[h] = jnp.zeros((count, 128), jnp.float32)

    @pl.loop(0, blocks)
    def _(block):
        @pl.when(active(block))
        def _():
            keys = beside(k_ref[pl.ds(pl.multiple_of(block * rows, rows), rows), :], bias(block))
            for h in range(2):
                scores = times_transposed(qa[h], keys)
                s[h, block] = scores
                m[h] = jnp.maximum(m[h], jnp.maximum(scores[:, :128], scores[:, 128:]))

    top = [jnp.max(m[h], axis=1, keepdims=True) for h in range(2)]

    @pl.loop(0, blocks)
    def _(block):
        @pl.when(active(block))
        def _():
            values = v_ref[pl.ds(pl.multiple_of(block * rows, rows), rows), :]
            for h in range(2):
                probs = jnp.exp(s[h, block] - top[h])
                l[h] = l[h] + (probs[:, :128] + probs[:, 128:])
                acc[h] = acc[h] + dot(probs.astype(jnp.bfloat16), values)

    out = []
    features = jnp.where(pair == 0, (lane == own).astype(jnp.float32), f_ref[...].astype(jnp.float32))
    for h in range(2):
        total = jnp.sum(l[h], axis=1, keepdims=True)
        out.append(acc[h] / total)
        start = LSE_LANE + 3 * (2 * pair + h)
        for number, piece in enumerate(pieces(top[h] + jnp.log(total))):
            features = jnp.where(lane == start + number, piece, features)
    result = jnp.where(lane < 64, out[0], out[1])
    o_ref[...] = result
    low_ref[...] = result.astype(jnp.bfloat16)
    f_ref[...] = features.astype(jnp.bfloat16)


def attend(meta, queries, kv, kind, blocks, items, shards, name):
    count, width = queries.shape
    pairs = width // 128
    total = kv.shape[0]
    rows = total // blocks
    column = lambda offset: (lambda p: (0, p + offset))
    tile = pl.BlockSpec((count, 128), column(0))
    return pl.pallas_call(
        partial(attend_kernel, items, shards, kind, blocks),
        grid=(pairs,),
        out_shape=(
            jax.ShapeDtypeStruct((count, width), jnp.float32),
            jax.ShapeDtypeStruct((count, width), jnp.bfloat16),
            jax.ShapeDtypeStruct((count, 128), jnp.bfloat16),
        ),
        in_specs=[
            pl.BlockSpec(memory_space=pltpu.SMEM),
            tile,
            pl.BlockSpec((total, 128), column(0)),
            pl.BlockSpec((total, 128), column(pairs)),
        ],
        out_specs=(tile, tile, pl.BlockSpec((count, 128), lambda p: (0, 0))),
        scratch_shapes=[
            pltpu.VMEM((2, count, 256), jnp.bfloat16),
            pltpu.VMEM((2, blocks, count, rows), jnp.float32),
            pltpu.VMEM((2, count, 128), jnp.float32),
            pltpu.VMEM((2, count, 128), jnp.float32),
            pltpu.VMEM((2, count, 128), jnp.float32),
        ],
        compiler_params=pltpu.CompilerParams(vmem_limit_bytes=40 * MIB),
        cost_estimate=pl.CostEstimate(
            flops=2 * count * total * width,
            bytes_accessed=4 * total * width,
            transcendentals=count * total * H // 2,
        ),
        name=name,
    )(meta, queries, kv, kv)


def query_grad_kernel(items, shards, kind, blocks, meta, q_ref, do_ref, f_ref, k_ref, v_ref, dq_ref, qa, da, acc):
    count = q_ref.shape[0]
    rows = k_ref.shape[0] // blocks
    frame = Frame(meta, items, count, shards)
    active, bias = block_rule(frame, kind, rows)
    pair = pl.program_id(0)
    features = f_ref[...]
    for h in range(2):
        qa[h] = beside(keep_head(q_ref[...], h) * 0.125, features)
        da[h] = beside(keep_head(do_ref[...], h), features)
        acc[h] = jnp.zeros((count, 128), jnp.float32)

    @pl.loop(0, blocks)
    def _(block):
        @pl.when(active(block))
        def _():
            here = pl.ds(pl.multiple_of(block * rows, rows), rows)
            keys, values, mask = k_ref[here, :], v_ref[here, :], bias(block)
            for h in range(2):
                head = 2 * pair + h
                probs = jnp.exp(
                    times_transposed(qa[h], beside(keys, mask + minus_ones(rows, LSE_LANE, head)))
                )
                slope = times_transposed(da[h], beside(values, minus_ones(rows, DELTA_LANE, head)))
                acc[h] = acc[h] + dot((probs * slope).astype(jnp.bfloat16), keys)

    dq_ref[...] = (jnp.where(lanes(count) < 64, acc[0], acc[1]) * 0.125).astype(jnp.bfloat16)


def query_grad(meta, queries, grad_out, features, kv, kind, blocks, items, shards, name):
    count, width = queries.shape
    pairs = width // 128
    total = kv.shape[0]
    column = lambda offset: (lambda p: (0, p + offset))
    tile = pl.BlockSpec((count, 128), column(0))
    return pl.pallas_call(
        partial(query_grad_kernel, items, shards, kind, blocks),
        grid=(pairs,),
        out_shape=jax.ShapeDtypeStruct((count, width), jnp.bfloat16),
        in_specs=[
            pl.BlockSpec(memory_space=pltpu.SMEM),
            tile,
            tile,
            pl.BlockSpec((count, 128), lambda p: (0, 0)),
            pl.BlockSpec((total, 128), column(0)),
            pl.BlockSpec((total, 128), column(pairs)),
        ],
        out_specs=tile,
        scratch_shapes=[
            pltpu.VMEM((2, count, 256), jnp.bfloat16),
            pltpu.VMEM((2, count, 256), jnp.bfloat16),
            pltpu.VMEM((2, count, 128), jnp.float32),
        ],
        compiler_params=pltpu.CompilerParams(vmem_limit_bytes=40 * MIB),
        cost_estimate=pl.CostEstimate(
            flops=3 * count * total * width,
            bytes_accessed=4 * total * width,
            transcendentals=count * total * H // 2,
        ),
        name=name,
    )(meta, queries, grad_out, features, kv, kv)


def key_grad_tile(frame, pair, k, v, mask, visit, dk_acc, dv_acc, ka, va):
    rows = k.shape[0]
    for h in range(2):
        head = 2 * pair + h
        ka[h] = beside(keep_head(k, h), mask + minus_ones(rows, LSE_LANE, head))
        va[h] = beside(keep_head(v, h), minus_ones(rows, DELTA_LANE, head))
        dk_acc[h] = jnp.zeros((rows, 128), jnp.float32)
        dv_acc[h] = jnp.zeros((rows, 128), jnp.float32)

    def step(q, do, features):
        q = (q.astype(jnp.float32) * 0.125).astype(jnp.bfloat16)
        q_wide = beside(q, features)
        do_wide = beside(do, features)
        for h in range(2):
            probs = jnp.exp(times_transposed(ka[h], q_wide))
            slope = times_transposed(va[h], do_wide)
            dv_acc[h] = dv_acc[h] + dot(probs.astype(jnp.bfloat16), do)
            dk_acc[h] = dk_acc[h] + dot((probs * slope).astype(jnp.bfloat16), q)

    visit(step)
    lane = lanes(rows)
    return (
        jnp.where(lane < 64, dk_acc[0], dk_acc[1]),
        jnp.where(lane < 64, dv_acc[0], dv_acc[1]),
    )


def frame_key_grad_kernel(items, shards, blocks, meta, q_ref, do_ref, f_ref, k_ref, v_ref, dk_ref, dv_ref, ka, va, dka, dva):
    count = k_ref.shape[0]
    frame = Frame(meta, items, count, shards)

    def visit(step):
        @pl.loop(0, blocks)
        def _(block):
            @pl.when(frame.base(block)[1])
            def _():
                here = pl.ds(pl.multiple_of(block * count, count), count)
                step(q_ref[here, :], do_ref[here, :], f_ref[here, :])

    dk, dv = key_grad_tile(
        frame, pl.program_id(0), k_ref[...], v_ref[...], window_bias(frame, jnp.int32(0)), visit, dka, dva, ka, va
    )
    dk_ref[...] = dk.astype(jnp.bfloat16)
    dv_ref[...] = dv.astype(jnp.bfloat16)


def key_scratch(rows):
    return [
        pltpu.VMEM((2, rows, 256), jnp.bfloat16),
        pltpu.VMEM((2, rows, 256), jnp.bfloat16),
        pltpu.VMEM((2, rows, 128), jnp.float32),
        pltpu.VMEM((2, rows, 128), jnp.float32),
    ]


def frame_key_grad(meta, q_window, do_window, kv, count, blocks, items, shards, name):
    total, width = q_window.shape
    pairs = width // 128
    column = lambda offset: (lambda p: (0, p + offset))
    tile = pl.BlockSpec((count, 128), column(0))
    wide = pl.BlockSpec((total, 128), column(0))
    return pl.pallas_call(
        partial(frame_key_grad_kernel, items, shards, blocks),
        grid=(pairs,),
        out_shape=(jax.ShapeDtypeStruct((count, width), jnp.bfloat16),) * 2,
        in_specs=[
            pl.BlockSpec(memory_space=pltpu.SMEM),
            wide,
            wide,
            pl.BlockSpec((total, 128), lambda p: (0, pairs)),
            tile,
            pl.BlockSpec((count, 128), column(pairs)),
        ],
        out_specs=(tile, tile),
        scratch_shapes=key_scratch(count),
        compiler_params=pltpu.CompilerParams(vmem_limit_bytes=40 * MIB),
        cost_estimate=pl.CostEstimate(
            flops=4 * count * total * width,
            bytes_accessed=4 * total * width,
            transcendentals=count * total * H // 2,
        ),
        name=name,
    )(meta, q_window, do_window, do_window, kv, kv)


def text_key_grad_kernel(items, shards, meta, q_ref, do_ref, f_ref, k_ref, v_ref, dk_ref, dv_ref, ka, va, dka, dva):
    count = q_ref.shape[0]
    rows = k_ref.shape[0] // items
    frame = Frame(meta, items, count, shards)
    for item in range(items):
        here = slice(item * rows, (item + 1) * rows)
        live = (item >= frame.first) & (item <= frame.last)

        @pl.when(live)
        def _(item=item, here=here):
            dk, dv = key_grad_tile(
                frame,
                pl.program_id(0),
                k_ref[here, :],
                v_ref[here, :],
                text_bias(frame, jnp.int32(item), rows),
                lambda step: step(q_ref[...], do_ref[...], f_ref[...]),
                dka,
                dva,
                ka,
                va,
            )
            dk_ref[here, :] = dk.astype(jnp.bfloat16)
            dv_ref[here, :] = dv.astype(jnp.bfloat16)

        @pl.when(jnp.logical_not(live))
        def _(here=here):
            dk_ref[here, :] = jnp.zeros((rows, 128), jnp.bfloat16)
            dv_ref[here, :] = jnp.zeros((rows, 128), jnp.bfloat16)


def text_key_grad(meta, queries, grad_out, features, kv, items, shards, name):
    count, width = queries.shape
    pairs = width // 128
    total = kv.shape[0]
    column = lambda offset: (lambda p: (0, p + offset))
    tile = pl.BlockSpec((count, 128), column(0))
    wide = pl.BlockSpec((total, 128), column(0))
    return pl.pallas_call(
        partial(text_key_grad_kernel, items, shards),
        grid=(pairs,),
        out_shape=(jax.ShapeDtypeStruct((total, width), jnp.bfloat16),) * 2,
        in_specs=[
            pl.BlockSpec(memory_space=pltpu.SMEM),
            tile,
            tile,
            pl.BlockSpec((count, 128), lambda p: (0, 0)),
            wide,
            pl.BlockSpec((total, 128), column(pairs)),
        ],
        out_specs=(wide, wide),
        scratch_shapes=key_scratch(total // items),
        compiler_params=pltpu.CompilerParams(vmem_limit_bytes=40 * MIB),
        cost_estimate=pl.CostEstimate(
            flops=4 * count * total * width,
            bytes_accessed=8 * total * width,
            transcendentals=count * total * H // 2,
        ),
        name=name,
    )(meta, queries, grad_out, features, kv, kv)


def with_deltas(features, grad_out, attn_exact):
    width = attn_exact.shape[1]
    lane = jnp.arange(128)[None, :]
    head = (jnp.arange(width) // (width // H))[:, None]
    pick = ((lane >= DELTA_LANE) & ((lane - DELTA_LANE) // 3 == head)).astype(jnp.float32)
    delta = jnp.dot(
        grad_out.astype(jnp.float32) * attn_exact,
        pick,
        precision=lax.Precision.HIGHEST,
        preferred_element_type=jnp.float32,
    )
    high = lax.reduce_precision(delta, 8, 7)
    middle = lax.reduce_precision(delta - high, 8, 7)
    which = (lane - DELTA_LANE) % 3
    piece = jnp.where(which == 0, high, jnp.where(which == 1, middle, delta - high - middle))
    inside = (lane >= DELTA_LANE) & (lane < DELTA_LANE + 3 * H)
    return jnp.where(inside, piece.astype(jnp.bfloat16), features)


def gather_window(own, reach, shards):
    swap = [(i, i ^ 1) for i in range(shards)]
    up = [(i, i + 2) for i in range(shards - 2)]
    down = [(i + 2, i) for i in range(shards - 2)]
    blocks = [own, lax.ppermute(own, "seq", swap)]
    below, above = own, own
    for _ in range(reach):
        below = lax.ppermute(below, "seq", up)
        above = lax.ppermute(above, "seq", down)
        blocks += [below, lax.ppermute(below, "seq", swap)]
        blocks += [above, lax.ppermute(above, "seq", swap)]
    return blocks


def body(
    frames,
    cotangent,
    modulation,
    lengths,
    text,
    text_len,
    w_qkv,
    w_o,
    w_cq,
    w_ckv,
    w_co,
    w_up,
    w_down,
):
    local = frames[0]
    count, width = local.shape
    items = lengths.shape[1]
    text_rows, text_width = text.shape[2:]
    shards = lax.axis_size("seq")
    position = lax.axis_index("seq")
    reach = min(-(-(LONGEST - 1) // (2 * count)), shards // 2 - 1)
    blocks = 2 + 4 * reach
    meta = jnp.concatenate([position[None].astype(jnp.int32), lengths[0], text_len[0]])
    item_range = jnp.arange(items, dtype=jnp.int32)
    ends = jnp.sum(jnp.where(item_range[None, :] <= item_range[:, None], lengths[0][None, :], 0), axis=1)
    place = position * count + jnp.arange(count, dtype=jnp.int32)
    query_items = jnp.sum((place[:, None] >= ends[None, :]).astype(jnp.int32), axis=1)[:, None]
    one_hot = (query_items == item_range[None, :]).astype(jnp.float32)
    mod = modulation[0]

    def per_frame(which):
        found = jnp.broadcast_to(mod[0, which][None, :], (count, width))
        for item in range(1, items):
            found = jnp.where(query_items == item, mod[item, which][None, :], found)
        return found

    window = gather_window(local, reach, shards)
    inputs = local.astype(jnp.float32)
    normed_one, inverse_one = layer_norm(inputs)
    hidden_one = (normed_one * (1.0 + per_frame(1)) + per_frame(0)).astype(jnp.bfloat16)
    queries = jnp.dot(hidden_one, w_qkv[:, :width], preferred_element_type=jnp.float32).astype(jnp.bfloat16)
    text_proj = jnp.dot(
        text[0].reshape(items * text_rows, text_width), w_ckv, preferred_element_type=jnp.float32
    ).astype(jnp.bfloat16)
    kv = project(meta, mod, w_qkv[:, width:], window, tuple(range(blocks)), items, shards, "project_keys")
    attn_exact, attended, features = attend(meta, queries, kv, "frames", blocks, items, shards, "self_attend")
    branch_one = jnp.dot(attended, w_o, preferred_element_type=jnp.float32)
    after_attn = inputs + per_frame(2) * branch_one
    normed_cross, inverse_cross = layer_norm(after_attn)
    cross_in = normed_cross.astype(jnp.bfloat16)
    cross_queries = jnp.dot(cross_in, w_cq, preferred_element_type=jnp.float32).astype(jnp.bfloat16)
    cross_exact, cross_out, cross_features = attend(
        meta, cross_queries, text_proj, "text", items, items, shards, "cross_attend"
    )
    branch_two = jnp.dot(cross_out, w_co, preferred_element_type=jnp.float32)
    after_cross = after_attn + branch_two
    normed_two, inverse_two = layer_norm(after_cross)
    hidden_two = (normed_two * (1.0 + per_frame(4)) + per_frame(3)).astype(jnp.bfloat16)
    pre_act = jnp.dot(hidden_two, w_up, preferred_element_type=jnp.float32)
    activated, gelu_back = jax.vjp(partial(jax.nn.gelu, approximate=True), pre_act)
    activated_low = activated.astype(jnp.bfloat16)
    branch_three = jnp.dot(activated_low, w_down, preferred_element_type=jnp.float32)
    gate_two = per_frame(5)
    result = after_cross + gate_two * branch_three
    grad_out = cotangent[0].astype(jnp.float32)
    grad_branch_three = (grad_out * gate_two).astype(jnp.bfloat16)
    grad_w_down = contract_rows(activated_low, grad_branch_three)
    grad_pre = gelu_back(times_transposed(grad_branch_three, w_down))[0].astype(jnp.bfloat16)
    grad_w_up = contract_rows(hidden_two, grad_pre)
    grad_hidden_two = times_transposed(grad_pre, w_up)
    grad_cross = grad_out + norm_back(grad_hidden_two * (1.0 + per_frame(4)), normed_two, inverse_two)
    grad_branch_two = grad_cross.astype(jnp.bfloat16)
    grad_w_co = contract_rows(cross_out, grad_branch_two)
    grad_cross_out = times_transposed(grad_branch_two, w_co).astype(jnp.bfloat16)
    cross_features = with_deltas(cross_features, grad_cross_out, cross_exact)
    grad_cross_queries = query_grad(
        meta, cross_queries, grad_cross_out, cross_features, text_proj, "text", items, items, shards, "cross_query_grad"
    )
    grad_text_keys, grad_text_values = text_key_grad(
        meta, cross_queries, grad_cross_out, cross_features, text_proj, items, shards, "cross_key_grad"
    )
    grad_w_cq = contract_rows(cross_in, grad_cross_queries)
    grad_attn_res = grad_cross + norm_back(
        times_transposed(grad_cross_queries, w_cq), normed_cross, inverse_cross
    )
    grad_branch_one = (grad_attn_res * per_frame(2)).astype(jnp.bfloat16)
    grad_w_o = contract_rows(attended, grad_branch_one)
    grad_attended = times_transposed(grad_branch_one, w_o).astype(jnp.bfloat16)
    features = with_deltas(features, grad_attended, attn_exact)
    grad_queries = query_grad(
        meta, queries, grad_attended, features, kv, "frames", blocks, items, shards, "self_query_grad"
    )
    do_window = jnp.concatenate(
        gather_window(jnp.concatenate([grad_attended, features], axis=1), reach, shards), axis=0
    )
    q_window = project(meta, mod, w_qkv[:, :width], window, tuple(range(blocks)), items, shards, "project_queries")
    grad_keys, grad_values = frame_key_grad(
        meta, q_window, do_window, kv, count, blocks, items, shards, "self_key_grad"
    )
    grad_projected = jnp.concatenate([grad_queries, grad_keys, grad_values], axis=1)
    grad_w_qkv = contract_rows(hidden_one, grad_projected)
    grad_hidden_one = times_transposed(grad_projected, w_qkv)
    grad_inputs = grad_attn_res + norm_back(
        grad_hidden_one * (1.0 + per_frame(1)), normed_one, inverse_one
    )

    def item_sum(values):
        return lax.dot_general(
            one_hot,
            values,
            (((0,), (0,)), ((), ())),
            precision=lax.Precision.HIGHEST,
            preferred_element_type=jnp.float32,
        )

    item_terms = jnp.stack(
        [
            item_sum(grad_hidden_one),
            item_sum(grad_hidden_one * normed_one),
            item_sum(grad_attn_res * branch_one),
            item_sum(grad_hidden_two),
            item_sum(grad_hidden_two * normed_two),
            item_sum(grad_out * branch_three),
        ],
        axis=1,
    )[None]
    text_terms = jnp.concatenate([grad_text_keys, grad_text_values], axis=1)
    share_rows = text_rows // shards
    text_terms = text_terms.reshape(items, shards, share_rows, 2 * width).transpose(1, 0, 2, 3)
    text_grad_low = lax.psum_scatter(
        text_terms.reshape(shards * items * share_rows, 2 * width), "seq", scatter_dimension=0, tiled=True
    )
    item_share = lax.psum_scatter(item_terms, "seq", scatter_dimension=3, tiled=True)
    text_mine = lax.dynamic_slice_in_dim(text[0], position * share_rows, share_rows, 1).reshape(
        items * share_rows, text_width
    )
    grad_text = times_transposed(text_grad_low, w_ckv).reshape(1, items, share_rows, text_width)
    grad_w_ckv = contract_rows(text_mine, text_grad_low)

    def reduce_weight(grad):
        part = lax.psum_scatter(grad.astype(jnp.bfloat16), "seq", scatter_dimension=0, tiled=True)
        return lax.psum_scatter(part, "batch", scatter_dimension=1, tiled=True).astype(jnp.float32)

    return (
        result.astype(jnp.bfloat16)[None],
        grad_inputs[None],
        item_share[:, :, :3],
        item_share[:, :, 3:],
        grad_text,
        reduce_weight(grad_w_qkv),
        reduce_weight(grad_w_o),
        reduce_weight(grad_w_cq),
        reduce_weight(grad_w_ckv),
        reduce_weight(grad_w_co),
        reduce_weight(grad_w_up),
        reduce_weight(grad_w_down),
    )


def solution(mesh):
    in_specs = (
        P("batch", "seq", None),
        P("batch", "seq", None),
        P("batch", None, None, None),
        P("batch", None),
        P("batch", None, None, None),
        P("batch", None),
        P(),
        P(),
        P(),
        P(),
        P(),
        P(),
        P(),
    )
    out_specs = (
        P("batch", "seq", None),
        P("batch", "seq", None),
        P("batch", None, None, "seq"),
        P("batch", None, None, "seq"),
        P("batch", None, "seq", None),
        P("seq", "batch"),
        P("seq", "batch"),
        P("seq", "batch"),
        P("seq", "batch"),
        P("seq", "batch"),
        P("seq", "batch"),
        P("seq", "batch"),
    )
    return jax.shard_map(body, mesh=mesh, in_specs=in_specs, out_specs=out_specs, check_vma=False)
```

profile of v0, /device:TPU:0, one launch (start us, length us, event | category | flops | bytes accessed | tf_op | source)
XLA Modules:
  0.0 704.4 jit_solution(2735050532309423364)
XLA Ops:
  8.8 6.3 collective-permute-start.1
  17.8 4.4 convolution_convert_fusion.4.k_ref.v_ref
  24.4 4.6 collective-permute-start.5
  31.0 5.7 collective-permute-done.7.refs_8_
  39.7 5.1 project_keys.1.k_ref.v_ref
  44.9 17.6 %self_attend.1 = (f32[256,768]{1,0:T(8,128)S(1)}, bf16[256,768]{1,0:T(8,128)(2,1)S(1)}, bf16[256,128]{1,0:T(8,128)(2,1)S(1)}) custom-call(s32[7]{0:T(128)S(1)} %pad_add_fusion.meta, bf16[256,768]{1,0:T(8,128)(2,1)S(1)} %convolution_convert_fusion.11.q_ref, bf16[2560,1536]{1,0:T(8,128)(2,1)S(1)} %project_keys.1.k_ref.v_ref, ...), custom_call_target="tpu_custom_call" | custom-call | flops 1006632960 | bytes 7864320 | tf_op jit(solution)/shard_map/self_attend/pallas_call | solution.py:251
  65.2 7.4 %cross_attend.1 = (f32[256,768]{1,0:T(8,128)S(1)}, bf16[256,768]{1,0:T(8,128)(2,1)S(1)}, bf16[256,128]{1,0:T(8,128)(2,1)S(1)}) custom-call(s32[7]{0:T(128)S(1)} %pad_add_fusion.meta, bf16[256,768]{1,0:T(8,128)(2,1)S(1)} %convolution_convert_fusion.10.q_ref, bf16[768,1536]{1,0:T(8,128)(2,1)S(1)} %convolution_convert_fusion.4.k_ref.v_ref, ...), custom_call_target="tpu_custom_call" | custom-call | flops 301989888 | bytes 2359296 | tf_op jit(solution)/shard_map/cross_attend/pallas_call | solution.py:251
  77.5 4.7 fusion.6
  88.2 14.6 %cross_key_grad.1 = (bf16[768,768]{1,0:T(8,128)(2,1)S(1)}, bf16[768,768]{1,0:T(8,128)(2,1)S(1)}) custom-call(s32[7]{0:T(128)S(1)} %pad_add_fusion.meta, bf16[256,768]{1,0:T(8,128)(2,1)S(1)} %convolution_convert_fusion.10.q_ref, bf16[256,768]{1,0:T(8,128)(2,1)S(1)} %convolution_convert_fusion.9.do_ref, bf16[256,128]{1,0:T(8,128)(2,1)S(1)} %fusion.62.f_ref, ...), custom_call_target="tpu_custom_call" | custom-call | flops 603979776 | bytes 4718592 | tf_op jit(solution)/shard_map/cross_key_grad/pallas_call | solution.py:469
  112.1 5.5 cross_query_grad.1
  126.8 31.0 %collective-permute-start.10 = (bf16[256,896]{1,0:T(8,128)(2,1)}, bf16[256,896]{1,0:T(8,128)(2,1)}, u32[]{:S(2)}, u32[]{:S(2)}) collective-permute-start(bf16[256,896]{1,0:T(8,128)(2,1)} %get-tuple-element.108), channel_id=1, source_target_pairs={{0,2},{1,3},{2,4},{3,5},{4,6},{5,7},{8,10},{9,11},{10,12},{11,13},... | collective-permute-start | bytes 1376264 | tf_op jit(solution)/shard_map/ppermute | solution.py:519
  162.5 3.8 collective-permute-done.10
  166.3 4.4 collective-permute-start.14
  178.2 15.6 %self_query_grad.1 = bf16[256,768]{1,0:T(8,128)(2,1)S(1)} custom-call(s32[7]{0:T(128)S(1)} %pad_add_fusion.meta, bf16[256,768]{1,0:T(8,128)(2,1)S(1)} %copy-done.30, bf16[256,768]{1,0:T(8,128)(2,1)S(1)} %copy-done.13, bf16[256,128]{1,0:T(8,128)(2,1)S(1)} %copy-done.38, bf16[2560,1536]{1,0:T(8,128)(2,1)S(1)} %copy-done.2, bf16[2560,1536]{1,0:T(8,128)(2,1)S(1)} %copy-done.2), custom_call_target="tpu_custom_call" | custom-call | flops 1509949440 | bytes 7864320 | tf_op jit(solution)/shard_map/self_query_grad/pallas_call | solution.py:318
  194.0 4.4 project_queries.1.q_ref
  202.8 16.4 %self_key_grad.1 = (bf16[256,768]{1,0:T(8,128)(2,1)S(1)}, bf16[256,768]{1,0:T(8,128)(2,1)S(1)}) custom-call(s32[7]{0:T(128)S(1)} %pad_add_fusion.meta, bf16[2560,768]{1,0:T(8,128)(2,1)S(1)} %project_queries.1.q_ref, bf16[2560,896]{1,0:T(8,128)(2,1)S(1)} %constant_dynamic-update-slice_fusion.do_ref.f_ref, ...), custom_call_target="tpu_custom_call" | custom-call | flops 2013265920 | bytes 7864320 | tf_op jit(solution)/shard_map/self_key_grad/pallas_call | solution.py:407
  224.1 6.6 convolution_convert_fusion
  231.4 5.5 convolution_convert_fusion.1
  242.7 4.3 fusion.41
  260.2 15.4 %reduce-scatter.35.cloned.1.call-done = bf16[96,768]{1,0:T(8,128)(2,1)} async-done(((bf16[768,768]{1,0:T(8,128)(2,1)}), bf16[96,768]{1,0:T(8,128)(2,1)}) %reduce-scatter.35.cloned.1.call-update) | async-done | bytes 147472 | tf_op jit(solution)/shard_map/reduce_scatter | solution.py:667
  277.4 42.5 %reduce-scatter.33.cloned.1.call-done = bf16[96,2304]{1,0:T(8,128)(2,1)} async-done(((bf16[768,2304]{1,0:T(8,128)(2,1)}), bf16[96,2304]{1,0:T(8,128)(2,1)}) %reduce-scatter.33.cloned.1.call-update) | async-done | bytes 442384 | tf_op jit(solution)/shard_map/reduce_scatter | solution.py:667
  322.1 53.5 %reduce-scatter.47.cloned.1.call-done = bf16[384,768]{1,0:T(8,128)(2,1)} async-done(((bf16[3072,768]{1,0:T(8,128)(2,1)}), bf16[384,768]{1,0:T(8,128)(2,1)}) %reduce-scatter.47.cloned.1.call-update) | async-done | bytes 589840 | tf_op jit(solution)/shard_map/reduce_scatter | solution.py:667
  377.8 53.6 %reduce-scatter.43.cloned.1.call-done = bf16[96,3072]{1,0:T(8,128)(2,1)} async-done(((bf16[768,3072]{1,0:T(8,128)(2,1)}), bf16[96,3072]{1,0:T(8,128)(2,1)}) %reduce-scatter.43.cloned.1.call-update) | async-done | bytes 589840 | tf_op jit(solution)/shard_map/reduce_scatter | solution.py:667
  434.0 38.6 %reduce-scatter.39.cloned.1.call-done = bf16[128,1536]{1,0:T(8,128)(2,1)} async-done(((bf16[1024,1536]{1,0:T(8,128)(2,1)}), bf16[128,1536]{1,0:T(8,128)(2,1)}) %reduce-scatter.39.cloned.1.call-update) | async-done | bytes 393232 | tf_op jit(solution)/shard_map/reduce_scatter | solution.py:667
  477.1 28.1 %reduce-scatter.49.cloned.1.call-done = f32[96,18]{1,0:T(8,128)} async-done(((f32[768,18]{1,0:T(8,128)}), f32[96,18]{1,0:T(8,128)}) %reduce-scatter.49.cloned.1.call-update) | async-done | bytes 6928
  510.2 19.7 %reduce-scatter.59.cloned.1.call-done = bf16[192,96]{1,0:T(8,128)(2,1)} async-done(((bf16[768,96]{1,0:T(8,128)(2,1)}), bf16[192,96]{1,0:T(8,128)(2,1)}) %reduce-scatter.59.cloned.1.call-update) | async-done | bytes 36880
  531.5 25.8 %reduce-scatter.55.cloned.1.call-done = bf16[192,96]{1,0:T(8,128)(2,1)} async-done(((bf16[768,96]{1,0:T(8,128)(2,1)}), bf16[192,96]{1,0:T(8,128)(2,1)}) %reduce-scatter.55.cloned.1.call-update) | async-done | bytes 36880
  558.8 25.6 %reduce-scatter.53.cloned.1.call-done = bf16[192,96]{1,0:T(8,128)(2,1)} async-done(((bf16[768,96]{1,0:T(8,128)(2,1)}), bf16[192,96]{1,0:T(8,128)(2,1)}) %reduce-scatter.53.cloned.1.call-update) | async-done | bytes 36880
  588.8 23.7 %reduce-scatter.51.cloned.1.call-done = bf16[576,96]{1,0:T(8,128)(2,1)} async-done(((bf16[2304,96]{1,0:T(8,128)(2,1)}), bf16[576,96]{1,0:T(8,128)(2,1)}) %reduce-scatter.51.cloned.1.call-update) | async-done | bytes 110608
  614.2 26.3 %reduce-scatter.61.cloned.1.call-done = bf16[192,384]{1,0:T(8,128)(2,1)} async-done(((bf16[768,384]{1,0:T(8,128)(2,1)}), bf16[192,384]{1,0:T(8,128)(2,1)}) %reduce-scatter.61.cloned.1.call-update) | async-done | bytes 147472
  642.4 26.0 %reduce-scatter.45.cloned.1.call-done = bf16[96,768]{1,0:T(8,128)(2,1)} async-done(((bf16[96,3072]{1,0:T(8,128)(2,1)}), bf16[96,768]{1,0:T(8,128)(2,1)}) %reduce-scatter.45.cloned.1.call-update) | async-done | bytes 147472 | tf_op jit(solution)/shard_map/reduce_scatter | solution.py:668
  670.0 25.7 %reduce-scatter.57.cloned.1.call-done = bf16[384,128]{1,0:T(8,128)(2,1)} async-done(((bf16[1536,128]{1,0:T(8,128)(2,1)}), bf16[384,128]{1,0:T(8,128)(2,1)}) %reduce-scatter.57.cloned.1.call-update) | async-done | bytes 98320
  (422 shorter events, 115.5 us)
Async XLA Ops:
  7.2 231.7 %reduce-scatter.31.cloned.1.call-start = ((), (), s32[]{:S(2)}) async-start(), calls=%async_computation.16 | async-start | bytes 2654208 | tf_op jit(solution)/shard_map/reduce_scatter | solution.py:656
  7.2 15.8 %collective-permute-start.3 = (bf16[256,768]{1,0:T(8,128)(2,1)}, bf16[256,768]{1,0:T(8,128)(2,1)}, u32[]{:S(2)}, u32[]{:S(2)}) collective-permute-start(bf16[256,768]{1,0:T(8,128)(2,1)} %bitcast.110), channel_id=1, source_target_pairs={{2,0},{3,1},{4,2},{5,3},{6,4},{7,5},{10,8},{11,9},{12,10},{13,11},... | collective-permute-start | bytes 1179656 | tf_op jit(solution)/shard_map/ppermute | solution.py:520
  8.8 15.6 %collective-permute-start.1 = (bf16[256,768]{1,0:T(8,128)(2,1)}, bf16[256,768]{1,0:T(8,128)(2,1)}, u32[]{:S(2)}, u32[]{:S(2)}) collective-permute-start(bf16[256,768]{1,0:T(8,128)(2,1)} %bitcast.111), channel_id=1, source_target_pairs={{0,2},{1,3},{2,4},{3,5},{4,6},{5,7},{8,10},{9,11},{10,12},{11,13},... | collective-permute-start | bytes 1179656 | tf_op jit(solution)/shard_map/ppermute | solution.py:519
  15.1 24.0 %collective-permute-start = (bf16[256,768]{1,0:T(8,128)(2,1)}, bf16[256,768]{1,0:T(8,128)(2,1)}, u32[]{:S(2)}, u32[]{:S(2)}) collective-permute-start(bf16[256,768]{1,0:T(8,128)(2,1)} %bitcast.112), channel_id=1, source_target_pairs={{0,1},{1,0},{2,3},{3,2},{4,5},{5,4},{6,7},{7,6},{8,9},{9,8},{10,11... | collective-permute-start | bytes 1179656 | tf_op jit(solution)/shard_map/ppermute | solution.py:516
  23.1 13.6 %collective-permute-start.7 = (bf16[256,768]{1,0:T(8,128)(2,1)}, bf16[256,768]{1,0:T(8,128)(2,1)S(1)}, u32[]{:S(2)}, u32[]{:S(2)}) collective-permute-start(bf16[256,768]{1,0:T(8,128)(2,1)} %collective-permute-done.3.refs_4_), channel_id=1, source_target_pairs={{2,0},{3,1},{4,2},{5,3},{6,4},{7,5},{10,8},{11,9},{12,10},{13,11},... | collective-permute-start | bytes 1179656 | tf_op jit(solution)/shard_map/ppermute | solution.py:520
  24.4 13.6 %collective-permute-start.5 = (bf16[256,768]{1,0:T(8,128)(2,1)}, bf16[256,768]{1,0:T(8,128)(2,1)S(1)}, u32[]{:S(2)}, u32[]{:S(2)}) collective-permute-start(bf16[256,768]{1,0:T(8,128)(2,1)} %collective-permute-done.1.refs_2_), channel_id=1, source_target_pairs={{0,2},{1,3},{2,4},{3,5},{4,6},{5,7},{8,10},{9,11},{10,12},{11,13},... | collective-permute-start | bytes 1179656 | tf_op jit(solution)/shard_map/ppermute | solution.py:519
  30.4 8.7 %collective-permute-start.4 = (bf16[256,768]{1,0:T(8,128)(2,1)}, bf16[256,768]{1,0:T(8,128)(2,1)S(1)}, u32[]{:S(2)}, u32[]{:S(2)}) collective-permute-start(bf16[256,768]{1,0:T(8,128)(2,1)} %collective-permute-done.3.refs_4_), channel_id=1, source_target_pairs={{0,1},{1,0},{2,3},{3,2},{4,5},{5,4},{6,7},{7,6},{8,9},{9,8},{10,11... | collective-permute-start | bytes 1179656 | tf_op jit(solution)/shard_map/ppermute | solution.py:522
  30.5 8.7 %collective-permute-start.2 = (bf16[256,768]{1,0:T(8,128)(2,1)}, bf16[256,768]{1,0:T(8,128)(2,1)S(1)}, u32[]{:S(2)}, u32[]{:S(2)}) collective-permute-start(bf16[256,768]{1,0:T(8,128)(2,1)} %collective-permute-done.1.refs_2_), channel_id=1, source_target_pairs={{0,1},{1,0},{2,3},{3,2},{4,5},{5,4},{6,7},{7,6},{8,9},{9,8},{10,11... | collective-permute-start | bytes 1179656 | tf_op jit(solution)/shard_map/ppermute | solution.py:521
  36.7 2.5 collective-permute-start.8
  104.6 152.0 %reduce-scatter.41.cloned.1.call-start = ((), (), s32[]{:S(2)}) async-start(), calls=%async_computation.21 | async-start | bytes 1327104 | tf_op jit(solution)/shard_map/reduce_scatter | solution.py:667
  107.5 150.9 %reduce-scatter.37.cloned.1.call-start = ((), (), s32[]{:S(2)}) async-start(), calls=%async_computation.19 | async-start | bytes 1327104 | tf_op jit(solution)/shard_map/reduce_scatter | solution.py:667
  120.1 155.6 %reduce-scatter.35.cloned.1.call-start = ((), (), s32[]{:S(2)}) async-start(), calls=%async_computation.18 | async-start | bytes 1327104 | tf_op jit(solution)/shard_map/reduce_scatter | solution.py:667
  126.8 39.6 %collective-permute-start.10 = (bf16[256,896]{1,0:T(8,128)(2,1)}, bf16[256,896]{1,0:T(8,128)(2,1)}, u32[]{:S(2)}, u32[]{:S(2)}) collective-permute-start(bf16[256,896]{1,0:T(8,128)(2,1)} %get-tuple-element.108), channel_id=1, source_target_pairs={{0,2},{1,3},{2,4},{3,5},{4,6},{5,7},{8,10},{9,11},{10,12},{11,13},... | collective-permute-start | bytes 1376264 | tf_op jit(solution)/shard_map/ppermute | solution.py:519
  157.8 13.0 %collective-permute-start.12 = (bf16[256,896]{1,0:T(8,128)(2,1)}, bf16[256,896]{1,0:T(8,128)(2,1)}, u32[]{:S(2)}, u32[]{:S(2)}) collective-permute-start(bf16[256,896]{1,0:T(8,128)(2,1)} %get-tuple-element.108), channel_id=1, source_target_pairs={{2,0},{3,1},{4,2},{5,3},{6,4},{7,5},{10,8},{11,9},{12,10},{13,11},... | collective-permute-start | bytes 1376264 | tf_op jit(solution)/shard_map/ppermute | solution.py:520
  160.8 159.1 %reduce-scatter.33.cloned.1.call-start = ((), (), s32[]{:S(2)}) async-start(), calls=%async_computation.17 | async-start | bytes 3981312 | tf_op jit(solution)/shard_map/reduce_scatter | solution.py:667
  160.9 38.1 %collective-permute-start.9 = (bf16[256,896]{1,0:T(8,128)(2,1)}, bf16[256,896]{1,0:T(8,128)(2,1)S(1)}, u32[]{:S(2)}, u32[]{:S(2)}) collective-permute-start(bf16[256,896]{1,0:T(8,128)(2,1)} %get-tuple-element.108), channel_id=1, source_target_pairs={{0,1},{1,0},{2,3},{3,2},{4,5},{5,4},{6,7},{7,6},{8,9},{9,8},{10,11... | collective-permute-start | bytes 1376264 | tf_op jit(solution)/shard_map/ppermute | solution.py:516
  166.3 33.7 %collective-permute-start.14 = (bf16[256,896]{1,0:T(8,128)(2,1)}, bf16[256,896]{1,0:T(8,128)(2,1)S(1)}, u32[]{:S(2)}, u32[]{:S(2)}) collective-permute-start(bf16[256,896]{1,0:T(8,128)(2,1)} %collective-permute-done.10), channel_id=1, source_target_pairs={{0,2},{1,3},{2,4},{3,5},{4,6},{5,7},{8,10},{9,11},{10,12},{11,13},... | collective-permute-start | bytes 1376264 | tf_op jit(solution)/shard_map/ppermute | solution.py:519
  170.8 29.9 %collective-permute-start.11 = (bf16[256,896]{1,0:T(8,128)(2,1)}, bf16[256,896]{1,0:T(8,128)(2,1)S(1)}, u32[]{:S(2)}, u32[]{:S(2)}) collective-permute-start(bf16[256,896]{1,0:T(8,128)(2,1)} %collective-permute-done.10), channel_id=1, source_target_pairs={{0,1},{1,0},{2,3},{3,2},{4,5},{5,4},{6,7},{7,6},{8,9},{9,8},{10,11... | collective-permute-start | bytes 1376264 | tf_op jit(solution)/shard_map/ppermute | solution.py:521
  170.8 29.3 %collective-permute-start.16 = (bf16[256,896]{1,0:T(8,128)(2,1)}, bf16[256,896]{1,0:T(8,128)(2,1)S(1)}, u32[]{:S(2)}, u32[]{:S(2)}) collective-permute-start(bf16[256,896]{1,0:T(8,128)(2,1)} %collective-permute-done.12), channel_id=1, source_target_pairs={{2,0},{3,1},{4,2},{5,3},{6,4},{7,5},{10,8},{11,9},{12,10},{13,11},... | collective-permute-start | bytes 1376264 | tf_op jit(solution)/shard_map/ppermute | solution.py:520
  198.4 3.4 collective-permute-start.13
  200.2 2.5 collective-permute-start.17
  223.5 152.1 %reduce-scatter.47.cloned.1.call-start = ((), (), s32[]{:S(2)}) async-start(), calls=%async_computation.24 | async-start | bytes 5308416 | tf_op jit(solution)/shard_map/reduce_scatter | solution.py:667
  230.7 200.7 %reduce-scatter.43.cloned.1.call-start = ((), (), s32[]{:S(2)}) async-start(), calls=%async_computation.22 | async-start | bytes 5308416 | tf_op jit(solution)/shard_map/reduce_scatter | solution.py:667
  237.0 235.6 %reduce-scatter.39.cloned.1.call-start = ((), (), s32[]{:S(2)}) async-start(), calls=%async_computation.20 | async-start | bytes 3538944 | tf_op jit(solution)/shard_map/reduce_scatter | solution.py:667
  242.6 262.6 %reduce-scatter.49.cloned.1.call-start = ((), (), s32[]{:S(2)}) async-start(), calls=%async_computation.25 | async-start | bytes 442368
  256.5 273.4 %reduce-scatter.59.cloned.1.call-start = ((), (), s32[]{:S(2)}) async-start(), calls=%async_computation.30 | async-start | bytes 245760
  258.4 298.9 %reduce-scatter.55.cloned.1.call-start = ((), (), s32[]{:S(2)}) async-start(), calls=%async_computation.28 | async-start | bytes 245760
  260.2 324.3 %reduce-scatter.53.cloned.1.call-start = ((), (), s32[]{:S(2)}) async-start(), calls=%async_computation.27 | async-start | bytes 245760
  277.4 335.1 %reduce-scatter.51.cloned.1.call-start = ((), (), s32[]{:S(2)}) async-start(), calls=%async_computation.26 | async-start | bytes 737280
  322.1 318.5 %reduce-scatter.61.cloned.1.call-start = ((), (), s32[]{:S(2)}) async-start(), calls=%async_computation.31 | async-start | bytes 737280
  377.8 290.6 %reduce-scatter.45.cloned.1.call-start = ((), (), s32[]{:S(2)}) async-start(), calls=%async_computation.23 | async-start | bytes 737280 | tf_op jit(solution)/shard_map/reduce_scatter | solution.py:668
  431.4 264.3 %reduce-scatter.57.cloned.1.call-start = ((), (), s32[]{:S(2)}) async-start(), calls=%async_computation.29 | async-start | bytes 491520
  (133 other events, 1769.3 us)
Sparse Core Ops, SparseCore 0:
  104.8 62.4 reduce-scatter.30
  169.5 39.7 reduce-scatter.40
  211.6 30.9 reduce-scatter.36
  244.7 30.8 reduce-scatter.34
  277.8 42.0 reduce-scatter.32
  322.2 53.4 reduce-scatter.46
  378.1 53.3 reduce-scatter.42
  433.8 38.6 reduce-scatter.38
  475.4 29.7 reduce-scatter.48
  507.8 22.0 reduce-scatter.58
  533.3 23.9 reduce-scatter.54
  560.5 23.9 reduce-scatter.52
  587.3 25.0 reduce-scatter.50
  615.4 25.0 reduce-scatter.60
  643.3 25.0 reduce-scatter.44
  671.3 24.4 reduce-scatter.56
where the time goes:
time: 716 us; the launch traced here: 704 us
  waiting for transfers between devices  417 us (58%)
  Pallas kernels  86.6 us (12%)
  matrix products  59.1 us (8%)
  starting transfers between devices  54.5 us (8%)
  local copies, waits for them, and re-layouts  52.2 us (7%)
  other arithmetic  18.8 us (3%)
  between operations  16.4 us (2%)
    reduce_scatter x7, waiting for transfers between devices, reduce_weight(): lax.psum_scatter(grad.astype(jnp.bfloat16), 'seq', scatter_dimension=0, t...  204 us
    unnamed x23, waiting for transfers between devices  175 us
    ppermute x4, starting transfers between devices, gather_window(): below = lax.ppermute(below, 'seq', up)  46.3 us
    unnamed x289, local copies, waits for them, and re-layouts  45.7 us
    reduce_scatter x1, waiting for transfers between devices, reduce_weight(): lax.psum_scatter(part, 'batch', scatter_dimension=1, tiled=True)  26 us
    dot_general x7, matrix products, contract_rows(): lax.dot_general(left, right, (((0,), (0,)), ((), ())), preferred_element_...  25.3 us
    pallas_call x2, Pallas kernels, attend(): pl.pallas_call(partial(attend_kernel, items, shards, kind, blocks), grid=...  25 us
    pallas_call x2, Pallas kernels, query_grad(): pl.pallas_call(partial(query_grad_kernel, items, shards, kind, blocks), g...  21.2 us
  transfers between devices with their start and end apart: 34, of which 18 were waited for; matrix products, arithmetic and copies ran while one was open for 13% of the time, Pallas kernels for 6%

commit v1 on v0

v1 whole, which is shorter than its diff:
```python
from functools import partial

import jax
import jax.numpy as jnp
from jax import lax
from jax.experimental import pallas as pl
from jax.experimental.pallas import tpu as pltpu
from jax.sharding import PartitionSpec as P

H = 12
LONGEST = 1024

epsilon = 1e-06
far = -1e30
LSE_LANE = 8
DELTA_LANE = 44
MIB = 1 << 20


def layer_norm(values):
    centred = values - jnp.mean(values, axis=-1, keepdims=True)
    inverse = lax.rsqrt(jnp.mean(centred * centred, axis=-1, keepdims=True) + epsilon)
    return (centred * inverse, inverse)


def norm_back(grad_normed, normed, inverse):
    return inverse * (
        grad_normed
        - jnp.mean(grad_normed, axis=-1, keepdims=True)
        - normed * jnp.mean(grad_normed * normed, axis=-1, keepdims=True)
    )


def contract_rows(left, right):
    return lax.dot_general(
        left, right, (((0,), (0,)), ((), ())), preferred_element_type=jnp.float32
    )


def times_transposed(left, right):
    return lax.dot_general(
        left, right, (((1,), (1,)), ((), ())), preferred_element_type=jnp.float32
    )


class Frame:
    def __init__(self, meta, items, count, shards):
        self.position = meta[0]
        self.items = items
        self.count = count
        self.shards = shards
        self.ends = []
        total = jnp.int32(0)
        for item in range(items):
            total = total + meta[1 + item]
            self.ends.append(total)
        self.text_len = [meta[1 + items + item] for item in range(items)]
        self.first = self.item_of(self.position * count)
        self.last = self.item_of(self.position * count + count - 1)
        self.low = jnp.int32(0)
        self.high = jnp.int32(0)
        for item in range(items):
            start = self.ends[item] - meta[1 + item]
            self.low = jnp.where(self.first == item, start, self.low)
            self.high = jnp.where(self.last == item, self.ends[item], self.high)

    def item_of(self, place):
        found = jnp.int32(0)
        for end in self.ends:
            found = found + (place >= end).astype(jnp.int32)
        return found

    def items_of_rows(self, base, rows):
        place = base + lax.broadcasted_iota(jnp.int32, (rows, 1), 0)
        found = jnp.zeros((rows, 1), jnp.int32)
        for end in self.ends:
            found = found + (place >= end).astype(jnp.int32)
        return found

    def base(self, block):
        pair = block // 2
        hop = (pair + 1) // 2
        step = jnp.where(pair % 2 == 1, -hop, hop)
        chip = self.position // 2 + step
        device = chip * 2 + (self.position % 2 + block % 2) % 2
        start = device * self.count
        live = (chip >= 0) & (chip < self.shards // 2)
        return start, live & (start < self.high) & (start + self.count > self.low)


def lanes(rows):
    return lax.broadcasted_iota(jnp.int32, (rows, 128), 1)


def lse_lanes(lane):
    return (lane >= LSE_LANE) & (lane < DELTA_LANE)


def delta_lanes(lane):
    return (lane >= DELTA_LANE) & (lane < DELTA_LANE + 3 * H)


def head_lanes(lane, base, head):
    start = base + 3 * head
    return (lane >= start) & (lane < start + 3)


def beside(left, right):
    return jnp.concatenate([left.astype(jnp.bfloat16), right.astype(jnp.bfloat16)], axis=1)


def pieces(values):
    high = values.astype(jnp.bfloat16).astype(jnp.float32)
    rest = values - high
    middle = rest.astype(jnp.bfloat16).astype(jnp.float32)
    return high, middle, rest - middle


def dot(left, right):
    return jnp.dot(left, right, preferred_element_type=jnp.float32)


def stack_heads(target, values, features):
    rows = values.shape[0]
    half = lanes(rows) // 64
    wide = values.astype(jnp.float32)
    for h in range(2):
        target[h * rows : (h + 1) * rows, :] = beside(jnp.where(half == h, wide, 0.0), features[h])


def merge_heads(stacked):
    rows = stacked.shape[0] // 2
    return jnp.where(lanes(rows) < 64, stacked[:rows], stacked[rows:])


def window_bias(frame, block):
    base, _ = frame.base(block)
    item = frame.items_of_rows(base, frame.count)
    lane = lanes(frame.count)
    return jnp.where((lane != item) & (lane < frame.items), far, 0.0)


def text_bias(frame, block, rows):
    slot = lax.broadcasted_iota(jnp.int32, (rows, 1), 0)
    length = jnp.int32(0)
    for item in range(frame.items):
        length = jnp.where(block == item, frame.text_len[item], length)
    lane = lanes(rows)
    dead = (lane != block) | (slot >= length)
    return jnp.where(dead & (lane < frame.items), far, 0.0)


def block_rule(frame, kind, rows):
    if kind == "frames":
        return (
            lambda block: frame.base(block)[1],
            lambda block: window_bias(frame, block),
        )
    return (
        lambda block: (block >= frame.first) & (block <= frame.last),
        lambda block: text_bias(frame, block, rows),
    )


def rows_of(block, rows):
    return pl.ds(pl.multiple_of(block * rows, rows), rows)


def each_active(blocks, active, step):
    @pl.loop(0, blocks)
    def _(block):
        @pl.when(active(block))
        def _():
            step(block)


def fill_bias(blocks, rows, active, bias, target, with_lse):
    @pl.when(pl.program_id(0) == 0)
    def _():
        def step(block):
            mask = bias(block)
            if with_lse:
                mask = jnp.where(lse_lanes(lanes(rows)), -1.0, mask)
            target[rows_of(block, rows), :] = mask.astype(jnp.bfloat16)

        each_active(blocks, active, step)


def project_kernel(items, shards, blocks, meta, mod_ref, *refs):
    w_refs, x_refs = refs[:2], refs[2:-2]
    hidden_ref, out_ref = refs[-2:]
    count, width = x_refs[0].shape
    frame = Frame(meta, items, count, shards)
    for number, block in enumerate(blocks):
        base, live = frame.base(jnp.int32(block))

        @pl.when(live)
        def _(number=number, base=base):
            normed, _ = layer_norm(x_refs[number][...].astype(jnp.float32))
            item = frame.items_of_rows(base, count)
            shift = jnp.zeros_like(normed)
            scale = jnp.zeros_like(normed)
            for i in range(items):
                shift = jnp.where(item == i, mod_ref[i, 0:1, :], shift)
                scale = jnp.where(item == i, mod_ref[i, 1:2, :], scale)
            hidden = (normed * (1.0 + scale) + shift).astype(jnp.bfloat16)
            here = slice(number * count, (number + 1) * count)
            hidden_ref[here, :] = hidden
            for c in range(2):
                out_ref[here, c * width : (c + 1) * width] = dot(hidden, w_refs[c][...]).astype(jnp.bfloat16)


def project(meta, modulation, weight, x_blocks, blocks, items, shards, name):
    count, width = x_blocks[0].shape
    total = len(blocks) * count
    whole = pl.BlockSpec(memory_space=pltpu.VMEM)
    return pl.pallas_call(
        partial(project_kernel, items, shards, blocks),
        grid=(1,),
        out_shape=(
            jax.ShapeDtypeStruct((total, width), jnp.bfloat16),
            jax.ShapeDtypeStruct((total, 2 * width), jnp.bfloat16),
        ),
        in_specs=[
            pl.BlockSpec(memory_space=pltpu.SMEM),
            whole,
            pl.BlockSpec((width, width), lambda i: (0, 1), pipeline_mode=pl.Buffered(1)),
            pl.BlockSpec((width, width), lambda i: (0, 2), pipeline_mode=pl.Buffered(1)),
        ]
        + [whole] * len(blocks),
        out_specs=(whole, whole),
        compiler_params=pltpu.CompilerParams(vmem_limit_bytes=40 * MIB),
        cost_estimate=pl.CostEstimate(
            flops=2 * total * width * width,
            bytes_accessed=2 * 4 * total * width,
            transcendentals=0,
        ),
        name=name,
    )(meta, modulation, weight, weight, *x_blocks)


def window_queries_kernel(items, shards, blocks, meta, h_ref, w_ref, q_ref):
    count = h_ref.shape[0] // blocks
    frame = Frame(meta, items, count, shards)

    def step(block):
        here = rows_of(block, count)
        q = dot(h_ref[here, :], w_ref[...]).astype(jnp.bfloat16)
        q_ref[here, :] = (q.astype(jnp.float32) * 0.125).astype(jnp.bfloat16)

    each_active(blocks, lambda block: frame.base(block)[1], step)


def window_queries(meta, hidden, weight, blocks, items, shards):
    total, width = hidden.shape
    whole = pl.BlockSpec(memory_space=pltpu.VMEM)
    return pl.pallas_call(
        partial(window_queries_kernel, items, shards, blocks),
        grid=(1,),
        out_shape=jax.ShapeDtypeStruct((total, width), jnp.bfloat16),
        in_specs=[
            pl.BlockSpec(memory_space=pltpu.SMEM),
            whole,
            pl.BlockSpec((width, width), lambda i: (0, 0), pipeline_mode=pl.Buffered(1)),
        ],
        out_specs=whole,
        compiler_params=pltpu.CompilerParams(vmem_limit_bytes=40 * MIB),
        cost_estimate=pl.CostEstimate(flops=total * width * width, bytes_accessed=4 * total * width, transcendentals=0),
        name="window_queries",
    )(meta, hidden, weight)


def attend_kernel(items, shards, kind, blocks, meta, q_ref, k_ref, v_ref, o_ref, low_ref, f_ref, qa, bias_ref, s, m, l, acc):
    count = q_ref.shape[0]
    rows = k_ref.shape[0] // blocks
    frame = Frame(meta, items, count, shards)
    active, bias = block_rule(frame, kind, rows)
    pair = pl.program_id(0)
    lane = lanes(count)
    own = frame.items_of_rows(frame.position * count, count)
    own_item = (lane == own).astype(jnp.float32)
    fill_bias(blocks, rows, active, bias, bias_ref, False)
    stack_heads(qa, q_ref[...], [own_item, own_item])
    m[...] = jnp.full((2 * count, 128), far, jnp.float32)
    l[...] = jnp.zeros((2 * count, 128), jnp.float32)
    acc[...] = jnp.zeros((2 * count, 128), jnp.float32)

    def score(block):
        here = rows_of(block, rows)
        scores = times_transposed(qa[...], jnp.concatenate([k_ref[here, :], bias_ref[here, :]], axis=1))
        s[block] = scores
        m[...] = jnp.maximum(m[...], jnp.maximum(scores[:, :128], scores[:, 128:]))

    each_active(blocks, active, score)
    top = jnp.max(m[...], axis=1, keepdims=True)
    m[...] = jnp.broadcast_to(top, (2 * count, 128))

    def weigh(block):
        here = rows_of(block, rows)
        high = m[...]
        left = jnp.exp(s[block, :, :128] - high)
        right = jnp.exp(s[block, :, 128:] - high)
        l[...] = l[...] + (left + right)
        acc[...] = acc[...] + dot(beside(left, right), v_ref[here, :])

    each_active(blocks, active, weigh)
    total = jnp.sum(l[...], axis=1, keepdims=True)
    result = merge_heads(acc[...] / total)
    lse = top + jnp.log(total)
    features = jnp.where(pair == 0, own_item, f_ref[...].astype(jnp.float32))
    for h in range(2):
        start = LSE_LANE + 3 * (2 * pair + h)
        for number, piece in enumerate(pieces(lse[h * count : (h + 1) * count])):
            features = jnp.where(lane == start + number, piece, features)
    o_ref[...] = result
    low_ref[...] = result.astype(jnp.bfloat16)
    f_ref[...] = features.astype(jnp.bfloat16)


def attend(meta, queries, kv, kind, blocks, items, shards, name):
    count, width = queries.shape
    pairs = width // 128
    total = kv.shape[0]
    rows = total // blocks
    column = lambda offset: (lambda p: (0, p + offset))
    tile = pl.BlockSpec((count, 128), column(0))
    return pl.pallas_call(
        partial(attend_kernel, items, shards, kind, blocks),
        grid=(pairs,),
        out_shape=(
            jax.ShapeDtypeStruct((count, width), jnp.float32),
            jax.ShapeDtypeStruct((count, width), jnp.bfloat16),
            jax.ShapeDtypeStruct((count, 128), jnp.bfloat16),
        ),
        in_specs=[
            pl.BlockSpec(memory_space=pltpu.SMEM),
            tile,
            pl.BlockSpec((total, 128), column(0)),
            pl.BlockSpec((total, 128), column(pairs)),
        ],
        out_specs=(tile, tile, pl.BlockSpec((count, 128), lambda p: (0, 0))),
        scratch_shapes=[
            pltpu.VMEM((2 * count, 256), jnp.bfloat16),
            pltpu.VMEM((total, 128), jnp.bfloat16),
            pltpu.VMEM((blocks, 2 * count, rows), jnp.float32),
            pltpu.VMEM((2 * count, 128), jnp.float32),
            pltpu.VMEM((2 * count, 128), jnp.float32),
            pltpu.VMEM((2 * count, 128), jnp.float32),
        ],
        compiler_params=pltpu.CompilerParams(vmem_limit_bytes=40 * MIB),
        cost_estimate=pl.CostEstimate(
            flops=2 * count * total * width,
            bytes_accessed=4 * total * width,
            transcendentals=count * total * H // 2,
        ),
        name=name,
    )(meta, queries, kv, kv)


def query_side(pair, f_ref, q_ref, do_ref, qa, da):
    lane = lanes(q_ref.shape[0])
    features = f_ref[...].astype(jnp.float32)
    heads = [2 * pair, 2 * pair + 1]
    stack_heads(
        qa,
        q_ref[...],
        [jnp.where((lane < LSE_LANE) | head_lanes(lane, LSE_LANE, head), features, 0.0) for head in heads],
    )
    stack_heads(
        da, do_ref[...], [jnp.where(head_lanes(lane, DELTA_LANE, head), features, 0.0) for head in heads]
    )


def query_step(qa, da, keys, values, bias):
    minus = jnp.where(delta_lanes(lanes(keys.shape[0])), -1.0, 0.0)
    probs = jnp.exp(times_transposed(qa[...], jnp.concatenate([keys, bias], axis=1)))
    slope = times_transposed(da[...], beside(values, minus))
    return dot((probs * slope).astype(jnp.bfloat16), keys)


def key_side(frame, pair, k, v, mask, ka, va):
    lane = lanes(k.shape[0])
    heads = [2 * pair, 2 * pair + 1]
    stack_heads(ka, k, [jnp.where(head_lanes(lane, LSE_LANE, head), -1.0, mask) for head in heads])
    stack_heads(va, v, [jnp.where(head_lanes(lane, DELTA_LANE, head), -1.0, 0.0) for head in heads])


def key_step(ka, va, q, do, features):
    probs = jnp.exp(times_transposed(ka[...], jnp.concatenate([q, features], axis=1)))
    slope = times_transposed(va[...], jnp.concatenate([do, features], axis=1))
    return dot((probs * slope).astype(jnp.bfloat16), q), dot(probs.astype(jnp.bfloat16), do)


def query_grad_kernel(items, shards, blocks, meta, q_ref, do_ref, f_ref, k_ref, v_ref, dq_ref, qa, da, bias_ref, acc):
    count = q_ref.shape[0]
    rows = k_ref.shape[0] // blocks
    frame = Frame(meta, items, count, shards)
    active, bias = block_rule(frame, "frames", rows)
    fill_bias(blocks, rows, active, bias, bias_ref, True)
    query_side(pl.program_id(0), f_ref, q_ref, do_ref, qa, da)
    acc[...] = jnp.zeros((2 * count, 128), jnp.float32)

    def step(block):
        here = rows_of(block, rows)
        acc[...] = acc[...] + query_step(qa, da, k_ref[here, :], v_ref[here, :], bias_ref[here, :])

    each_active(blocks, active, step)
    dq_ref[...] = (merge_heads(acc[...]) * 0.125).astype(jnp.bfloat16)


def query_grad(meta, queries, grad_out, features, kv, blocks, items, shards, name):
    count, width = queries.shape
    pairs = width // 128
    total = kv.shape[0]
    column = lambda offset: (lambda p: (0, p + offset))
    tile = pl.BlockSpec((count, 128), column(0))
    return pl.pallas_call(
        partial(query_grad_kernel, items, shards, blocks),
        grid=(pairs,),
        out_shape=jax.ShapeDtypeStruct((count, width), jnp.bfloat16),
        in_specs=[
            pl.BlockSpec(memory_space=pltpu.SMEM),
            tile,
            tile,
            pl.BlockSpec((count, 128), lambda p: (0, 0)),
            pl.BlockSpec((total, 128), column(0)),
            pl.BlockSpec((total, 128), column(pairs)),
        ],
        out_specs=tile,
        scratch_shapes=[
            pltpu.VMEM((2 * count, 256), jnp.bfloat16),
            pltpu.VMEM((2 * count, 256), jnp.bfloat16),
            pltpu.VMEM((total, 128), jnp.bfloat16),
            pltpu.VMEM((2 * count, 128), jnp.float32),
        ],
        compiler_params=pltpu.CompilerParams(vmem_limit_bytes=40 * MIB),
        cost_estimate=pl.CostEstimate(
            flops=3 * count * total * width,
            bytes_accessed=4 * total * width,
            transcendentals=count * total * H // 2,
        ),
        name=name,
    )(meta, queries, grad_out, features, kv, kv)


def frame_key_grad_kernel(items, shards, blocks, meta, q_ref, do_ref, f_ref, k_ref, v_ref, dk_ref, dv_ref, ka, va, dka, dva):
    count = k_ref.shape[0]
    frame = Frame(meta, items, count, shards)
    key_side(frame, pl.program_id(0), k_ref[...], v_ref[...], window_bias(frame, jnp.int32(0)), ka, va)
    dka[...] = jnp.zeros((2 * count, 128), jnp.float32)
    dva[...] = jnp.zeros((2 * count, 128), jnp.float32)

    def step(block):
        here = rows_of(block, count)
        dk, dv = key_step(ka, va, q_ref[here, :], do_ref[here, :], f_ref[here, :])
        dka[...] = dka[...] + dk
        dva[...] = dva[...] + dv

    each_active(blocks, lambda block: frame.base(block)[1], step)
    dk_ref[...] = merge_heads(dka[...]).astype(jnp.bfloat16)
    dv_ref[...] = merge_heads(dva[...]).astype(jnp.bfloat16)


def frame_key_grad(meta, q_window, do_window, kv, count, blocks, items, shards, name):
    total, width = q_window.shape
    pairs = width // 128
    column = lambda offset: (lambda p: (0, p + offset))
    tile = pl.BlockSpec((count, 128), column(0))
    wide = pl.BlockSpec((total, 128), column(0))
    return pl.pallas_call(
        partial(frame_key_grad_kernel, items, shards, blocks),
        grid=(pairs,),
        out_shape=(jax.ShapeDtypeStruct((count, width), jnp.bfloat16),) * 2,
        in_specs=[
            pl.BlockSpec(memory_space=pltpu.SMEM),
            wide,
            wide,
            pl.BlockSpec((total, 128), lambda p: (0, pairs)),
            tile,
            pl.BlockSpec((count, 128), column(pairs)),
        ],
        out_specs=(tile, tile),
        scratch_shapes=[pltpu.VMEM((2 * count, 256), jnp.bfloat16)] * 2
        + [pltpu.VMEM((2 * count, 128), jnp.float32)] * 2,
        compiler_params=pltpu.CompilerParams(vmem_limit_bytes=40 * MIB),
        cost_estimate=pl.CostEstimate(
            flops=4 * count * total * width,
            bytes_accessed=4 * total * width,
            transcendentals=count * total * H // 2,
        ),
        name=name,
    )(meta, q_window, do_window, do_window, kv, kv)


def text_grad_kernel(items, shards, meta, q_ref, do_ref, f_ref, k_ref, v_ref, dq_ref, dkv_ref, qa, da, ka, va, acc):
    count = q_ref.shape[0]
    rows = k_ref.shape[0] // items
    share = rows // shards
    frame = Frame(meta, items, count, shards)
    pair = pl.program_id(0)
    query_side(pair, f_ref, q_ref, do_ref, qa, da)
    acc[...] = jnp.zeros((2 * count, 128), jnp.float32)

    @pl.loop(0, items)
    def _(item):
        here = rows_of(item, rows)
        live = (item >= frame.first) & (item <= frame.last)
        target = pl.ds(pl.multiple_of(item * share, share), share)

        @pl.when(live)
        def _():
            keys, values = k_ref[here, :], v_ref[here, :]
            mask = text_bias(frame, item, rows)
            bias = jnp.where(lse_lanes(lanes(rows)), -1.0, mask).astype(jnp.bfloat16)
            acc[...] = acc[...] + query_step(qa, da, keys, values, bias)
            key_side(frame, pair, keys, values, mask, ka, va)
            grads = key_step(ka, va, q_ref[...], do_ref[...], f_ref[...])
            for which, grad in enumerate(grads):
                merged = merge_heads(grad).astype(jnp.bfloat16)
                for piece in range(shards):
                    dkv_ref[which, piece ^ frame.position, target, :] = merged[piece * share : (piece + 1) * share]

        @pl.when(jnp.logical_not(live))
        def _():
            for which in range(2):
                for piece in range(shards):
                    dkv_ref[which, piece, target, :] = jnp.zeros((share, 128), jnp.bfloat16)

    dq_ref[...] = (merge_heads(acc[...]) * 0.125).astype(jnp.bfloat16)


def text_grad(meta, queries, grad_out, features, kv, items, shards, name):
    count, width = queries.shape
    pairs = width // 128
    total = kv.shape[0]
    column = lambda offset: (lambda p: (0, p + offset))
    tile = pl.BlockSpec((count, 128), column(0))
    rows = total // items
    return pl.pallas_call(
        partial(text_grad_kernel, items, shards),
        grid=(pairs,),
        out_shape=(
            jax.ShapeDtypeStruct((count, width), jnp.bfloat16),
            jax.ShapeDtypeStruct((2, shards, total // shards, width), jnp.bfloat16),
        ),
        in_specs=[
            pl.BlockSpec(memory_space=pltpu.SMEM),
            tile,
            tile,
            pl.BlockSpec((count, 128), lambda p: (0, 0)),
            pl.BlockSpec((total, 128), column(0)),
            pl.BlockSpec((total, 128), column(pairs)),
        ],
        out_specs=(tile, pl.BlockSpec((2, shards, total // shards, 128), lambda p: (0, 0, 0, p))),
        scratch_shapes=[pltpu.VMEM((2 * count, 256), jnp.bfloat16)] * 2
        + [pltpu.VMEM((2 * rows, 256), jnp.bfloat16)] * 2
        + [pltpu.VMEM((2 * count, 128), jnp.float32)],
        compiler_params=pltpu.CompilerParams(vmem_limit_bytes=40 * MIB),
        cost_estimate=pl.CostEstimate(
            flops=7 * count * rows * 2 * width,
            bytes_accessed=8 * total * width,
            transcendentals=count * rows * H * 2,
        ),
        name=name,
    )(meta, queries, grad_out, features, kv, kv)


UNIT = 192


def turned(x_ref, start, width):
    eye = (
        lax.broadcasted_iota(jnp.int32, (width, width), 0) == lax.broadcasted_iota(jnp.int32, (width, width), 1)
    ).astype(jnp.bfloat16)
    return times_transposed(eye, x_ref[:, pl.ds(pl.multiple_of(start, 128), width)]).astype(jnp.bfloat16)


def turned_rows(x_ref, core):
    row = lax.broadcasted_iota(jnp.int32, (384, 768), 0)
    column = lax.broadcasted_iota(jnp.int32, (384, 768), 1)
    chip = (row >= 96).astype(jnp.int32) + (row >= 192).astype(jnp.int32) + (row >= 288).astype(jnp.int32)
    pick = (column == row + 96 * (chip + core)).astype(jnp.bfloat16)
    return times_transposed(pick, x_ref[...]).astype(jnp.bfloat16)


def pack_kernel(items, kinds, firsts, meta, *refs):
    position = meta[0]
    core, chip = position % 2, position // 2
    mine = meta[1 + 2 * items]
    inputs = refs[: 4 * len(kinds)]
    outputs = refs[4 * len(kinds) :]

    def store(group, owner, owner_chip, row, values):
        relative = owner ^ mine
        first = firsts[group]
        low = values.astype(jnp.bfloat16)
        where = ((relative >> (1 - first)) % 2, owner_chip ^ chip, slice(row, row + values.shape[0]))

        @pl.when((relative >> first) % 2 == 1)
        def _():
            outputs[2 * group][where] = low

        @pl.when((relative >> first) % 2 == 0)
        def _():
            outputs[2 * group + 1][where] = low

    def store_split(group, pair, row, values, chips):
        rolled = pltpu.roll(values, UNIT, 1)
        each = values.shape[0] // len(chips)
        left = lax.broadcasted_iota(jnp.int32, (each // 2, 384), 1) < UNIT
        for number, owner_chip in enumerate(chips):
            upper = slice(number * each, number * each + each // 2)
            lower = slice(number * each + each // 2, (number + 1) * each)
            store(group, 2 * pair, owner_chip, row, jnp.where(left, values[upper], rolled[lower]))
            store(group, 2 * pair + 1, owner_chip, row, jnp.where(left, rolled[upper], values[lower]))

    row = 0
    for number, kind in enumerate(kinds):
        x_own, x_sib, y_own, y_sib = inputs[4 * number : 4 * number + 4]

        def product(own, sib, column):
            here = pl.ds(column * 384, 384) if isinstance(column, int) else pl.ds(pl.multiple_of(column * 384, 128), 384)
            return dot(own, y_own[:, here]) + dot(sib, y_sib[:, here])

        if kind == "down":
            for owner_chip in range(4):
                start = owner_chip * 768 + core * 384
                own, sib = turned(x_own, start, 384), turned(x_sib, start, 384)
                for pair in range(2):
                    store_split(0, pair, row, product(own, sib, pair), [owner_chip])
            row += 192
        elif kind == "text":
            for owner_chip in range(4):
                start = owner_chip * 256 + core * 128
                own, sib = turned(x_own, start, 128), turned(x_sib, start, 128)
                for owner in range(4):
                    store(0, owner, owner_chip, row, product(own, sib, owner))
            row += 128
        else:
            own, sib = turned_rows(x_own, core), turned_rows(x_sib, core)
            if kind == "square":
                for pair in range(2):
                    store_split(0, pair, row, product(own, sib, pair), range(4))
                row += 48
            elif kind == "up":
                for column in range(8):
                    values = product(own, sib, column)
                    for owner_chip in range(4):
                        store(
                            0,
                            column // 2,
                            owner_chip,
                            row + (column % 2) * 96,
                            values[owner_chip * 96 : (owner_chip + 1) * 96],
                        )
                row += 192
            elif kind == "qkv":
                for owner, column in enumerate((0, 2, 3, 5)):
                    values = product(own, sib, column)
                    for owner_chip in range(4):
                        store(0, owner, owner_chip, 0, values[owner_chip * 96 : (owner_chip + 1) * 96])
                for pair, column in enumerate((1, 4)):
                    store_split(1, pair, 0, product(own, sib, column), range(4))


PACKED_ROWS = {"down": 192, "text": 128, "square": 48, "up": 192}


def pack(meta, kinds, operands, firsts, items, name):
    group_rows = [96, 48] if kinds == ("qkv",) else [sum(PACKED_ROWS[kind] for kind in kinds)]
    whole = pl.BlockSpec(memory_space=pltpu.VMEM)
    shapes = [jax.ShapeDtypeStruct((2, 4, rows, 384), jnp.bfloat16) for rows in group_rows for _ in range(2)]
    return pl.pallas_call(
        partial(pack_kernel, items, kinds, firsts),
        out_shape=tuple(shapes),
        in_specs=[pl.BlockSpec(memory_space=pltpu.SMEM)] + [whole] * len(operands),
        out_specs=tuple([whole] * len(shapes)),
        compiler_params=pltpu.CompilerParams(vmem_limit_bytes=40 * MIB),
        cost_estimate=pl.CostEstimate(
            flops=2 * 512 * 16 * sum(group_rows) * 384,
            bytes_accessed=32 * sum(group_rows) * 384,
            transcendentals=0,
        ),
        name=name,
    )(meta, *operands)


def trade(values, axis, bit):
    size = lax.axis_size(axis)
    return lax.ppermute(values, axis, [(i, i ^ (1 << bit)) for i in range(size)])


def halve(keep, send, axis, bit):
    total = keep.astype(jnp.float32) + trade(send, axis, bit).astype(jnp.float32)
    return total


def reduce_packed(send, keep, first):
    part = halve(keep, send, "batch", first).astype(jnp.bfloat16)
    part = halve(part[0], part[1], "batch", 1 - first).astype(jnp.bfloat16)
    part = part.reshape(2, 2, *part.shape[1:])
    part = halve(part[:, 0], part[:, 1], "seq", 1).astype(jnp.bfloat16)
    return halve(part[0], part[1], "seq", 2)


def unsplit(rows):
    return jnp.concatenate([rows[:, :UNIT], rows[:, UNIT:]], axis=0)


def with_deltas(features, grad_out, attn_exact):
    width = attn_exact.shape[1]
    lane = jnp.arange(128)[None, :]
    head = (jnp.arange(width) // (width // H))[:, None]
    pick = ((lane >= DELTA_LANE) & ((lane - DELTA_LANE) // 3 == head)).astype(jnp.float32)
    delta = jnp.dot(
        grad_out.astype(jnp.float32) * attn_exact,
        pick,
        precision=lax.Precision.HIGHEST,
        preferred_element_type=jnp.float32,
    )
    high = lax.reduce_precision(delta, 8, 7)
    middle = lax.reduce_precision(delta - high, 8, 7)
    which = (lane - DELTA_LANE) % 3
    piece = jnp.where(which == 0, high, jnp.where(which == 1, middle, delta - high - middle))
    inside = (lane >= DELTA_LANE) & (lane < DELTA_LANE + 3 * H)
    return jnp.where(inside, piece.astype(jnp.bfloat16), features)


def gather_window(own, reach, shards):
    swap = [(i, i ^ 1) for i in range(shards)]
    up = [(i, i + 2) for i in range(shards - 2)]
    down = [(i + 2, i) for i in range(shards - 2)]
    blocks = [own, lax.ppermute(own, "seq", swap)]
    below, above = own, own
    for _ in range(reach):
        below = lax.ppermute(below, "seq", up)
        above = lax.ppermute(above, "seq", down)
        blocks += [below, lax.ppermute(below, "seq", swap)]
        blocks += [above, lax.ppermute(above, "seq", swap)]
    return blocks


def body(
    frames,
    cotangent,
    modulation,
    lengths,
    text,
    text_len,
    w_qkv,
    w_o,
    w_cq,
    w_ckv,
    w_co,
    w_up,
    w_down,
):
    local = frames[0]
    count, width = local.shape
    items = lengths.shape[1]
    text_rows, text_width = text.shape[2:]
    shards = lax.axis_size("seq")
    position = lax.axis_index("seq")
    reach = min(-(-(LONGEST - 1) // (2 * count)), shards // 2 - 1)
    blocks = 2 + 4 * reach
    meta = jnp.concatenate(
        [position[None].astype(jnp.int32), lengths[0], text_len[0], lax.axis_index("batch")[None].astype(jnp.int32)]
    )
    item_range = jnp.arange(items, dtype=jnp.int32)
    ends = jnp.sum(jnp.where(item_range[None, :] <= item_range[:, None], lengths[0][None, :], 0), axis=1)
    place = position * count + jnp.arange(count, dtype=jnp.int32)
    query_items = jnp.sum((place[:, None] >= ends[None, :]).astype(jnp.int32), axis=1)[:, None]
    one_hot = (query_items == item_range[None, :]).astype(jnp.float32)
    mod = modulation[0]

    def per_frame(which):
        found = jnp.broadcast_to(mod[0, which][None, :], (count, width))
        for item in range(1, items):
            found = jnp.where(query_items == item, mod[item, which][None, :], found)
        return found

    swap = [(i, i ^ 1) for i in range(shards)]

    def sibling(values):
        return lax.ppermute(values, "seq", swap)

    fast = shards == 8 and lax.axis_size("batch") == 4 and width == 768
    window = gather_window(local, reach, shards)
    inputs = local.astype(jnp.float32)
    normed_one, inverse_one = layer_norm(inputs)
    hidden_one = (normed_one * (1.0 + per_frame(1)) + per_frame(0)).astype(jnp.bfloat16)
    queries = jnp.dot(hidden_one, w_qkv[:, :width], preferred_element_type=jnp.float32).astype(jnp.bfloat16)
    queries = (queries.astype(jnp.float32) * 0.125).astype(jnp.bfloat16)
    text_proj = jnp.dot(
        text[0].reshape(items * text_rows, text_width), w_ckv, preferred_element_type=jnp.float32
    ).astype(jnp.bfloat16)
    hidden_window, kv = project(meta, mod, w_qkv, window, tuple(range(blocks)), items, shards, "project_keys")
    attn_exact, attended, features = attend(meta, queries, kv, "frames", blocks, items, shards, "self_attend")
    branch_one = jnp.dot(attended, w_o, preferred_element_type=jnp.float32)
    after_attn = inputs + per_frame(2) * branch_one
    normed_cross, inverse_cross = layer_norm(after_attn)
    cross_in = normed_cross.astype(jnp.bfloat16)
    cross_queries = jnp.dot(cross_in, w_cq, preferred_element_type=jnp.float32).astype(jnp.bfloat16)
    cross_queries = (cross_queries.astype(jnp.float32) * 0.125).astype(jnp.bfloat16)
    cross_exact, cross_out, cross_features = attend(
        meta, cross_queries, text_proj, "text", items, items, shards, "cross_attend"
    )
    branch_two = jnp.dot(cross_out, w_co, preferred_element_type=jnp.float32)
    after_cross = after_attn + branch_two
    normed_two, inverse_two = layer_norm(after_cross)
    hidden_two = (normed_two * (1.0 + per_frame(4)) + per_frame(3)).astype(jnp.bfloat16)
    pre_act = jnp.dot(hidden_two, w_up, preferred_element_type=jnp.float32)
    activated, gelu_back = jax.vjp(partial(jax.nn.gelu, approximate=True), pre_act)
    activated_low = activated.astype(jnp.bfloat16)
    gate_two = per_frame(5)
    grad_out = cotangent[0].astype(jnp.float32)
    grad_branch_three = (grad_out * gate_two).astype(jnp.bfloat16)
    grad_pre = gelu_back(times_transposed(grad_branch_three, w_down))[0].astype(jnp.bfloat16)
    branch_three = jnp.dot(activated_low, w_down, preferred_element_type=jnp.float32)
    result = after_cross + gate_two * branch_three
    grad_hidden_two = times_transposed(grad_pre, w_up)
    grad_cross = grad_out + norm_back(grad_hidden_two * (1.0 + per_frame(4)), normed_two, inverse_two)
    grad_branch_two = grad_cross.astype(jnp.bfloat16)
    grad_cross_out = times_transposed(grad_branch_two, w_co).astype(jnp.bfloat16)
    cross_features = with_deltas(cross_features, grad_cross_out, cross_exact)
    grad_cross_queries, text_terms = text_grad(
        meta, cross_queries, grad_cross_out, cross_features, text_proj, items, shards, "cross_grad"
    )
    grad_attn_res = grad_cross + norm_back(
        times_transposed(grad_cross_queries, w_cq), normed_cross, inverse_cross
    )
    grad_branch_one = (grad_attn_res * per_frame(2)).astype(jnp.bfloat16)
    grad_attended = times_transposed(grad_branch_one, w_o).astype(jnp.bfloat16)
    features = with_deltas(features, grad_attended, attn_exact)
    grad_queries = query_grad(
        meta, queries, grad_attended, features, kv, blocks, items, shards, "self_query_grad"
    )
    do_window = jnp.concatenate(
        gather_window(jnp.concatenate([grad_attended, features], axis=1), reach, shards), axis=0
    )
    q_window = window_queries(meta, hidden_window, w_qkv, blocks, items, shards)
    grad_keys, grad_values = frame_key_grad(
        meta, q_window, do_window, kv, count, blocks, items, shards, "self_key_grad"
    )
    grad_projected = jnp.concatenate([grad_queries, grad_keys, grad_values], axis=1)
    grad_hidden_one = times_transposed(grad_projected, w_qkv)
    grad_inputs = grad_attn_res + norm_back(
        grad_hidden_one * (1.0 + per_frame(1)), normed_one, inverse_one
    )

    def item_sum(values):
        return lax.dot_general(
            one_hot,
            values,
            (((0,), (0,)), ((), ())),
            precision=lax.Precision.HIGHEST,
            preferred_element_type=jnp.float32,
        )

    def item_share(terms):
        total = jnp.concatenate(terms, axis=0)
        for bit in range(shards.bit_length() - 1):
            total = total + trade(total, "seq", bit)
        own = width // shards
        mine = lax.dynamic_slice_in_dim(total, position * own, own, 1)
        return mine.reshape(len(terms), items, own).transpose(1, 0, 2)

    early = item_share(
        [
            item_sum(grad_attn_res * branch_one),
            item_sum(grad_hidden_two),
            item_sum(grad_hidden_two * normed_two),
            item_sum(grad_out * branch_three),
        ]
    )
    late = item_share([item_sum(grad_hidden_one), item_sum(grad_hidden_one * normed_one)])
    grad_mod = jnp.concatenate([late, early[:, :1]], axis=1)[None]
    grad_mod_mlp = early[:, 1:][None]
    for bit in range(shards.bit_length() - 1):
        text_terms = text_terms.reshape(2, -1, 2, *text_terms.shape[2:])
        text_terms = halve(text_terms[:, :, 0], text_terms[:, :, 1], "seq", bit).astype(jnp.bfloat16)
    share_rows = text_rows // shards
    text_grad_low = jnp.concatenate([text_terms[0, 0], text_terms[1, 0]], axis=1)

    def text_of(device):
        return lax.dynamic_slice_in_dim(text[0], device * share_rows, share_rows, 1).reshape(
            items * share_rows, text_width
        )

    grad_text = times_transposed(text_grad_low, w_ckv).reshape(1, items, share_rows, text_width)
    weights = weight_grads_fast if fast else weight_grads
    return (
        result.astype(jnp.bfloat16)[None],
        grad_inputs[None],
        grad_mod,
        grad_mod_mlp,
        grad_text,
        *weights(
            meta,
            items,
            sibling,
            (hidden_one, grad_projected),
            (attended, grad_branch_one),
            (cross_in, grad_cross_queries),
            (text_of(position), text_grad_low, text_of(position ^ 1)),
            (cross_out, grad_branch_two),
            (hidden_two, grad_pre),
            (activated_low, grad_branch_three),
        ),
    )


def weight_grads(meta, items, sibling, *pairs):
    def reduce_weight(left, right, *_):
        grad = contract_rows(left, right).astype(jnp.bfloat16)
        part = lax.psum_scatter(grad, "seq", scatter_dimension=0, tiled=True)
        return lax.psum_scatter(part, "batch", scatter_dimension=1, tiled=True).astype(jnp.float32)

    return tuple(reduce_weight(*pair) for pair in pairs)


def weight_grads_fast(meta, items, sibling, qkv, o, cq, ckv, co, up, down):
    def operands(left, right):
        return (left, sibling(left), right, sibling(right))

    def pack_and_reduce(kinds, arrays, firsts, name):
        packed = pack(meta, kinds, arrays, firsts, items, name)
        return [reduce_packed(packed[2 * i], packed[2 * i + 1], first) for i, first in enumerate(firsts)]

    X, Y = 0, 1
    [down_rows] = pack_and_reduce(("down",), operands(*down), (Y,), "pack_down")
    [up_rows] = pack_and_reduce(("up",), operands(*up), (X,), "pack_up")
    [square_rows] = pack_and_reduce(
        ("square",) * 3, operands(*co) + operands(*cq) + operands(*o), (Y,), "pack_square"
    )
    text_own, low, text_sib = ckv
    [text_rows] = pack_and_reduce(("text",), (text_own, text_sib, low, sibling(low)), (X,), "pack_text")
    plain, split = pack_and_reduce(("qkv",), operands(*qkv), (X, Y), "pack_qkv")
    split = unsplit(split)
    even = lax.axis_index("batch") % 2 == 0
    grad_qkv = jnp.where(
        even, jnp.concatenate([plain, split], axis=1), jnp.concatenate([split, plain], axis=1)
    )
    return (
        grad_qkv,
        unsplit(square_rows[96:]),
        unsplit(square_rows[48:96]),
        text_rows,
        unsplit(square_rows[:48]),
        jnp.concatenate([up_rows[:96], up_rows[96:]], axis=1),
        unsplit(down_rows),
    )


def solution(mesh):
    in_specs = (
        P("batch", "seq", None),
        P("batch", "seq", None),
        P("batch", None, None, None),
        P("batch", None),
        P("batch", None, None, None),
        P("batch", None),
        P(),
        P(),
        P(),
        P(),
        P(),
        P(),
        P(),
    )
    out_specs = (
        P("batch", "seq", None),
        P("batch", "seq", None),
        P("batch", None, None, "seq"),
        P("batch", None, None, "seq"),
        P("batch", None, "seq", None),
        P("seq", "batch"),
        P("seq", "batch"),
        P("seq", "batch"),
        P("seq", "batch"),
        P("seq", "batch"),
        P("seq", "batch"),
        P("seq", "batch"),
    )
    return jax.shard_map(body, mesh=mesh, in_specs=in_specs, out_specs=out_specs, check_vma=False)
```

time: 716 us -> 461 us (0.64); the launches traced: 704 us -> 457 us
  waiting for transfers between devices: 417 us -> 99.3 us
  starting transfers between devices: 54.5 us -> 125 us
  Pallas kernels: 86.6 us -> 120 us
  matrix products: 59.1 us -> 38.2 us
  between operations: 16.4 us -> 2.58 us
  other arithmetic: 18.8 us -> 31.2 us
  local copies, waits for them, and re-layouts: 52.2 us -> 41.5 us
    reduce_scatter x9 -> x0, waiting for transfers between devices: 229 us -> none  [the longest x7 204 us: reduce_weight(): lax.psum_scatter(grad.astype(jnp.bfloat16), 'seq', scatter_dimension=0, t...]
    unnamed x23 -> x0, waiting for transfers between devices: 175 us -> none
    ppermute x0 -> x46, starting transfers between devices: none -> 98.1 us  [the longest x33 94.9 us: trade(): return lax.ppermute(values, axis, [(i, i ^ 1 << bit) for i in range(size)])]
    ppermute x0 -> x46, waiting for transfers between devices: none -> 79 us  [the longest x33 79 us: trade(): return lax.ppermute(values, axis, [(i, i ^ 1 << bit) for i in range(size)])]
    pallas_call x5 -> x9, Pallas kernels: 45.3 us -> 73.5 us  [the longest x5 26.8 us: pack(): pl.pallas_call(partial(pack_kernel, items, kinds, firsts), out_shape=tupl...]
    ppermute x4, starting transfers between devices: 46.3 us -> 20 us  [gather_window(): below = lax.ppermute(below, 'seq', up)]
    dot_general x7 -> x0, matrix products: 25.3 us -> none  [contract_rows(): lax.dot_general(left, right, (((0,), (0,)), ((), ())), preferred_element_...]
    unnamed x289 -> x174, local copies, waits for them, and re-layouts: 45.7 us -> 26.7 us
  transfers between devices with their start and end apart: 34 -> 64, of which waited for: 18 -> 22; matrix products, arithmetic and copies ran while one was open for 13% -> 14% of each run, Pallas kernels for 6% -> 14%
where the time goes in v1:
time: 461 us; the launch traced here: 457 us
  starting transfers between devices  125 us (27%)
  Pallas kernels  120 us (26%)
  waiting for transfers between devices  99.3 us (22%)
  local copies, waits for them, and re-layouts  41.5 us (9%)
  matrix products  38.2 us (8%)
  other arithmetic  31.2 us (7%)
    ppermute x33, starting transfers between devices, trade(): return lax.ppermute(values, axis, [(i, i ^ 1 << bit) for i in range(size)])  94.9 us
    ppermute x33, waiting for transfers between devices, trade(): return lax.ppermute(values, axis, [(i, i ^ 1 << bit) for i in range(size)])  79 us
    pallas_call x2, Pallas kernels, attend(): pl.pallas_call(partial(attend_kernel, items, shards, kind, blocks), grid=...  29.1 us
    pallas_call x5, Pallas kernels, pack(): pl.pallas_call(partial(pack_kernel, items, kinds, firsts), out_shape=tupl...  26.8 us
    unnamed x174, local copies, waits for them, and re-layouts  26.7 us
    ppermute x4, starting transfers between devices, gather_window(): below = lax.ppermute(below, 'seq', up)  20 us
    ppermute x4, waiting for transfers between devices, gather_window(): above = lax.ppermute(above, 'seq', down)  17.9 us
    pallas_call x1, Pallas kernels, query_grad(): pl.pallas_call(partial(query_grad_kernel, items, shards, blocks), grid=(p...  17.9 us
  transfers between devices with their start and end apart: 64, of which 22 were waited for; matrix products, arithmetic and copies ran while one was open for 14% of the time, Pallas kernels for 14%

profile of v1, /device:TPU:0, one launch (start us, length us, event | category | flops | bytes accessed | tf_op | source)
XLA Modules:
  0.0 456.8 jit_solution(3709969361882364759)
XLA Ops:
  0.7 5.9 %collective-permute-start.1 = (bf16[256,768]{1,0:T(8,128)(2,1)}, bf16[256,768]{1,0:T(8,128)(2,1)}, u32[]{:S(2)}, u32[]{:S(2)}) collective-permute-start(bf16[256,768]{1,0:T(8,128)(2,1)} %bitcast.257), channel_id=1, source_target_pairs={{0,2},{1,3},{2,4},{3,5},{4,6},{5,7},{8,10},{9,11},{10,12},{11,13},... | collective-permute-start | bytes 1179656 | tf_op jit(solution)/shard_map/ppermute | solution.py:736
  12.3 5.4 %convolution_convert_fusion.k_ref.v_ref = bf16[768,1536]{1,0:T(8,128)(2,1)} fusion(bf16[768,1024]{1,0:T(8,128)(2,1)} %bitcast.284, bf16[1024,1536]{1,0:T(8,128)(2,1)S(1)} %copy-done), kind=kOutput, calls=%fused_computation.2 | convolution fusion | flops 2417098752 | bytes 7077888 | tf_op jit(solution)/shard_map/dot_general | solution.py:794
  19.0 5.3 %collective-permute-start.5 = (bf16[256,768]{1,0:T(8,128)(2,1)}, bf16[256,768]{1,0:T(8,128)(2,1)}, u32[]{:S(2)}, u32[]{:S(2)}) collective-permute-start(bf16[256,768]{1,0:T(8,128)(2,1)} %collective-permute-done.1.refs_4_), channel_id=1, source_target_pairs={{0,2},{1,3},{2,4},{3,5},{4,6},{5,7},{8,10},{9,11},{10,12},{11,13},... | collective-permute-start | bytes 1179656 | tf_op jit(solution)/shard_map/ppermute | solution.py:736
  32.9 4.9 %collective-permute-done.7.refs_10_ = bf16[256,768]{1,0:T(8,128)(2,1)} collective-permute-done((bf16[256,768]{1,0:T(8,128)(2,1)}, bf16[256,768]{1,0:T(8,128)(2,1)}, u32[]{:S(2)}, u32[]{:S(2)}) %collective-permute-start.7) | collective-permute-done | bytes 393248 | tf_op jit(solution)/shard_map/ppermute | solution.py:737
  41.4 9.5 %project_keys.1 = (bf16[2560,768]{1,0:T(8,128)(2,1)S(1)}, bf16[2560,1536]{1,0:T(8,128)(2,1)}) custom-call(s32[8]{0:T(128)S(1)} %pad_add_fusion.meta, f32[3,6,768]{2,1,0:T(8,128)S(1)} %bitcast.264, bf16[768,2304]{1,0:T(8,128)(2,1)S(1)} %copy-done.7, bf16[768,2304]{1,0:T(8,128)(2,1)S(1)} %copy-done.7, bf16[256,768]{1,0:T(8,128)(2,1)S(1)} %bitcast.260, ...), custom_call_target="tpu_custom_call" | custom-call | flops 3019898880 | bytes 15728640 | tf_op jit(solution)/shard_map/project_keys/pallas_call | solution.py:217
  54.2 21.6 %self_attend.1 = (f32[256,768]{1,0:T(8,128)S(1)}, bf16[256,768]{1,0:T(8,128)(2,1)}, bf16[256,128]{1,0:T(8,128)(2,1)S(1)}) custom-call(s32[8]{0:T(128)S(1)} %pad_add_fusion.meta, bf16[256,768]{1,0:T(8,128)(2,1)S(1)} %fusion.13.q_ref, bf16[2560,1536]{1,0:T(8,128)(2,1)S(1)} %copy-done.1, bf16[2560,1536]{1,0:T(8,128)(2,1)S(1)} %copy-done.1), custom_call_target="tpu_custom_call" | custom-call | flops 1006632960 | bytes 7864320 | tf_op jit(solution)/shard_map/self_attend/pallas_call | solution.py:327
  80.4 7.4 %cross_attend.1 = (f32[256,768]{1,0:T(8,128)S(1)}, bf16[256,768]{1,0:T(8,128)(2,1)S(1)}, bf16[256,128]{1,0:T(8,128)(2,1)S(1)}) custom-call(s32[8]{0:T(128)S(1)} %pad_add_fusion.meta, bf16[256,768]{1,0:T(8,128)(2,1)S(1)} %fusion.10.q_ref, bf16[768,1536]{1,0:T(8,128)(2,1)S(1)} %copy-done.2, bf16[768,1536]{1,0:T(8,128)(2,1)S(1)} %copy-done.2), custom_call_target="tpu_custom_call" | custom-call | flops 301989888 | bytes 2359296 | tf_op jit(solution)/shard_map/cross_attend/pallas_call | solution.py:327
  90.4 4.0 fusion.119
  94.4 7.2 %fusion.6 = (bf16[256,3072]{1,0:T(8,128)(2,1)}, bf16[256,3072]{1,0:T(8,128)(2,1)S(1)}) fusion(f32[256,3072]{1,0:T(8,128)S(1)} %fusion.119, bf16[256,768]{1,0:T(8,128)(2,1)} %get-tuple-element.140.refs_0_, bf16[768,3072]{1,0:T(8,128)(2,1)} %param.24), kind=kOutput, calls=%fused_computation.9 | convolution fusion | flops 1225261056 | bytes 11403264 | tf_op jit(solution)/shard_map/dot_general | solution.py:812
  109.5 16.4 %cross_grad.1 = (bf16[256,768]{1,0:T(8,128)(2,1)S(1)}, bf16[2,8,96,768]{3,2,1,0:T(8,128)(2,1)S(1)}) custom-call(s32[8]{0:T(128)S(1)} %pad_add_fusion.meta, bf16[256,768]{1,0:T(8,128)(2,1)S(1)} %fusion.10.q_ref, bf16[256,768]{1,0:T(8,128)(2,1)S(1)} %convolution_convert_fusion.2.do_ref, bf16[256,128]{1,0:T(8,128)(2,1)S(1)} %fusion.80.f_ref, ...), custom_call_target="tpu_custom_call" | custom-call | flops 704643072 | bytes 4718592 | tf_op jit(solution)/shard_map/cross_grad/pallas_call | solution.py:539
  138.3 7.3 %collective-permute-start.23 = (f32[12,768]{1,0:T(8,128)S(1)}, f32[12,768]{1,0:T(8,128)S(1)}, u32[]{:S(2)}, u32[]{:S(2)}) collective-permute-start(f32[12,768]{1,0:T(8,128)S(1)} %add.254), channel_id=1, source_target_pairs={{0,4},{1,5},{2,6},{3,7},{4,0},{5,1},{6,2},{7,3},{8,12},{9,13},{10,... | collective-permute-start | bytes 110600 | tf_op jit(solution)/shard_map/ppermute | solution.py:690
  148.7 4.2 collective-permute-start.10
  154.1 17.9 %self_query_grad.1 = bf16[256,768]{1,0:T(8,128)(2,1)S(1)} custom-call(s32[8]{0:T(128)S(1)} %pad_add_fusion.meta, bf16[256,768]{1,0:T(8,128)(2,1)S(1)} %fusion.13.q_ref, bf16[256,768]{1,0:T(8,128)(2,1)S(1)} %convolution_convert_fusion.1.do_ref, bf16[256,128]{1,0:T(8,128)(2,1)S(1)} %fusion.88.f_ref, bf16[2560,1536]{1,0:T(8,128)(2,1)S(1)} %bitcast.256, ...), custom_call_target="tpu_custom_call" | custom-call | flops 1509949440 | bytes 7864320 | tf_op jit(solution)/shard_map/self_query_grad/pallas_call | solution.py:417
  191.2 5.9 %pack_square.1 = (bf16[2,4,144,384]{3,2,1,0:T(8,128)(2,1)S(1)}, bf16[2,4,144,384]{3,2,1,0:T(8,128)(2,1)S(1)}) custom-call(s32[8]{0:T(128)S(1)} %pad_add_fusion.meta, bf16[256,768]{1,0:T(8,128)(2,1)S(1)} %copy-done.20, bf16[256,768]{1,0:T(8,128)(2,1)} %collective-permute-done.37.refs_1_, bf16[256,768]{1,0:T(8,128)(2,1)S(1)} %copy-done.12, ...), custom_call_target="tpu_custom_call" | custom-call | flops 905969664 | bytes 1769472 | tf_op jit(solution)/shard_map/pack_square/pallas_call | solution.py:673
  197.1 4.5 collective-permute-start.14
  204.0 21.0 %collective-permute-start.43 = (bf16[2,4,144,384]{3,2,1,0:T(8,128)(2,1)S(1)}, bf16[2,4,144,384]{3,2,1,0:T(8,128)(2,1)S(1)}, u32[]{:S(2)}, u32[]{:S(2)}) collective-permute-start(bf16[2,4,144,384]{3,2,1,0:T(8,128)(2,1)S(1)} %get-tuple-element.53), channel_id=1, source_target_pairs={{0,16},{8,24},{16,0},{24,8},{1,17},{9,25},{17,1},{25,9},{2,18},{10... | collective-permute-start | bytes 2654216 | tf_op jit(solution)/shard_map/ppermute | solution.py:690
  231.6 13.0 %collective-permute-done.16 = bf16[256,896]{1,0:T(8,128)(2,1)S(1)} collective-permute-done((bf16[256,896]{1,0:T(8,128)(2,1)}, bf16[256,896]{1,0:T(8,128)(2,1)S(1)}, u32[]{:S(2)}, u32[]{:S(2)}) %collective-permute-start.16) | collective-permute-done | bytes 458784 | tf_op jit(solution)/shard_map/ppermute | solution.py:737
  248.0 16.9 %self_key_grad.1 = (bf16[256,768]{1,0:T(8,128)(2,1)S(1)}, bf16[256,768]{1,0:T(8,128)(2,1)S(1)}) custom-call(s32[8]{0:T(128)S(1)} %pad_add_fusion.meta, bf16[2560,768]{1,0:T(8,128)(2,1)S(1)} %copy-done.5, bf16[2560,896]{1,0:T(8,128)(2,1)S(1)} %constant_dynamic-update-slice_fusion.do_ref.f_ref, ...), custom_call_target="tpu_custom_call" | custom-call | flops 2013265920 | bytes 7864320 | tf_op jit(solution)/shard_map/self_key_grad/pallas_call | solution.py:470
  269.0 4.8 %collective-permute-start.19 = (f32[6,768]{1,0:T(8,128)S(1)}, f32[6,768]{1,0:T(8,128)S(1)}, u32[]{:S(2)}, u32[]{:S(2)}) collective-permute-start(f32[6,768]{1,0:T(8,128)S(1)} %fusion.104), channel_id=1, source_target_pairs={{0,2},{1,3},{2,0},{3,1},{4,6},{5,7},{6,4},{7,5},{8,10},{9,11},{10,... | collective-permute-start | bytes 55304 | tf_op jit(solution)/shard_map/ppermute | solution.py:690
  280.3 8.9 %collective-permute-start.44 = (bf16[4,144,384]{2,1,0:T(8,128)(2,1)}, bf16[4,144,384]{2,1,0:T(8,128)(2,1)}, u32[]{:S(2)}, u32[]{:S(2)}) collective-permute-start(bf16[4,144,384]{2,1,0:T(8,128)(2,1)} %slice_bitcast_fusion.6), channel_id=1, source_target_pairs={{0,8},{8,0},{16,24},{24,16},{1,9},{9,1},{17,25},{25,17},{2,10},{10... | collective-permute-start | bytes 1327112 | tf_op jit(solution)/shard_map/ppermute | solution.py:690
  293.4 6.6 %pack_down.1 = (bf16[2,4,192,384]{3,2,1,0:T(8,128)(2,1)S(1)}, bf16[2,4,192,384]{3,2,1,0:T(8,128)(2,1)S(1)}) custom-call(s32[8]{0:T(128)S(1)} %pad_add_fusion.meta, bf16[256,3072]{1,0:T(8,128)(2,1)S(1)} %copy-done.36, bf16[256,3072]{1,0:T(8,128)(2,1)} %collective-permute-done.58.refs_1_, bf16[256,768]{1,0:T(8,128)(2,1)} %get-tuple-element.139.refs_2_, ...), custom_call_target="tpu_custom_call" | custom-call | flops 1207959552 | bytes 2359296 | tf_op jit(solution)/shard_map/pack_down/pallas_call | solution.py:673
  300.3 13.2 %collective-permute-start.60 = (bf16[2,4,192,384]{3,2,1,0:T(8,128)(2,1)S(1)}, bf16[2,4,192,384]{3,2,1,0:T(8,128)(2,1)S(1)}, u32[]{:S(2)}, u32[]{:S(2)}) collective-permute-start(bf16[2,4,192,384]{3,2,1,0:T(8,128)(2,1)S(1)} %get-tuple-element.59), channel_id=1, source_target_pairs={{0,16},{8,24},{16,0},{24,8},{1,17},{9,25},{17,1},{25,9},{2,18},{10... | collective-permute-start | bytes 3538952 | tf_op jit(solution)/shard_map/ppermute | solution.py:690
  313.5 5.9 %pack_up.1 = (bf16[2,4,192,384]{3,2,1,0:T(8,128)(2,1)S(1)}, bf16[2,4,192,384]{3,2,1,0:T(8,128)(2,1)S(1)}) custom-call(s32[8]{0:T(128)S(1)} %pad_add_fusion.meta, bf16[256,768]{1,0:T(8,128)(2,1)} %get-tuple-element.140.refs_0_, bf16[256,768]{1,0:T(8,128)(2,1)} %collective-permute-done.52.refs_1_, bf16[256,3072]{1,0:T(8,128)(2,1)} %get-tuple-element.114.refs_2_, ...), custom_call_target="tpu_custom_call" | custom-call | flops 1207959552 | bytes 2359296 | tf_op jit(solution)/shard_map/pack_up/pallas_call | solution.py:673
  322.6 5.5 %collective-permute-done.45 = bf16[2,144,384]{2,1,0:T(8,128)(2,1)S(1)} collective-permute-done((bf16[2,144,384]{2,1,0:T(8,128)(2,1)S(1)}, bf16[2,144,384]{2,1,0:T(8,128)(2,1)S(1)}, u32[]{:S(2)}, u32[]{:S(2)}) %collective-permute-start.45) | collective-permute-done | bytes 221216 | tf_op jit(solution)/shard_map/ppermute | solution.py:690
  331.2 4.9 %collective-permute-done.46 = bf16[144,384]{1,0:T(8,128)(2,1)S(1)} collective-permute-done((bf16[144,384]{1,0:T(8,128)(2,1)S(1)}, bf16[144,384]{1,0:T(8,128)(2,1)S(1)}, u32[]{:S(2)}, u32[]{:S(2)}) %collective-permute-start.46) | collective-permute-done | bytes 110624 | tf_op jit(solution)/shard_map/ppermute | solution.py:690
  339.0 7.1 %collective-permute-done.26 = bf16[2,1,96,768]{3,2,1,0:T(8,128)(2,1)S(1)} collective-permute-done((bf16[2,1,96,768]{3,2,1,0:T(8,128)(2,1)S(1)}, bf16[2,1,96,768]{3,2,1,0:T(8,128)(2,1)S(1)}, u32[]{:S(2)}, u32[]{:S(2)}) %collective-permute-start.26) | collective-permute-done | bytes 294944 | tf_op jit(solution)/shard_map/ppermute | solution.py:690
  348.1 4.8 %pack_text.1 = (bf16[2,4,128,384]{3,2,1,0:T(8,128)(2,1)S(1)}, bf16[2,4,128,384]{3,2,1,0:T(8,128)(2,1)S(1)}) custom-call(s32[8]{0:T(128)S(1)} %pad_add_fusion.meta, bf16[96,1024]{1,0:T(8,128)(2,1)S(1)} %bitcast.266, bf16[96,1024]{1,0:T(8,128)(2,1)S(1)} %bitcast.265, bf16[96,1536]{1,0:T(8,128)(2,1)S(1)} %pad_maximum_fusion.2.refs_2_, ...), custom_call_target="tpu_custom_call" | custom-call | flops 805306368 | bytes 1572864 | tf_op jit(solution)/shard_map/pack_text/pallas_call | solution.py:673
  360.2 7.5 %collective-permute-done.33 = bf16[2,4,48,384]{3,2,1,0:T(8,128)(2,1)S(1)} collective-permute-done((bf16[2,4,48,384]{3,2,1,0:T(8,128)(2,1)S(1)}, bf16[2,4,48,384]{3,2,1,0:T(8,128)(2,1)S(1)}, u32[]{:S(2)}, u32[]{:S(2)}) %collective-permute-start.33) | collective-permute-done | bytes 294944 | tf_op jit(solution)/shard_map/ppermute | solution.py:690
  370.0 19.2 %collective-permute-done.34 = bf16[4,48,384]{2,1,0:T(8,128)(2,1)S(1)} collective-permute-done((bf16[4,48,384]{2,1,0:T(8,128)(2,1)S(1)}, bf16[4,48,384]{2,1,0:T(8,128)(2,1)S(1)}, u32[]{:S(2)}, u32[]{:S(2)}) %collective-permute-start.34) | collective-permute-done | bytes 147488 | tf_op jit(solution)/shard_map/ppermute | solution.py:690
  389.2 5.1 %collective-permute-start.35 = (bf16[2,48,384]{2,1,0:T(8,128)(2,1)S(1)}, bf16[2,48,384]{2,1,0:T(8,128)(2,1)S(1)}, u32[]{:S(2)}, u32[]{:S(2)}) collective-permute-start(bf16[2,48,384]{2,1,0:T(8,128)(2,1)S(1)} %slice_bitcast_fusion.34), channel_id=1, source_target_pairs={{0,2},{1,3},{2,0},{3,1},{4,6},{5,7},{6,4},{7,5},{8,10},{9,11},{10,... | collective-permute-start | bytes 221192 | tf_op jit(solution)/shard_map/ppermute | solution.py:690
  411.2 5.9 %collective-permute-done.55 = bf16[4,192,384]{2,1,0:T(8,128)(2,1)} collective-permute-done((bf16[4,192,384]{2,1,0:T(8,128)(2,1)}, bf16[4,192,384]{2,1,0:T(8,128)(2,1)}, u32[]{:S(2)}, u32[]{:S(2)}) %collective-permute-start.55) | collective-permute-done | bytes 589856 | tf_op jit(solution)/shard_map/ppermute | solution.py:690
  437.1 10.5 %collective-permute-done.32 = bf16[96,384]{1,0:T(8,128)(2,1)S(1)} collective-permute-done((bf16[96,384]{1,0:T(8,128)(2,1)S(1)}, bf16[96,384]{1,0:T(8,128)(2,1)S(1)}, u32[]{:S(2)}, u32[]{:S(2)}) %collective-permute-start.32) | collective-permute-done | bytes 73760 | tf_op jit(solution)/shard_map/ppermute | solution.py:690
  (415 shorter events, 166.1 us)
Async XLA Ops:
  0.7 18.4 %collective-permute-start.1 = (bf16[256,768]{1,0:T(8,128)(2,1)}, bf16[256,768]{1,0:T(8,128)(2,1)}, u32[]{:S(2)}, u32[]{:S(2)}) collective-permute-start(bf16[256,768]{1,0:T(8,128)(2,1)} %bitcast.257), channel_id=1, source_target_pairs={{0,2},{1,3},{2,4},{3,5},{4,6},{5,7},{8,10},{9,11},{10,12},{11,13},... | collective-permute-start | bytes 1179656 | tf_op jit(solution)/shard_map/ppermute | solution.py:736
  7.9 33.5 %collective-permute-start = (bf16[256,768]{1,0:T(8,128)(2,1)}, bf16[256,768]{1,0:T(8,128)(2,1)}, u32[]{:S(2)}, u32[]{:S(2)}) collective-permute-start(bf16[256,768]{1,0:T(8,128)(2,1)} %bitcast.259), channel_id=1, source_target_pairs={{0,1},{1,0},{2,3},{3,2},{4,5},{5,4},{6,7},{7,6},{8,9},{9,8},{10,11... | collective-permute-start | bytes 1179656 | tf_op jit(solution)/shard_map/ppermute | solution.py:733
  128.8 43.2 %collective-permute-start.40 = (bf16[256,768]{1,0:T(8,128)(2,1)S(1)}, bf16[256,768]{1,0:T(8,128)(2,1)S(1)}, u32[]{:S(2)}, u32[]{:S(2)}) collective-permute-start(bf16[256,768]{1,0:T(8,128)(2,1)S(1)} %get-tuple-element.41.refs_6_), channel_id=1, source_target_pairs={{0,1},{1,0},{2,3},{3,2},{4,5},{5,4},{6,7},{7,6},{8,9},{9,8},{10,11... | collective-permute-start | bytes 1179656 | tf_op jit(solution)/shard_map/ppermute | solution.py:785
  129.4 43.0 %collective-permute-start.38 = (bf16[256,768]{1,0:T(8,128)(2,1)S(1)}, bf16[256,768]{1,0:T(8,128)(2,1)}, u32[]{:S(2)}, u32[]{:S(2)}) collective-permute-start(bf16[256,768]{1,0:T(8,128)(2,1)S(1)} %get-tuple-element.110.refs_2_), channel_id=1, source_target_pairs={{0,1},{1,0},{2,3},{3,2},{4,5},{5,4},{6,7},{7,6},{8,9},{9,8},{10,11... | collective-permute-start | bytes 1179656 | tf_op jit(solution)/shard_map/ppermute | solution.py:785
  129.5 43.2 %collective-permute-start.37 = (bf16[256,768]{1,0:T(8,128)(2,1)S(1)}, bf16[256,768]{1,0:T(8,128)(2,1)}, u32[]{:S(2)}, u32[]{:S(2)}) collective-permute-start(bf16[256,768]{1,0:T(8,128)(2,1)S(1)} %get-tuple-element.38.refs_0_), channel_id=1, source_target_pairs={{0,1},{1,0},{2,3},{3,2},{4,5},{5,4},{6,7},{7,6},{8,9},{9,8},{10,11... | collective-permute-start | bytes 1179656 | tf_op jit(solution)/shard_map/ppermute | solution.py:785
  147.9 26.0 %collective-permute-start.39 = (bf16[256,768]{1,0:T(8,128)(2,1)S(1)}, bf16[256,768]{1,0:T(8,128)(2,1)}, u32[]{:S(2)}, u32[]{:S(2)}) collective-permute-start(bf16[256,768]{1,0:T(8,128)(2,1)S(1)} %fusion.51.refs_4_), channel_id=1, source_target_pairs={{0,1},{1,0},{2,3},{3,2},{4,5},{5,4},{6,7},{7,6},{8,9},{9,8},{10,11... | collective-permute-start | bytes 1179656 | tf_op jit(solution)/shard_map/ppermute | solution.py:785
  148.7 33.4 %collective-permute-start.10 = (bf16[256,896]{1,0:T(8,128)(2,1)}, bf16[256,896]{1,0:T(8,128)(2,1)}, u32[]{:S(2)}, u32[]{:S(2)}) collective-permute-start(bf16[256,896]{1,0:T(8,128)(2,1)} %get-tuple-element.123), channel_id=1, source_target_pairs={{0,2},{1,3},{2,4},{3,5},{4,6},{5,7},{8,10},{9,11},{10,12},{11,13},... | collective-permute-start | bytes 1376264 | tf_op jit(solution)/shard_map/ppermute | solution.py:736
  172.3 24.7 %collective-permute-start.9 = (bf16[256,896]{1,0:T(8,128)(2,1)}, bf16[256,896]{1,0:T(8,128)(2,1)}, u32[]{:S(2)}, u32[]{:S(2)}) collective-permute-start(bf16[256,896]{1,0:T(8,128)(2,1)} %get-tuple-element.123), channel_id=1, source_target_pairs={{0,1},{1,0},{2,3},{3,2},{4,5},{5,4},{6,7},{7,6},{8,9},{9,8},{10,11... | collective-permute-start | bytes 1376264 | tf_op jit(solution)/shard_map/ppermute | solution.py:733
  172.6 29.0 %collective-permute-start.12 = (bf16[256,896]{1,0:T(8,128)(2,1)}, bf16[256,896]{1,0:T(8,128)(2,1)}, u32[]{:S(2)}, u32[]{:S(2)}) collective-permute-start(bf16[256,896]{1,0:T(8,128)(2,1)} %get-tuple-element.123), channel_id=1, source_target_pairs={{2,0},{3,1},{4,2},{5,3},{6,4},{7,5},{10,8},{11,9},{12,10},{13,11},... | collective-permute-start | bytes 1376264 | tf_op jit(solution)/shard_map/ppermute | solution.py:737
  173.9 53.0 %collective-permute-start.24 = (bf16[2,4,96,768]{3,2,1,0:T(8,128)(2,1)}, bf16[2,4,96,768]{3,2,1,0:T(8,128)(2,1)}, u32[]{:S(2)}, u32[]{:S(2)}) collective-permute-start(bf16[2,4,96,768]{3,2,1,0:T(8,128)(2,1)} %slice_bitcast_fusion), channel_id=1, source_target_pairs={{0,1},{1,0},{2,3},{3,2},{4,5},{5,4},{6,7},{7,6},{8,9},{9,8},{10,11... | collective-permute-start | bytes 3538952 | tf_op jit(solution)/shard_map/ppermute | solution.py:690
  182.1 21.9 %collective-permute-start.11 = (bf16[256,896]{1,0:T(8,128)(2,1)}, bf16[256,896]{1,0:T(8,128)(2,1)S(1)}, u32[]{:S(2)}, u32[]{:S(2)}) collective-permute-start(bf16[256,896]{1,0:T(8,128)(2,1)} %collective-permute-done.10), channel_id=1, source_target_pairs={{0,1},{1,0},{2,3},{3,2},{4,5},{5,4},{6,7},{7,6},{8,9},{9,8},{10,11... | collective-permute-start | bytes 1376264 | tf_op jit(solution)/shard_map/ppermute | solution.py:738
  183.7 106.2 %collective-permute-start.58 = (bf16[256,3072]{1,0:T(8,128)(2,1)}, bf16[256,3072]{1,0:T(8,128)(2,1)}, u32[]{:S(2)}, u32[]{:S(2)}) collective-permute-start(bf16[256,3072]{1,0:T(8,128)(2,1)} %copy-done.35), channel_id=1, source_target_pairs={{0,1},{1,0},{2,3},{3,2},{4,5},{5,4},{6,7},{7,6},{8,9},{9,8},{10,11... | collective-permute-start | bytes 4718600 | tf_op jit(solution)/shard_map/ppermute | solution.py:785
  197.1 29.4 %collective-permute-start.14 = (bf16[256,896]{1,0:T(8,128)(2,1)}, bf16[256,896]{1,0:T(8,128)(2,1)S(1)}, u32[]{:S(2)}, u32[]{:S(2)}) collective-permute-start(bf16[256,896]{1,0:T(8,128)(2,1)} %collective-permute-done.10), channel_id=1, source_target_pairs={{0,2},{1,3},{2,4},{3,5},{4,6},{5,7},{8,10},{9,11},{10,12},{11,13},... | collective-permute-start | bytes 1376264 | tf_op jit(solution)/shard_map/ppermute | solution.py:736
  201.6 24.5 %collective-permute-start.13 = (bf16[256,896]{1,0:T(8,128)(2,1)}, bf16[256,896]{1,0:T(8,128)(2,1)S(1)}, u32[]{:S(2)}, u32[]{:S(2)}) collective-permute-start(bf16[256,896]{1,0:T(8,128)(2,1)} %collective-permute-done.12), channel_id=1, source_target_pairs={{0,1},{1,0},{2,3},{3,2},{4,5},{5,4},{6,7},{7,6},{8,9},{9,8},{10,11... | collective-permute-start | bytes 1376264 | tf_op jit(solution)/shard_map/ppermute | solution.py:739
  204.0 41.3 %collective-permute-start.43 = (bf16[2,4,144,384]{3,2,1,0:T(8,128)(2,1)S(1)}, bf16[2,4,144,384]{3,2,1,0:T(8,128)(2,1)S(1)}, u32[]{:S(2)}, u32[]{:S(2)}) collective-permute-start(bf16[2,4,144,384]{3,2,1,0:T(8,128)(2,1)S(1)} %get-tuple-element.53), channel_id=1, source_target_pairs={{0,16},{8,24},{16,0},{24,8},{1,17},{9,25},{17,1},{25,9},{2,18},{10... | collective-permute-start | bytes 2654216 | tf_op jit(solution)/shard_map/ppermute | solution.py:690
  226.2 63.7 %collective-permute-start.59 = (bf16[256,768]{1,0:T(8,128)(2,1)}, bf16[256,768]{1,0:T(8,128)(2,1)}, u32[]{:S(2)}, u32[]{:S(2)}) collective-permute-start(bf16[256,768]{1,0:T(8,128)(2,1)} %get-tuple-element.139.refs_2_), channel_id=1, source_target_pairs={{0,1},{1,0},{2,3},{3,2},{4,5},{5,4},{6,7},{7,6},{8,9},{9,8},{10,11... | collective-permute-start | bytes 1179656 | tf_op jit(solution)/shard_map/ppermute | solution.py:785
  226.5 73.8 %collective-permute-start.53 = (bf16[256,3072]{1,0:T(8,128)(2,1)}, bf16[256,3072]{1,0:T(8,128)(2,1)}, u32[]{:S(2)}, u32[]{:S(2)}) collective-permute-start(bf16[256,3072]{1,0:T(8,128)(2,1)} %get-tuple-element.114.refs_2_), channel_id=1, source_target_pairs={{0,1},{1,0},{2,3},{3,2},{4,5},{5,4},{6,7},{7,6},{8,9},{9,8},{10,11... | collective-permute-start | bytes 4718600 | tf_op jit(solution)/shard_map/ppermute | solution.py:785
  246.4 53.6 %collective-permute-start.52 = (bf16[256,768]{1,0:T(8,128)(2,1)}, bf16[256,768]{1,0:T(8,128)(2,1)}, u32[]{:S(2)}, u32[]{:S(2)}) collective-permute-start(bf16[256,768]{1,0:T(8,128)(2,1)} %get-tuple-element.140.refs_0_), channel_id=1, source_target_pairs={{0,1},{1,0},{2,3},{3,2},{4,5},{5,4},{6,7},{7,6},{8,9},{9,8},{10,11... | collective-permute-start | bytes 1179656 | tf_op jit(solution)/shard_map/ppermute | solution.py:785
  280.3 39.0 %collective-permute-start.44 = (bf16[4,144,384]{2,1,0:T(8,128)(2,1)}, bf16[4,144,384]{2,1,0:T(8,128)(2,1)}, u32[]{:S(2)}, u32[]{:S(2)}) collective-permute-start(bf16[4,144,384]{2,1,0:T(8,128)(2,1)} %slice_bitcast_fusion.6), channel_id=1, source_target_pairs={{0,8},{8,0},{16,24},{24,16},{1,9},{9,1},{17,25},{25,17},{2,10},{10... | collective-permute-start | bytes 1327112 | tf_op jit(solution)/shard_map/ppermute | solution.py:690
  289.9 64.2 %collective-permute-start.27 = (bf16[256,768]{1,0:T(8,128)(2,1)}, bf16[256,768]{1,0:T(8,128)(2,1)S(1)}, u32[]{:S(2)}, u32[]{:S(2)}) collective-permute-start(bf16[256,768]{1,0:T(8,128)(2,1)} %copy-done.30), channel_id=1, source_target_pairs={{0,1},{1,0},{2,3},{3,2},{4,5},{5,4},{6,7},{7,6},{8,9},{9,8},{10,11... | collective-permute-start | bytes 1179656 | tf_op jit(solution)/shard_map/ppermute | solution.py:785
  289.9 30.7 %collective-permute-start.25 = (bf16[2,2,96,768]{3,2,0,1:T(8,128)(2,1)}, bf16[2,2,96,768]{3,2,0,1:T(8,128)(2,1)S(1)}, u32[]{:S(2)}, u32[]{:S(2)}) collective-permute-start(bf16[2,2,96,768]{3,2,0,1:T(8,128)(2,1)} %bitcast.281), channel_id=1, source_target_pairs={{0,2},{1,3},{2,0},{3,1},{4,6},{5,7},{6,4},{7,5},{8,10},{9,11},{10,... | collective-permute-start | bytes 1769480 | tf_op jit(solution)/shard_map/ppermute | solution.py:690
  300.1 54.0 %collective-permute-start.28 = (bf16[256,2304]{1,0:T(8,128)(2,1)S(1)}, bf16[256,2304]{1,0:T(8,128)(2,1)S(1)}, u32[]{:S(2)}, u32[]{:S(2)}) collective-permute-start(bf16[256,2304]{1,0:T(8,128)(2,1)S(1)} %copy-done.23), channel_id=1, source_target_pairs={{0,1},{1,0},{2,3},{3,2},{4,5},{5,4},{6,7},{7,6},{8,9},{9,8},{10,11... | collective-permute-start | bytes 3538952 | tf_op jit(solution)/shard_map/ppermute | solution.py:785
  300.3 59.6 %collective-permute-start.60 = (bf16[2,4,192,384]{3,2,1,0:T(8,128)(2,1)S(1)}, bf16[2,4,192,384]{3,2,1,0:T(8,128)(2,1)S(1)}, u32[]{:S(2)}, u32[]{:S(2)}) collective-permute-start(bf16[2,4,192,384]{3,2,1,0:T(8,128)(2,1)S(1)} %get-tuple-element.59), channel_id=1, source_target_pairs={{0,16},{8,24},{16,0},{24,8},{1,17},{9,25},{17,1},{25,9},{2,18},{10... | collective-permute-start | bytes 3538952 | tf_op jit(solution)/shard_map/ppermute | solution.py:690
  319.4 74.9 %collective-permute-start.54 = (bf16[2,4,192,384]{3,2,1,0:T(8,128)(2,1)S(1)}, bf16[2,4,192,384]{3,2,1,0:T(8,128)(2,1)S(1)}, u32[]{:S(2)}, u32[]{:S(2)}) collective-permute-start(bf16[2,4,192,384]{3,2,1,0:T(8,128)(2,1)S(1)} %get-tuple-element.57), channel_id=1, source_target_pairs={{0,8},{8,0},{16,24},{24,16},{1,9},{9,1},{17,25},{25,17},{2,10},{10... | collective-permute-start | bytes 3538952 | tf_op jit(solution)/shard_map/ppermute | solution.py:690
  352.9 51.3 %collective-permute-start.48 = (bf16[2,4,128,384]{3,2,1,0:T(8,128)(2,1)S(1)}, bf16[2,4,128,384]{3,2,1,0:T(8,128)(2,1)S(1)}, u32[]{:S(2)}, u32[]{:S(2)}) collective-permute-start(bf16[2,4,128,384]{3,2,1,0:T(8,128)(2,1)S(1)} %get-tuple-element.55), channel_id=1, source_target_pairs={{0,8},{8,0},{16,24},{24,16},{1,9},{9,1},{17,25},{25,17},{2,10},{10... | collective-permute-start | bytes 2359304 | tf_op jit(solution)/shard_map/ppermute | solution.py:690
  357.8 44.5 %collective-permute-start.29 = (bf16[2,4,96,384]{3,2,1,0:T(8,128)(2,1)S(1)}, bf16[2,4,96,384]{3,2,1,0:T(8,128)(2,1)S(1)}, u32[]{:S(2)}, u32[]{:S(2)}) collective-permute-start(bf16[2,4,96,384]{3,2,1,0:T(8,128)(2,1)S(1)} %get-tuple-element.49), channel_id=1, source_target_pairs={{0,8},{8,0},{16,24},{24,16},{1,9},{9,1},{17,25},{25,17},{2,10},{10... | collective-permute-start | bytes 1769480 | tf_op jit(solution)/shard_map/ppermute | solution.py:690
  367.7 21.4 %collective-permute-start.34 = (bf16[4,48,384]{2,1,0:T(8,128)(2,1)S(1)}, bf16[4,48,384]{2,1,0:T(8,128)(2,1)S(1)}, u32[]{:S(2)}, u32[]{:S(2)}) collective-permute-start(bf16[4,48,384]{2,1,0:T(8,128)(2,1)S(1)} %slice_bitcast_fusion.24), channel_id=1, source_target_pairs={{0,8},{8,0},{16,24},{24,16},{1,9},{9,1},{17,25},{25,17},{2,10},{10... | collective-permute-start | bytes 442376 | tf_op jit(solution)/shard_map/ppermute | solution.py:690
  369.0 37.4 %collective-permute-start.61 = (bf16[4,192,384]{2,1,0:T(8,128)(2,1)S(1)}, bf16[4,192,384]{2,1,0:T(8,128)(2,1)S(1)}, u32[]{:S(2)}, u32[]{:S(2)}) collective-permute-start(bf16[4,192,384]{2,1,0:T(8,128)(2,1)S(1)} %slice_bitcast_fusion.2), channel_id=1, source_target_pairs={{0,8},{8,0},{16,24},{24,16},{1,9},{9,1},{17,25},{25,17},{2,10},{10... | collective-permute-start | bytes 1769480 | tf_op jit(solution)/shard_map/ppermute | solution.py:690
  403.2 20.2 %collective-permute-start.30 = (bf16[4,96,384]{2,1,0:T(8,128)(2,1)}, bf16[4,96,384]{2,1,0:T(8,128)(2,1)}, u32[]{:S(2)}, u32[]{:S(2)}) collective-permute-start(bf16[4,96,384]{2,1,0:T(8,128)(2,1)} %slice_bitcast_fusion.12), channel_id=1, source_target_pairs={{0,16},{8,24},{16,0},{24,8},{1,17},{9,25},{17,1},{25,9},{2,18},{10... | collective-permute-start | bytes 884744 | tf_op jit(solution)/shard_map/ppermute | solution.py:690
  405.3 24.0 %collective-permute-start.49 = (bf16[4,128,384]{2,1,0:T(8,128)(2,1)}, bf16[4,128,384]{2,1,0:T(8,128)(2,1)}, u32[]{:S(2)}, u32[]{:S(2)}) collective-permute-start(bf16[4,128,384]{2,1,0:T(8,128)(2,1)} %slice_bitcast_fusion.8), channel_id=1, source_target_pairs={{0,16},{8,24},{16,0},{24,8},{1,17},{9,25},{17,1},{25,9},{2,18},{10... | collective-permute-start | bytes 1179656 | tf_op jit(solution)/shard_map/ppermute | solution.py:690
  409.2 23.6 %collective-permute-start.62 = (bf16[2,192,384]{1,2,0:T(8,128)(2,1)}, bf16[2,192,384]{1,2,0:T(8,128)(2,1)}, u32[]{:S(2)}, u32[]{:S(2)}) collective-permute-start(bf16[2,192,384]{1,2,0:T(8,128)(2,1)} %bitcast.283), channel_id=1, source_target_pairs={{0,2},{1,3},{2,0},{3,1},{4,6},{5,7},{6,4},{7,5},{8,10},{9,11},{10,... | collective-permute-start | bytes 884744 | tf_op jit(solution)/shard_map/ppermute | solution.py:690
  430.5 17.9 %collective-permute-start.50 = (bf16[2,128,384]{2,1,0:T(8,128)(2,1)S(1)}, bf16[2,128,384]{2,1,0:T(8,128)(2,1)S(1)}, u32[]{:S(2)}, u32[]{:S(2)}) collective-permute-start(bf16[2,128,384]{2,1,0:T(8,128)(2,1)S(1)} %slice_bitcast_fusion.20), channel_id=1, source_target_pairs={{0,2},{1,3},{2,0},{3,1},{4,6},{5,7},{6,4},{7,5},{8,10},{9,11},{10,... | collective-permute-start | bytes 589832 | tf_op jit(solution)/shard_map/ppermute | solution.py:690
  (112 other events, 1169.3 us)

commit v2 on v1

v2 whole, which is shorter than its diff:
```python
from functools import partial

import jax
import jax.numpy as jnp
from jax import lax
from jax.experimental import pallas as pl
from jax.experimental.pallas import tpu as pltpu
from jax.sharding import PartitionSpec as P

H = 12
LONGEST = 1024

epsilon = 1e-06
far = -1e30
LSE_LANE = 8
DELTA_LANE = 44
MIB = 1 << 20


def layer_norm(values):
    centred = values - jnp.mean(values, axis=-1, keepdims=True)
    inverse = lax.rsqrt(jnp.mean(centred * centred, axis=-1, keepdims=True) + epsilon)
    return (centred * inverse, inverse)


def norm_back(grad_normed, normed, inverse):
    return inverse * (
        grad_normed
        - jnp.mean(grad_normed, axis=-1, keepdims=True)
        - normed * jnp.mean(grad_normed * normed, axis=-1, keepdims=True)
    )


def contract_rows(left, right):
    return lax.dot_general(
        left, right, (((0,), (0,)), ((), ())), preferred_element_type=jnp.float32
    )


def times_transposed(left, right):
    return lax.dot_general(
        left, right, (((1,), (1,)), ((), ())), preferred_element_type=jnp.float32
    )


class Frame:
    def __init__(self, meta, items, count, shards):
        self.position = meta[0]
        self.items = items
        self.count = count
        self.shards = shards
        self.ends = []
        total = jnp.int32(0)
        for item in range(items):
            total = total + meta[1 + item]
            self.ends.append(total)
        self.text_len = [meta[1 + items + item] for item in range(items)]
        self.first = self.item_of(self.position * count)
        self.last = self.item_of(self.position * count + count - 1)
        self.low = jnp.int32(0)
        self.high = jnp.int32(0)
        for item in range(items):
            start = self.ends[item] - meta[1 + item]
            self.low = jnp.where(self.first == item, start, self.low)
            self.high = jnp.where(self.last == item, self.ends[item], self.high)

    def item_of(self, place):
        found = jnp.int32(0)
        for end in self.ends:
            found = found + (place >= end).astype(jnp.int32)
        return found

    def items_of_rows(self, base, rows):
        place = base + lax.broadcasted_iota(jnp.int32, (rows, 1), 0)
        found = jnp.zeros((rows, 1), jnp.int32)
        for end in self.ends:
            found = found + (place >= end).astype(jnp.int32)
        return found

    def items_of_chip(self, block):
        start, _ = self.chip(block)
        core = self.position % 2
        return jnp.concatenate(
            [
                self.items_of_rows(start + core * self.count, self.count),
                self.items_of_rows(start + (1 - core) * self.count, self.count),
            ],
            axis=0,
        )

    def chip(self, block):
        hop = (block + 1) // 2
        chip = self.position // 2 + jnp.where(block % 2 == 1, -hop, hop)
        rows = 2 * self.count
        start = chip * rows
        live = (chip >= 0) & (chip < self.shards // 2)
        return start, live & (start < self.high) & (start + rows > self.low)


def lanes(rows):
    return lax.broadcasted_iota(jnp.int32, (rows, 128), 1)


def lse_lanes(lane):
    return (lane >= LSE_LANE) & (lane < DELTA_LANE)


def delta_lanes(lane):
    return (lane >= DELTA_LANE) & (lane < DELTA_LANE + 3 * H)


def head_lanes(lane, base, head):
    start = base + 3 * head
    return (lane >= start) & (lane < start + 3)


def beside(left, right):
    return jnp.concatenate([left.astype(jnp.bfloat16), right.astype(jnp.bfloat16)], axis=1)


def pieces(values):
    high = values.astype(jnp.bfloat16).astype(jnp.float32)
    rest = values - high
    middle = rest.astype(jnp.bfloat16).astype(jnp.float32)
    return high, middle, rest - middle


def dot(left, right):
    return jnp.dot(left, right, preferred_element_type=jnp.float32)


def stack_heads(target, values, features):
    rows = values.shape[0]
    half = lanes(rows) // 64
    wide = values.astype(jnp.float32)
    for h in range(2):
        target[h * rows : (h + 1) * rows, :] = beside(jnp.where(half == h, wide, 0.0), features[h])


def merge_heads(stacked):
    rows = stacked.shape[0] // 2
    return jnp.where(lanes(rows) < 64, stacked[:rows], stacked[rows:])


def item_bias(frame, item):
    lane = lanes(item.shape[0])
    return jnp.where((lane != item) & (lane < frame.items), far, 0.0)


def text_bias(frame, block, rows):
    slot = lax.broadcasted_iota(jnp.int32, (rows, 1), 0)
    length = jnp.int32(0)
    for item in range(frame.items):
        length = jnp.where(block == item, frame.text_len[item], length)
    lane = lanes(rows)
    dead = (lane != block) | (slot >= length)
    return jnp.where(dead & (lane < frame.items), far, 0.0)


def block_rule(frame, kind, rows):
    if kind == "frames":
        return (
            lambda block: frame.chip(block)[1],
            lambda block: item_bias(frame, frame.items_of_chip(block)),
        )
    return (
        lambda block: (block >= frame.first) & (block <= frame.last),
        lambda block: text_bias(frame, block, rows),
    )


def rows_of(block, rows):
    return pl.ds(pl.multiple_of(block * rows, rows), rows)


def each_active(blocks, active, step):
    @pl.loop(0, blocks)
    def _(block):
        @pl.when(active(block))
        def _():
            step(block)


def fill_bias(blocks, rows, active, bias, target, with_lse):
    @pl.when(pl.program_id(0) == 0)
    def _():
        def step(block):
            mask = bias(block)
            if with_lse:
                mask = jnp.where(lse_lanes(lanes(rows)), -1.0, mask)
            target[rows_of(block, rows), :] = mask.astype(jnp.bfloat16)

        each_active(blocks, active, step)


def project_kernel(items, shards, chips, meta, mod_ref, w_ref, *refs):
    number = len(chips)
    x_refs = refs[: 2 * number]
    q_ref, kv_ref, own_ref, x_s, h_s, q_s, kv_s, in_sem, out_sem = refs[-9:]
    count, width = x_refs[0].shape
    rows = 2 * count
    frame = Frame(meta, items, count, shards)

    def live(index):
        return frame.chip(index + chips[0])[1]

    for index in range(number):

        @pl.when(live(jnp.int32(index)))
        def _(index=index):
            for part in range(2):
                block = 2 * index + part
                pltpu.make_async_copy(
                    x_refs[block], x_s.at[pl.ds(block * count, count), :], in_sem.at[block]
                ).start()

    def writes(index):
        here = rows_of(index, rows)
        there = rows_of(index + chips[0], rows)
        return (
            pltpu.make_async_copy(q_s.at[here, :], q_ref.at[there, :], out_sem.at[2 * index]),
            pltpu.make_async_copy(kv_s.at[here, :], kv_ref.at[there, :], out_sem.at[2 * index + 1]),
        )

    @pl.loop(0, number)
    def _(index):
        @pl.when(live(index))
        def _():
            start = frame.chip(index + chips[0])[0]
            for part in range(2):
                block = 2 * index + part
                here = rows_of(block, count)
                pltpu.make_async_copy(x_refs[0], x_s.at[here, :], in_sem.at[block]).wait()
                normed, _ = layer_norm(x_s[here, :].astype(jnp.float32))
                item = frame.items_of_rows(start + (frame.position + part) % 2 * count, count)
                shift = jnp.broadcast_to(mod_ref[0, 0:1, :], normed.shape)
                scale = jnp.broadcast_to(mod_ref[0, 1:2, :], normed.shape)
                for i in range(1, items):
                    shift = jnp.where(item == i, mod_ref[i, 0:1, :], shift)
                    scale = jnp.where(item == i, mod_ref[i, 1:2, :], scale)
                h_s[part * count : (part + 1) * count, :] = (normed * (1.0 + scale) + shift).astype(jnp.bfloat16)
            both = rows_of(index, rows)
            hidden = h_s[...]
            q = dot(hidden, w_ref[:, :width]).astype(jnp.bfloat16)
            q_s[both, :] = (q.astype(jnp.float32) * 0.125).astype(jnp.bfloat16)
            kv_s[both, :width] = dot(hidden, w_ref[:, width : 2 * width]).astype(jnp.bfloat16)
            kv_s[both, width:] = dot(hidden, w_ref[:, 2 * width :]).astype(jnp.bfloat16)
            for write in writes(index):
                write.start()

        @pl.when(index == 0)
        def _():
            own_ref[...] = h_s[:count, :]

    @pl.loop(0, number)
    def _(index):
        @pl.when(live(index))
        def _():
            for write in writes(index):
                write.wait()


def project(meta, modulation, weight, x_blocks, chips, total, earlier, items, shards, name):
    count, width = x_blocks[0].shape
    part = len(x_blocks) * count
    whole = pl.BlockSpec(memory_space=pltpu.VMEM)
    anywhere = pl.BlockSpec(memory_space=pl.ANY)
    before = 3 + len(x_blocks)
    return pl.pallas_call(
        partial(project_kernel, items, shards, chips),
        out_shape=(
            jax.ShapeDtypeStruct((total, width), jnp.bfloat16),
            jax.ShapeDtypeStruct((total, 2 * width), jnp.bfloat16),
            jax.ShapeDtypeStruct((count, width), jnp.bfloat16),
        ),
        in_specs=[pl.BlockSpec(memory_space=pltpu.SMEM), whole, whole]
        + [anywhere] * (len(x_blocks) + len(earlier)),
        out_specs=(anywhere, anywhere, whole),
        input_output_aliases={before: 0, before + 1: 1} if earlier else {},
        scratch_shapes=[
            pltpu.VMEM((part, width), jnp.bfloat16),
            pltpu.VMEM((2 * count, width), jnp.bfloat16),
            pltpu.VMEM((part, width), jnp.bfloat16),
            pltpu.VMEM((part, 2 * width), jnp.bfloat16),
            pltpu.SemaphoreType.DMA((len(x_blocks),)),
            pltpu.SemaphoreType.DMA((len(x_blocks),)),
        ],
        compiler_params=pltpu.CompilerParams(vmem_limit_bytes=40 * MIB),
        cost_estimate=pl.CostEstimate(
            flops=3 * part * width * width,
            bytes_accessed=2 * 4 * part * width,
            transcendentals=0,
        ),
        name=name,
    )(meta, modulation, weight, *x_blocks, *earlier)


def heads_of(ref, here, pair):
    return ref[here, pair * 128 : (pair + 1) * 128]


def spread(count, group, base):
    return pl.BlockSpec((count, group * 128), lambda p: (0, p + base // group))


ALL = slice(None)


def attend_kernel(items, shards, kind, blocks, group, meta, q_ref, k_ref, v_ref, o_ref, low_ref, f_ref, qa, bias_ref, s, m, l, acc):
    count = q_ref.shape[0]
    rows = k_ref.shape[0] // blocks
    frame = Frame(meta, items, count, shards)
    active, bias = block_rule(frame, kind, rows)
    step = pl.program_id(0)
    lane = lanes(count)
    own = frame.items_of_rows(frame.position * count, count)
    own_item = (lane == own).astype(jnp.float32)
    fill_bias(blocks, rows, active, bias, bias_ref, False)
    for g in range(group):
        stack_heads(qa.at[g], heads_of(q_ref, ALL, g), [own_item, own_item])
        m[g] = jnp.full((2 * count, 128), far, jnp.float32)
        l[g] = jnp.zeros((2 * count, 128), jnp.float32)
        acc[g] = jnp.zeros((2 * count, 128), jnp.float32)

    def score(block):
        here = rows_of(block, rows)
        for g in range(group):
            scores = times_transposed(qa[g], jnp.concatenate([heads_of(k_ref, here, g), bias_ref[here, :]], axis=1))
            s[g, block] = scores
            high = m[g]
            for c in range(rows // 128):
                high = jnp.maximum(high, scores[:, c * 128 : (c + 1) * 128])
            m[g] = high

    each_active(blocks, active, score)
    tops = []
    for g in range(group):
        tops.append(jnp.max(m[g], axis=1, keepdims=True))
        m[g] = jnp.broadcast_to(tops[g], (2 * count, 128))

    def weigh(block):
        here = rows_of(block, rows)
        for g in range(group):
            high = m[g]
            total = l[g]
            parts = []
            for c in range(rows // 128):
                part = jnp.exp(s[g, block, :, c * 128 : (c + 1) * 128] - high)
                total = total + part
                parts.append(part.astype(jnp.bfloat16))
            l[g] = total
            acc[g] = acc[g] + dot(jnp.concatenate(parts, axis=1), heads_of(v_ref, here, g))

    each_active(blocks, active, weigh)
    features = jnp.where(step == 0, own_item, f_ref[...].astype(jnp.float32))
    for g in range(group):
        total = jnp.sum(l[g], axis=1, keepdims=True)
        result = merge_heads(acc[g] / total)
        lse = tops[g] + jnp.log(total)
        for h in range(2):
            start = LSE_LANE + 3 * (2 * (step * group + g) + h)
            for number, piece in enumerate(pieces(lse[h * count : (h + 1) * count])):
                features = jnp.where(lane == start + number, piece, features)
        o_ref[:, g * 128 : (g + 1) * 128] = result
        low_ref[:, g * 128 : (g + 1) * 128] = result.astype(jnp.bfloat16)
    f_ref[...] = features.astype(jnp.bfloat16)


def attend(meta, count, queries, kv, kind, blocks, items, shards, name, group=3):
    width = queries.shape[1]
    pairs = width // 128
    total = kv.shape[0]
    rows = total // blocks
    tile = spread(count, group, 0)
    return pl.pallas_call(
        partial(attend_kernel, items, shards, kind, blocks, group),
        grid=(pairs // group,),
        out_shape=(
            jax.ShapeDtypeStruct((count, width), jnp.float32),
            jax.ShapeDtypeStruct((count, width), jnp.bfloat16),
            jax.ShapeDtypeStruct((count, 128), jnp.bfloat16),
        ),
        in_specs=[
            pl.BlockSpec(memory_space=pltpu.SMEM),
            tile,
            spread(total, group, 0),
            spread(total, group, pairs),
        ],
        out_specs=(tile, tile, pl.BlockSpec((count, 128), lambda p: (0, 0))),
        scratch_shapes=[
            pltpu.VMEM((group, 2 * count, 256), jnp.bfloat16),
            pltpu.VMEM((total, 128), jnp.bfloat16),
            pltpu.VMEM((group, blocks, 2 * count, rows), jnp.float32),
            pltpu.VMEM((group, 2 * count, 128), jnp.float32),
            pltpu.VMEM((group, 2 * count, 128), jnp.float32),
            pltpu.VMEM((group, 2 * count, 128), jnp.float32),
        ],
        compiler_params=pltpu.CompilerParams(vmem_limit_bytes=48 * MIB),
        cost_estimate=pl.CostEstimate(
            flops=2 * count * total * width,
            bytes_accessed=4 * total * width,
            transcendentals=count * total * H // 2,
        ),
        name=name,
    )(meta, queries, kv, kv)


def query_side(pair, features, q, do, qa, da):
    lane = lanes(q.shape[0])
    heads = [2 * pair, 2 * pair + 1]
    stack_heads(qa, q, [jnp.where((lane < LSE_LANE) | head_lanes(lane, LSE_LANE, head), features, 0.0) for head in heads])
    stack_heads(da, do, [jnp.where(head_lanes(lane, DELTA_LANE, head), features, 0.0) for head in heads])


def query_step(qa, da, keys, values, bias):
    minus = jnp.where(delta_lanes(lanes(keys.shape[0])), -1.0, 0.0)
    probs = jnp.exp(times_transposed(qa[...], jnp.concatenate([keys, bias], axis=1)))
    slope = times_transposed(da[...], beside(values, minus))
    return dot((probs * slope).astype(jnp.bfloat16), keys)


def key_side(pair, k, v, mask, ka, va):
    lane = lanes(k.shape[0])
    heads = [2 * pair, 2 * pair + 1]
    stack_heads(ka, k, [jnp.where(head_lanes(lane, LSE_LANE, head), -1.0, mask) for head in heads])
    stack_heads(va, v, [jnp.where(head_lanes(lane, DELTA_LANE, head), -1.0, 0.0) for head in heads])


def key_step(ka, va, q, do, features):
    probs = jnp.exp(times_transposed(ka[...], jnp.concatenate([q, features], axis=1)))
    slope = times_transposed(va[...], jnp.concatenate([do, features], axis=1))
    return dot((probs * slope).astype(jnp.bfloat16), q), dot(probs.astype(jnp.bfloat16), do)


def query_grad_kernel(items, shards, blocks, group, meta, q_ref, do_ref, f_ref, k_ref, v_ref, dq_ref, qa, da, bias_ref, acc):
    count = q_ref.shape[0]
    rows = k_ref.shape[0] // blocks
    frame = Frame(meta, items, count, shards)
    active, bias = block_rule(frame, "frames", rows)
    fill_bias(blocks, rows, active, bias, bias_ref, True)
    features = f_ref[...].astype(jnp.float32)
    for g in range(group):
        pair = pl.program_id(0) * group + g
        query_side(pair, features, heads_of(q_ref, ALL, g), heads_of(do_ref, ALL, g), qa.at[g], da.at[g])
        acc[g] = jnp.zeros((2 * count, 128), jnp.float32)

    def step(block):
        here = rows_of(block, rows)
        for g in range(group):
            acc[g] = acc[g] + query_step(
                qa.at[g], da.at[g], heads_of(k_ref, here, g), heads_of(v_ref, here, g), bias_ref[here, :]
            )

    each_active(blocks, active, step)
    for g in range(group):
        dq_ref[:, g * 128 : (g + 1) * 128] = (merge_heads(acc[g]) * 0.125).astype(jnp.bfloat16)


def query_grad(meta, queries, grad_out, features, kv, blocks, items, shards, name, group=3):
    count, width = grad_out.shape
    pairs = width // 128
    total = kv.shape[0]
    tile = spread(count, group, 0)
    return pl.pallas_call(
        partial(query_grad_kernel, items, shards, blocks, group),
        grid=(pairs // group,),
        out_shape=jax.ShapeDtypeStruct((count, width), jnp.bfloat16),
        in_specs=[
            pl.BlockSpec(memory_space=pltpu.SMEM),
            tile,
            tile,
            pl.BlockSpec((count, 128), lambda p: (0, 0)),
            spread(total, group, 0),
            spread(total, group, pairs),
        ],
        out_specs=tile,
        scratch_shapes=[
            pltpu.VMEM((group, 2 * count, 256), jnp.bfloat16),
            pltpu.VMEM((group, 2 * count, 256), jnp.bfloat16),
            pltpu.VMEM((total, 128), jnp.bfloat16),
            pltpu.VMEM((group, 2 * count, 128), jnp.float32),
        ],
        compiler_params=pltpu.CompilerParams(vmem_limit_bytes=48 * MIB),
        cost_estimate=pl.CostEstimate(
            flops=3 * count * total * width,
            bytes_accessed=4 * total * width,
            transcendentals=count * total * H // 2,
        ),
        name=name,
    )(meta, queries, grad_out, features, kv, kv)


def frame_key_grad_kernel(items, shards, blocks, group, meta, q_ref, k_ref, v_ref, all_ref, dk_ref, dv_ref, ka, va, dka, dva, do_s, sem):
    count, width = dk_ref.shape[0], do_s.shape[1] - 128
    rows = q_ref.shape[0] // blocks
    frame = Frame(meta, items, count, shards)

    def arrivals(act):
        @pl.when(pl.program_id(0) == 0)
        def _():
            for block in range(2 * blocks):
                start, live = frame.chip(jnp.int32(block // 2))
                first = start + (frame.position + block) % 2 * count

                @pl.when(live)
                def _(block=block, first=first):
                    act(
                        pltpu.make_async_copy(
                            all_ref.at[pl.ds(pl.multiple_of(first, count), count), :],
                            do_s.at[pl.ds(block * count, count), :],
                            sem.at[block],
                        )
                    )

    arrivals(lambda copy: copy.start())
    mask = item_bias(frame, frame.items_of_rows(frame.position * count, count))
    for g in range(group):
        pair = pl.program_id(0) * group + g
        key_side(pair, heads_of(k_ref, ALL, g), heads_of(v_ref, ALL, g), mask, ka.at[g], va.at[g])
        dka[g] = jnp.zeros((2 * count, 128), jnp.float32)
        dva[g] = jnp.zeros((2 * count, 128), jnp.float32)
    arrivals(lambda copy: copy.wait())

    def step(block):
        here = rows_of(block, rows)
        for g in range(group):
            column = pl.multiple_of((pl.program_id(0) * group + g) * 128, 128)
            dk, dv = key_step(
                ka.at[g], va.at[g], heads_of(q_ref, here, g), do_s[here, pl.ds(column, 128)], do_s[here, width:]
            )
            dka[g] = dka[g] + dk
            dva[g] = dva[g] + dv

    each_active(blocks, lambda block: frame.chip(block)[1], step)
    for g in range(group):
        dk_ref[:, g * 128 : (g + 1) * 128] = merge_heads(dka[g]).astype(jnp.bfloat16)
        dv_ref[:, g * 128 : (g + 1) * 128] = merge_heads(dva[g]).astype(jnp.bfloat16)


def frame_key_grad(meta, q_window, do_all, kv, count, blocks, items, shards, name, group=3):
    total, width = q_window.shape
    pairs = width // 128
    tile = spread(count, group, 0)
    wide = spread(total, group, 0)
    return pl.pallas_call(
        partial(frame_key_grad_kernel, items, shards, blocks, group),
        grid=(pairs // group,),
        out_shape=(jax.ShapeDtypeStruct((count, width), jnp.bfloat16),) * 2,
        in_specs=[
            pl.BlockSpec(memory_space=pltpu.SMEM),
            wide,
            tile,
            spread(count, group, pairs),
        ]
        + [pl.BlockSpec(memory_space=pl.ANY)],
        out_specs=(tile, tile),
        scratch_shapes=[pltpu.VMEM((group, 2 * count, 256), jnp.bfloat16)] * 2
        + [pltpu.VMEM((group, 2 * count, 128), jnp.float32)] * 2
        + [pltpu.VMEM((total, width + 128), jnp.bfloat16), pltpu.SemaphoreType.DMA((2 * blocks,))],
        compiler_params=pltpu.CompilerParams(vmem_limit_bytes=48 * MIB),
        cost_estimate=pl.CostEstimate(
            flops=4 * count * total * width,
            bytes_accessed=4 * total * width,
            transcendentals=count * total * H // 2,
        ),
        name=name,
    )(meta, q_window, kv, kv, do_all)


def text_grad_kernel(items, shards, group, meta, q_ref, do_ref, f_ref, k_ref, v_ref, dq_ref, dkv_ref, qa, da, ka, va, acc):
    count = q_ref.shape[0]
    rows = k_ref.shape[0] // items
    frame = Frame(meta, items, count, shards)
    features = f_ref[...].astype(jnp.float32)
    pairs = [pl.program_id(0) * group + g for g in range(group)]
    for g in range(group):
        query_side(pairs[g], features, heads_of(q_ref, ALL, g), heads_of(do_ref, ALL, g), qa.at[g], da.at[g])
        acc[g] = jnp.zeros((2 * count, 128), jnp.float32)

    @pl.loop(0, items)
    def _(item):
        here = rows_of(item, rows)
        live = (item >= frame.first) & (item <= frame.last)

        @pl.when(live)
        def _():
            mask = text_bias(frame, item, rows)
            bias = jnp.where(lse_lanes(lanes(rows)), -1.0, mask).astype(jnp.bfloat16)
            for g in range(group):
                keys, values = heads_of(k_ref, here, g), heads_of(v_ref, here, g)
                acc[g] = acc[g] + query_step(qa.at[g], da.at[g], keys, values, bias)
                key_side(pairs[g], keys, values, mask, ka.at[g], va.at[g])
                grads = key_step(ka.at[g], va.at[g], heads_of(q_ref, ALL, g), heads_of(do_ref, ALL, g), f_ref[...])
                for which, grad in enumerate(grads):
                    dkv_ref[which, here, g * 128 : (g + 1) * 128] = merge_heads(grad).astype(jnp.bfloat16)

        @pl.when(jnp.logical_not(live))
        def _():
            for which in range(2):
                dkv_ref[which, here, :] = jnp.zeros((rows, group * 128), jnp.bfloat16)

    for g in range(group):
        dq_ref[:, g * 128 : (g + 1) * 128] = (merge_heads(acc[g]) * 0.125).astype(jnp.bfloat16)


def text_grad(meta, queries, grad_out, features, kv, items, shards, name, group=3):
    count, width = queries.shape
    pairs = width // 128
    total = kv.shape[0]
    tile = spread(count, group, 0)
    rows = total // items
    return pl.pallas_call(
        partial(text_grad_kernel, items, shards, group),
        grid=(pairs // group,),
        out_shape=(
            jax.ShapeDtypeStruct((count, width), jnp.bfloat16),
            jax.ShapeDtypeStruct((2, total, width), jnp.bfloat16),
        ),
        in_specs=[
            pl.BlockSpec(memory_space=pltpu.SMEM),
            tile,
            tile,
            pl.BlockSpec((count, 128), lambda p: (0, 0)),
            spread(total, group, 0),
            spread(total, group, pairs),
        ],
        out_specs=(tile, pl.BlockSpec((2, total, group * 128), lambda p: (0, 0, p))),
        scratch_shapes=[pltpu.VMEM((group, 2 * count, 256), jnp.bfloat16)] * 2
        + [pltpu.VMEM((group, 2 * rows, 256), jnp.bfloat16)] * 2
        + [pltpu.VMEM((group, 2 * count, 128), jnp.float32)],
        compiler_params=pltpu.CompilerParams(vmem_limit_bytes=48 * MIB),
        cost_estimate=pl.CostEstimate(
            flops=7 * count * rows * 2 * width,
            bytes_accessed=8 * total * width,
            transcendentals=count * rows * H * 2,
        ),
        name=name,
    )(meta, queries, grad_out, features, kv, kv)


def mlp_kernel(h_ref, d_ref, up_ref, down_ref, act_ref, m_ref, dh_ref):
    step = pl.program_id(0)
    last = pl.num_programs(0) - 1

    @pl.when(step < last)
    def _():
        u = dot(h_ref[...], up_ref[...])
        slope = times_transposed(d_ref[...], down_ref[...])
        inner = 0.7978845608028654 * (u + 0.044715 * (u * u * u))
        t = jnp.tanh(inner)
        g = (0.5 * u * (1.0 + t)).astype(jnp.bfloat16)
        bend = 0.7978845608028654 * (1.0 + 0.134145 * (u * u))
        du = (slope * (0.5 * (1.0 + t) + 0.5 * u * (1.0 - t * t) * bend)).astype(jnp.bfloat16)
        act_ref[0, 0] = g
        act_ref[0, 1] = du
        m = dot(g, down_ref[...])
        dh = times_transposed(du, up_ref[...])

        @pl.when(step == 0)
        def _():
            m_ref[...] = m
            dh_ref[...] = dh

        @pl.when(step > 0)
        def _():
            m_ref[...] = m_ref[...] + m
            dh_ref[...] = dh_ref[...] + dh

    @pl.when(step == last)
    def _():
        act_ref[0, 0] = h_ref[...]
        act_ref[0, 1] = d_ref[...]


def mlp(hidden, grad, w_up, w_down):
    count, width = hidden.shape
    chunks = w_up.shape[1] // width
    whole = pl.BlockSpec((count, width), lambda c: (0, 0))
    held = lambda c: jnp.minimum(c, chunks - 1)
    return pl.pallas_call(
        mlp_kernel,
        grid=(chunks + 1,),
        out_shape=(
            jax.ShapeDtypeStruct((chunks + 1, 2, count, width), jnp.bfloat16),
            jax.ShapeDtypeStruct((count, width), jnp.float32),
            jax.ShapeDtypeStruct((count, width), jnp.float32),
        ),
        in_specs=[
            whole,
            whole,
            pl.BlockSpec((width, width), lambda c: (0, held(c))),
            pl.BlockSpec((width, width), lambda c: (held(c), 0)),
        ],
        out_specs=(pl.BlockSpec((1, 2, count, width), lambda c: (c, 0, 0, 0)), whole, whole),
        compiler_params=pltpu.CompilerParams(vmem_limit_bytes=40 * MIB),
        cost_estimate=pl.CostEstimate(
            flops=8 * count * width * w_up.shape[1],
            bytes_accessed=4 * width * w_up.shape[1] + 4 * count * w_up.shape[1],
            transcendentals=count * w_up.shape[1],
        ),
        name="mlp",
    )(hidden, grad, w_up, w_down)


UNIT = 192
X_BIT, Y_BIT = 0, 1


def rows_picked(x, core):
    row = lax.broadcasted_iota(jnp.int32, (384, 768), 0)
    column = lax.broadcasted_iota(jnp.int32, (384, 768), 1)
    chip = (row >= 96).astype(jnp.int32) + (row >= 192).astype(jnp.int32) + (row >= 288).astype(jnp.int32)
    pick = (column == row + 96 * (chip + core)).astype(jnp.bfloat16)
    return times_transposed(pick, x).astype(jnp.bfloat16)


def one_above_other(upper, lower):
    return jnp.concatenate([upper, lower], axis=0)


def finish_kernel(items, shards, meta, mod_ref, w_ref, d_ref, x_ref, dx_ref, a_ref, dh_ref, n_ref, dy_ref, m_ref, out_ref, sum_ref):
    count, width = x_ref.shape
    frame = Frame(meta, items, count, shards)
    item = frame.items_of_rows(frame.position * count, count)
    grad = times_transposed(d_ref[...], w_ref[...])
    normed, inverse = layer_norm(x_ref[...].astype(jnp.float32))
    scale = jnp.zeros((count, width), jnp.float32)
    for i in range(items):
        scale = jnp.where(item == i, mod_ref[i, 1:2, :], scale)
    dx = dx_ref[...]
    out_ref[...] = dx + norm_back(grad * (1.0 + scale), normed, inverse)
    dh = dh_ref[...]
    terms = (
        grad,
        grad * normed,
        dx * a_ref[...],
        dh,
        dh * n_ref[...],
        dy_ref[...].astype(jnp.float32) * m_ref[...],
    )
    for number, term in enumerate(terms):
        rows = [jnp.sum(jnp.where(item == i, term, 0.0), axis=0, keepdims=True) for i in range(items)]
        rows += [jnp.zeros((8 - items, width), jnp.float32)]
        sum_ref[number] = jnp.concatenate(rows, axis=0)


def finish(meta, modulation, weight, grads, frames, *arrays_items_shards):
    *arrays, items, shards = arrays_items_shards
    count, width = frames.shape
    whole = pl.BlockSpec(memory_space=pltpu.VMEM)
    return pl.pallas_call(
        partial(finish_kernel, items, shards),
        out_shape=(
            jax.ShapeDtypeStruct((count, width), jnp.float32),
            jax.ShapeDtypeStruct((6, 8, width), jnp.float32),
        ),
        in_specs=[pl.BlockSpec(memory_space=pltpu.SMEM)] + [whole] * (4 + len(arrays)),
        out_specs=(whole, whole),
        compiler_params=pltpu.CompilerParams(vmem_limit_bytes=40 * MIB),
        cost_estimate=pl.CostEstimate(
            flops=6 * count * width * width, bytes_accessed=6 * width * width + 30 * count * width, transcendentals=0
        ),
        name="finish",
    )(meta, modulation, weight, grads, frames, *arrays)


class Packer:
    def __init__(self, meta, items, outputs):
        self.core, self.chip = meta[0] % 2, meta[0] // 2
        self.mine = meta[1 + 2 * items]
        self.outputs = outputs

    def store(self, name, owner, owner_chip, row, values):
        scratch, first = self.outputs[name]
        relative = owner ^ self.mine
        where = ((relative >> first) % 2, (relative >> (1 - first)) % 2, owner_chip ^ self.chip)
        scratch[where + (slice(row, row + values.shape[0]),)] = values.astype(jnp.bfloat16)

    def store_split(self, name, pair, row, values, chips):
        rolled = pltpu.roll(values, UNIT, 1)
        each = values.shape[0] // len(chips)
        left = lax.broadcasted_iota(jnp.int32, (each // 2, 384), 1) < UNIT
        for number, owner_chip in enumerate(chips):
            upper = slice(number * each, number * each + each // 2)
            lower = slice(number * each + each // 2, (number + 1) * each)
            self.store(name, 2 * pair, owner_chip, row, jnp.where(left, values[upper], rolled[lower]))
            self.store(name, 2 * pair + 1, owner_chip, row, jnp.where(left, rolled[upper], values[lower]))


def core_columns(core, number, each):
    return pl.ds(pl.multiple_of(number * 2 * each + core * each, 128), each)


def third(values, number):
    return values[:, number * 384 : (number + 1) * 384]


def pack_mlp_kernel(items, meta, own, sib, down_s, up_s):
    packer = Packer(meta, items, {"down": (down_s, Y_BIT), "up": (up_s, X_BIT)})
    both = lambda chunk, which: one_above_other(own[chunk, which], sib[chunk, which])
    grad = both(4, 1)
    for owner_chip in range(4):
        here = core_columns(packer.core, 0, 384)
        left = one_above_other(own[owner_chip, 0, :, here], sib[owner_chip, 0, :, here])
        values = contract_rows(left, grad)
        for pair in range(2):
            packer.store_split("down", pair, 0, third(values, pair), [owner_chip])
    left = rows_picked(both(4, 0), packer.core)
    for owner in range(4):
        values = dot(left, both(owner, 1))
        for owner_chip in range(4):
            for half in range(2):
                packer.store(
                    "up", owner, owner_chip, half * 96, third(values, half)[owner_chip * 96 : (owner_chip + 1) * 96]
                )


def pack_middle_kernel(items, meta, own, sib, text_own, text_sib, text, rows_ref, square_s, text_s):
    packer = Packer(meta, items, {"square": (square_s, Y_BIT), "text": (text_s, X_BIT)})
    both = lambda which: one_above_other(own[which], sib[which])
    for number in range(3):
        values = dot(rows_picked(both(2 * number), packer.core), both(2 * number + 1))
        for pair in range(2):
            packer.store_split("square", pair, number * 48, third(values, pair), range(4))
    sums = [
        (text_own[which].astype(jnp.float32) + text_sib[which].astype(jnp.float32)).astype(jnp.bfloat16)
        for which in range(2)
    ]
    left = jnp.concatenate([text[:, core_columns(packer.core, chip, 128)] for chip in range(4)], axis=1)
    for which in range(2):
        values = contract_rows(left, sums[which])
        for owner_chip in range(4):
            for half in range(2):
                packer.store(
                    "text", 2 * which + half, owner_chip, 0, third(values, half)[owner_chip * 128 : (owner_chip + 1) * 128]
                )
    share = text.shape[0] // items // 8
    for item in range(items):
        for which in range(2):
            for owner_chip in range(4):
                start = (item * 8 + owner_chip * 2) * share
                pick = jnp.where(
                    packer.core == 0, sums[which][start : start + share], sums[which][start + share : start + 2 * share]
                )
                rows_ref[owner_chip ^ packer.chip, which, item * share : (item + 1) * share, :] = pick


def pack_qkv_kernel(items, meta, h_own, h_sib, own, sib, plain_s, split_s):
    packer = Packer(meta, items, {"plain": (plain_s, X_BIT), "split": (split_s, Y_BIT)})
    left = rows_picked(one_above_other(h_own[...], h_sib[...]), packer.core)
    values = []
    for number in range(3):
        product = dot(left, one_above_other(own[number], sib[number]))
        values += [third(product, 0), third(product, 1)]
    for owner, column in enumerate((0, 2, 3, 5)):
        for owner_chip in range(4):
            packer.store("plain", owner, owner_chip, 0, values[column][owner_chip * 96 : (owner_chip + 1) * 96])
    for pair, column in enumerate((1, 4)):
        packer.store_split("split", pair, 0, values[column], range(4))


def packing(kernel, items, inputs, groups, more, *refs):
    ins, refs = refs[:inputs], refs[inputs:]
    outs, extra, scratch, sem = refs[: 2 * groups], refs[2 * groups : -groups - 1], refs[-groups - 1 : -1], refs[-1]
    kernel(items, *ins, *extra, *scratch)
    copies = [
        pltpu.make_async_copy(scratch[i // 2].at[1 - i % 2], outs[i], sem.at[i]) for i in range(2 * groups)
    ]
    for copy in copies:
        copy.start()
    for copy in copies:
        copy.wait()


def pack(kernel, meta, operands, rows, items, name, more=()):
    whole = pl.BlockSpec(memory_space=pltpu.VMEM)
    shapes = [jax.ShapeDtypeStruct((2, 4, each, 384), jnp.bfloat16) for each in rows for _ in range(2)] + list(more)
    return pl.pallas_call(
        partial(packing, kernel, items, 1 + len(operands), len(rows), more),
        out_shape=tuple(shapes),
        in_specs=[pl.BlockSpec(memory_space=pltpu.SMEM)] + [whole] * len(operands),
        out_specs=tuple([pl.BlockSpec(memory_space=pl.ANY)] * (2 * len(rows)) + [whole] * len(more)),
        scratch_shapes=[pltpu.VMEM((2, 2, 4, each, 384), jnp.bfloat16) for each in rows]
        + [pltpu.SemaphoreType.DMA((2 * len(rows),))],
        compiler_params=pltpu.CompilerParams(vmem_limit_bytes=48 * MIB),
        cost_estimate=pl.CostEstimate(
            flops=2 * 512 * 16 * sum(rows) * 384,
            bytes_accessed=32 * sum(rows) * 384 + 2 * sum(each.size for each in operands),
            transcendentals=0,
        ),
        name=name,
    )(meta, *operands)


def trade(values, axis, bit):
    size = lax.axis_size(axis)
    return lax.ppermute(values, axis, [(i, i ^ (1 << bit)) for i in range(size)])


def halve(keep, send, axis, bit, after=()):
    got = trade(send, axis, bit)
    if after:
        [keep] = hold((keep,), *after)
    return keep.astype(jnp.float32) + got.astype(jnp.float32)


def over_batch(send, keep, first, after=((), ())):
    part = halve(keep, send, "batch", first, after[0]).astype(jnp.bfloat16)
    return halve(part[0], part[1], "batch", 1 - first, after[1]).astype(jnp.bfloat16)


def over_chips(part, after=((), ())):
    part = part.reshape(2, 2, *part.shape[1:])
    part = halve(part[:, 0], part[:, 1], "seq", 1, after[0]).astype(jnp.bfloat16)
    return halve(part[0], part[1], "seq", 2, after[1])


def unsplit(rows):
    return jnp.concatenate([rows[:, :UNIT], rows[:, UNIT:]], axis=0)


def with_deltas(features, grad_out, attn_exact):
    width = attn_exact.shape[1]
    lane = jnp.arange(128)[None, :]
    head = (jnp.arange(width) // (width // H))[:, None]
    pick = ((lane >= DELTA_LANE) & ((lane - DELTA_LANE) // 3 == head)).astype(jnp.float32)
    delta = jnp.dot(
        grad_out.astype(jnp.float32) * attn_exact,
        pick,
        precision=lax.Precision.HIGHEST,
        preferred_element_type=jnp.float32,
    )
    high = lax.reduce_precision(delta, 8, 7)
    middle = lax.reduce_precision(delta - high, 8, 7)
    which = (lane - DELTA_LANE) % 3
    piece = jnp.where(which == 0, high, jnp.where(which == 1, middle, delta - high - middle))
    inside = (lane >= DELTA_LANE) & (lane < DELTA_LANE + 3 * H)
    return jnp.where(inside, piece.astype(jnp.bfloat16), features)


def hop(below, above, shards):
    up = [(i, i + 2) for i in range(shards - 2)]
    return lax.ppermute(below, "seq", up), lax.ppermute(above, "seq", [(j, i) for i, j in up])


def hold(values, *first):
    held = lax.optimization_barrier((*values, *first))
    return held[: len(values)]


def body(
    frames,
    cotangent,
    modulation,
    lengths,
    text,
    text_len,
    w_qkv,
    w_o,
    w_cq,
    w_ckv,
    w_co,
    w_up,
    w_down,
):
    local = frames[0]
    count, width = local.shape
    items = lengths.shape[1]
    text_rows, text_width = text.shape[2:]
    shards = lax.axis_size("seq")
    position = lax.axis_index("seq")
    reach = min(-(-(LONGEST - 1) // (2 * count)), shards // 2 - 1)
    chips = 1 + 2 * reach
    meta = jnp.concatenate(
        [position[None].astype(jnp.int32), lengths[0], text_len[0], lax.axis_index("batch")[None].astype(jnp.int32)]
    )
    item_range = jnp.arange(items, dtype=jnp.int32)
    ends = jnp.sum(jnp.where(item_range[None, :] <= item_range[:, None], lengths[0][None, :], 0), axis=1)
    place = position * count + jnp.arange(count, dtype=jnp.int32)
    query_items = jnp.sum((place[:, None] >= ends[None, :]).astype(jnp.int32), axis=1)[:, None]
    mod = modulation[0]

    def per_frame(which):
        found = jnp.broadcast_to(mod[0, which][None, :], (count, width))
        for item in range(1, items):
            found = jnp.where(query_items == item, mod[item, which][None, :], found)
        return found

    swap = [(i, i ^ 1) for i in range(shards)]

    def sibling(values):
        return lax.ppermute(values, "seq", swap)

    fast = shards == 8 and lax.axis_size("batch") == 4 and width == 768

    text_proj = jnp.dot(
        text[0].reshape(items * text_rows, text_width), w_ckv, preferred_element_type=jnp.float32
    ).astype(jnp.bfloat16)
    sides = list(hold(hop(local, local, shards), text_proj))
    for _ in range(1, reach):
        sides += hop(*sides[-2:], shards)

    def with_siblings(blocks):
        return [each for block in blocks for each in (block, sibling(block))]

    total = 2 * chips * count
    near = with_siblings([local] + sides[:2])
    q_window, kv, hidden_one = project(meta, mod, w_qkv, near, range(3), total, (), items, shards, "project_near")
    if reach > 1:
        apart = with_siblings(hold(sides[2:], kv))
        q_window, kv, _ = project(
            meta, mod, w_qkv, apart, range(3, chips), total, (q_window, kv), items, shards, "project_far"
        )
    inputs = local.astype(jnp.float32)
    attn_exact, attended, features = attend(meta, count, q_window, kv, "frames", chips, items, shards, "self_attend")
    if fast:
        hidden_sib = sibling(hidden_one)
        [attended] = hold((attended,), hidden_sib)
    branch_one = jnp.dot(attended, w_o, preferred_element_type=jnp.float32)
    after_attn = inputs + per_frame(2) * branch_one
    normed_cross, inverse_cross = layer_norm(after_attn)
    cross_in = normed_cross.astype(jnp.bfloat16)
    cross_queries = jnp.dot(cross_in, w_cq, preferred_element_type=jnp.float32).astype(jnp.bfloat16)
    cross_queries = (cross_queries.astype(jnp.float32) * 0.125).astype(jnp.bfloat16)
    cross_exact, cross_out, cross_features = attend(
        meta, count, cross_queries, text_proj, "text", items, items, shards, "cross_attend"
    )
    branch_two = jnp.dot(cross_out, w_co, preferred_element_type=jnp.float32)
    after_cross = after_attn + branch_two
    normed_two, inverse_two = layer_norm(after_cross)
    hidden_two = (normed_two * (1.0 + per_frame(4)) + per_frame(3)).astype(jnp.bfloat16)
    gate_two = per_frame(5)
    grad_out = cotangent[0].astype(jnp.float32)
    grad_branch_three = (grad_out * gate_two).astype(jnp.bfloat16)
    acts, branch_three, grad_hidden_two = mlp(hidden_two, grad_branch_three, w_up, w_down)
    if fast:
        mlp_parts = pack(
            pack_mlp_kernel, meta, (acts, sibling(acts)), (192, 192), items, "pack_mlp"
        )
    result = after_cross + gate_two * branch_three
    grad_cross = grad_out + norm_back(grad_hidden_two * (1.0 + per_frame(4)), normed_two, inverse_two)
    grad_branch_two = grad_cross.astype(jnp.bfloat16)
    if fast:
        grad_branch_two, *mlp_parts = lax.optimization_barrier((grad_branch_two, *mlp_parts))
    grad_cross_out = times_transposed(grad_branch_two, w_co).astype(jnp.bfloat16)
    cross_features = with_deltas(cross_features, grad_cross_out, cross_exact)
    grad_cross_queries, text_terms = text_grad(
        meta, cross_queries, grad_cross_out, cross_features, text_proj, items, shards, "cross_grad"
    )
    grad_attn_res = grad_cross + norm_back(
        times_transposed(grad_cross_queries, w_cq), normed_cross, inverse_cross
    )
    grad_branch_one = (grad_attn_res * per_frame(2)).astype(jnp.bfloat16)
    if fast:
        text_sib = sibling(text_terms)
        [grad_branch_one] = hold((grad_branch_one,), text_sib)
    grad_attended = times_transposed(grad_branch_one, w_o).astype(jnp.bfloat16)
    features = with_deltas(features, grad_attended, attn_exact)
    if fast:
        middle = jnp.stack([cross_out, grad_branch_two, cross_in, grad_cross_queries, attended, grad_branch_one])
        middle_sib = sibling(middle)
    do_all = lax.all_gather(jnp.concatenate([grad_attended, features], axis=1), "seq", axis=0, tiled=True)
    grad_queries = query_grad(
        meta, q_window, grad_attended, features, kv, chips, items, shards, "self_query_grad"
    )
    share_rows = text_rows // shards
    if fast:
        middle_parts = pack(
            pack_middle_kernel,
            meta,
            (middle, middle_sib, text_terms, text_sib, text[0].reshape(items * text_rows, text_width)),
            (144, 128),
            items,
            "pack_middle",
            (jax.ShapeDtypeStruct((4, 2, items * share_rows, width), jnp.bfloat16),),
        )
        [do_all] = hold((do_all,), middle_parts[0])
    grad_keys, grad_values = frame_key_grad(
        meta, q_window, do_all, kv, count, chips, items, shards, "self_key_grad"
    )
    grad_projected = jnp.concatenate([grad_queries, grad_keys, grad_values], axis=1)
    if fast:
        kv_own = jnp.stack([grad_queries, grad_keys, grad_values])
        kv_sib = sibling(kv_own)
        qkv_parts = pack(
            pack_qkv_kernel,
            meta,
            (hidden_one, hidden_sib, kv_own, kv_sib),
            (96, 48),
            items,
            "pack_qkv",
        )
        [grad_projected] = hold((grad_projected,), *qkv_parts)
    grad_inputs, terms = finish(
        meta, mod, w_qkv, grad_projected, local, grad_attn_res, branch_one, grad_hidden_two, normed_two, cotangent[0],
        branch_three, items, shards,
    )
    for bit in range(shards.bit_length() - 1):
        terms = terms + trade(terms, "seq", bit)
    own = width // shards
    terms = lax.dynamic_slice_in_dim(terms, position * own, own, 2)
    shares = terms[:, :items].transpose(1, 0, 2)
    if fast:
        points = ((grad_queries,), (middle_parts[0],))
        down_part = over_batch(*mlp_parts[:2], Y_BIT, points)
        up_part = over_batch(*mlp_parts[2:], X_BIT, points)
        first_rows = over_chips(
            jnp.concatenate([down_part, up_part], axis=1), ((grad_keys,), (qkv_parts[0],))
        )
        points = ((grad_keys,), (qkv_parts[0],))
        square_send, square_keep, text_send, text_keep, text_part = middle_parts
        text_total = over_chips(text_part, points).astype(jnp.bfloat16)
        square_part = over_batch(square_send, square_keep, Y_BIT, points)
        text_w_part = over_batch(text_send, text_keep, X_BIT, points)
        middle_rows = over_chips(jnp.concatenate([square_part, text_w_part], axis=1))
        plain_send, plain_keep, split_send, split_keep = qkv_parts
        plain_part, split_part = over_batch(plain_send, plain_keep, X_BIT), over_batch(split_send, split_keep, Y_BIT)
        last_rows = over_chips(jnp.concatenate([plain_part, split_part], axis=1))
        plain, split = last_rows[:96], unsplit(last_rows[96:])
        even = lax.axis_index("batch") % 2 == 0
        grads = (
            jnp.where(even, jnp.concatenate([plain, split], axis=1), jnp.concatenate([split, plain], axis=1)),
            unsplit(middle_rows[96:144]),
            unsplit(middle_rows[48:96]),
            middle_rows[144:],
            unsplit(middle_rows[:48]),
            jnp.concatenate([first_rows[192:288], first_rows[288:]], axis=1),
            unsplit(first_rows[:192]),
        )
    else:
        shared = text_terms.reshape(2, items, shards, share_rows, width).transpose(2, 0, 1, 3, 4)
        text_total = lax.psum_scatter(shared, "seq", scatter_dimension=0, tiled=True)
        text_total = text_total.reshape(2, items * share_rows, width)
    text_grad_low = jnp.concatenate([text_total[0], text_total[1]], axis=1)
    grad_text = times_transposed(text_grad_low, w_ckv).reshape(1, items, share_rows, text_width)
    if not fast:
        text_mine = lax.dynamic_slice_in_dim(text[0], position * share_rows, share_rows, 1)
        grads = reduced_grads(
            (hidden_one, grad_projected),
            (attended, grad_branch_one),
            (cross_in, grad_cross_queries),
            (text_mine.reshape(items * share_rows, text_width), text_grad_low),
            (cross_out, grad_branch_two),
            (hidden_two, acts[:-1, 1].transpose(1, 0, 2).reshape(count, -1)),
            (acts[:-1, 0].transpose(1, 0, 2).reshape(count, -1), grad_branch_three),
        )
    return (
        result.astype(jnp.bfloat16)[None],
        grad_inputs[None],
        shares[:, :3][None],
        shares[:, 3:][None],
        grad_text,
        *grads,
    )


def reduced_grads(*pairs):
    def reduce_weight(left, right):
        grad = contract_rows(left, right).astype(jnp.bfloat16)
        part = lax.psum_scatter(grad, "seq", scatter_dimension=0, tiled=True)
        return lax.psum_scatter(part, "batch", scatter_dimension=1, tiled=True).astype(jnp.float32)

    return tuple(reduce_weight(*pair) for pair in pairs)


def solution(mesh):
    in_specs = (
        P("batch", "seq", None),
        P("batch", "seq", None),
        P("batch", None, None, None),
        P("batch", None),
        P("batch", None, None, None),
        P("batch", None),
        P(),
        P(),
        P(),
        P(),
        P(),
        P(),
        P(),
    )
    out_specs = (
        P("batch", "seq", None),
        P("batch", "seq", None),
        P("batch", None, None, "seq"),
        P("batch", None, None, "seq"),
        P("batch", None, "seq", None),
        P("seq", "batch"),
        P("seq", "batch"),
        P("seq", "batch"),
        P("seq", "batch"),
        P("seq", "batch"),
        P("seq", "batch"),
        P("seq", "batch"),
    )
    return jax.shard_map(body, mesh=mesh, in_specs=in_specs, out_specs=out_specs, check_vma=False)
```

time: 461 us -> 323 us (0.70)
  starting transfers between devices: 125 us -> 50.1 us
  waiting for transfers between devices: 99.3 us -> 56.4 us
  matrix products: 38.2 us -> 12.6 us
  Pallas kernels: 120 us -> 106 us
  between operations: 2.58 us -> 15.8 us
  local copies, waits for them, and re-layouts: 41.5 us -> 51.2 us
  other arithmetic: 31.2 us -> 25.2 us
    ppermute x33 -> x23, starting transfers between devices: 94.9 us -> 37.3 us  [trade(): return lax.ppermute(values, axis, [(i, i ^ 1 << bit) for i in range(size)])]
    ppermute x33 -> x23, waiting for transfers between devices: 79 us -> 42.5 us  [trade(): return lax.ppermute(values, axis, [(i, i ^ 1 << bit) for i in range(size)])]
    ppermute x18 -> x4, starting transfers between devices: 26.4 us -> 11.3 us  [the longest x2 8.71 us: hop(): lax.ppermute(below, 'seq', up)]
    ppermute x18 -> x4, waiting for transfers between devices: 20.3 us -> 6.07 us  [the longest x2 4.9 us: hop(): lax.ppermute(above, 'seq', [(j, i) for i, j in up])]
    pallas_call x12, Pallas kernels: 120 us -> 106 us  [the longest x2 20.9 us: attend(): pl.pallas_call(partial(attend_kernel, items, shards, kind, blocks, group)...]
    unnamed x174 -> x180, local copies, waits for them, and re-layouts: 26.7 us -> 40 us
    dot_general x9 -> x0, matrix products: 13.2 us -> none  [the longest x1 7.17 us: body(): pre_act = jnp.dot(hidden_two, w_up, preferred_element_type=jnp.float32)]
    dot_general x7 -> x4, matrix products: 14.6 us -> 3.46 us  [times_transposed(): lax.dot_general(left, right, (((1,), (1,)), ((), ())), preferred_element_...]
  transfers between devices with their start and end apart: 64 -> 38, of which waited for: 22 -> 16; matrix products, arithmetic and copies ran while one was open for 14% -> 17% of each run, Pallas kernels for 14% -> 23%
where the time goes in v2:
time: 323 us; the launch traced here: 317 us
  Pallas kernels  106 us (33%)
  waiting for transfers between devices  56.4 us (17%)
  local copies, waits for them, and re-layouts  51.2 us (16%)
  starting transfers between devices  50.1 us (16%)
  other arithmetic  25.2 us (8%)
  between operations  15.8 us (5%)
  matrix products  12.6 us (4%)
    ppermute x23, waiting for transfers between devices, trade(): return lax.ppermute(values, axis, [(i, i ^ 1 << bit) for i in range(size)])  42.5 us
    unnamed x180, local copies, waits for them, and re-layouts  40 us
    ppermute x23, starting transfers between devices, trade(): return lax.ppermute(values, axis, [(i, i ^ 1 << bit) for i in range(size)])  37.3 us
    pallas_call x2, Pallas kernels, attend(): pl.pallas_call(partial(attend_kernel, items, shards, kind, blocks, group)...  20.9 us
    pallas_call x3, Pallas kernels, pack(): pl.pallas_call(partial(packing, kernel, items, 1 + len(operands), len(row...  18.5 us
    pallas_call x1, Pallas kernels, frame_key_grad(): pl.pallas_call(partial(frame_key_grad_kernel, items, shards, blocks, grou...  16.3 us
    pallas_call x2, Pallas kernels, project(): pl.pallas_call(partial(project_kernel, items, shards, chips), out_shape=(...  14.8 us
    pallas_call x1, Pallas kernels, query_grad(): pl.pallas_call(partial(query_grad_kernel, items, shards, blocks, group),...  12.8 us
  transfers between devices with their start and end apart: 38, of which 16 were waited for; matrix products, arithmetic and copies ran while one was open for 17% of the time, Pallas kernels for 23%

profile of v2, /device:TPU:0, one launch (start us, length us, event | category | flops | bytes accessed | tf_op | source)
XLA Modules:
  0.0 317.1 jit_solution(10474565695282324011)
XLA Ops:
  7.2 5.9 %collective-permute-start = (bf16[256,768]{1,0:T(8,128)(2,1)}, bf16[256,768]{1,0:T(8,128)(2,1)}, u32[]{:S(2)}, u32[]{:S(2)}) collective-permute-start(bf16[256,768]{1,0:T(8,128)(2,1)} %bitcast.146), channel_id=1, source_target_pairs={{0,2},{1,3},{2,4},{3,5},{4,6},{5,7},{8,10},{9,11},{10,12},{11,13},... | collective-permute-start | bytes 1179656 | tf_op jit(solution)/shard_map/ppermute | solution.py:943
  14.6 5.3 %convolution_convert_fusion.k_ref.v_ref = bf16[768,1536]{1,0:T(8,128)(2,1)} fusion(bf16[768,1024]{1,0:T(8,128)(2,1)} %bitcast.153, bf16[1024,1536]{1,0:T(8,128)(2,1)S(1)} %copy-done), kind=kOutput, calls=%fused_computation | convolution fusion | flops 2417098752 | bytes 7077888 | tf_op jit(solution)/shard_map/dot_general | solution.py:996
  21.1 4.8 %collective-permute-done.1.refs_4_ = bf16[256,768]{1,0:T(8,128)(2,1)} collective-permute-done((bf16[256,768]{1,0:T(8,128)(2,1)}, bf16[256,768]{1,0:T(8,128)(2,1)}, u32[]{:S(2)}, u32[]{:S(2)}) %collective-permute-start.1) | collective-permute-done | bytes 393248 | tf_op jit(solution)/shard_map/ppermute | solution.py:943
  26.5 2.8 collective-permute-start.2
  33.6 8.4 %project_near.1 = (bf16[2560,768]{1,0:T(8,128)(2,1)S(1)}, bf16[2560,1536]{1,0:T(8,128)(2,1)}, bf16[256,768]{1,0:T(8,128)(2,1)S(1)}) custom-call(s32[8]{0:T(128)S(1)} %pad_add_fusion.meta.refs_0_, f32[3,6,768]{2,1,0:T(8,128)S(1)} %bitcast.156, bf16[768,2304]{1,0:T(8,128)(2,1)S(1)} %copy-done.4, bf16[256,768]{1,0:T(8,128)(2,1)S(1)} %bitcast.149, ...), custom_call_target="tpu_custom_call" | custom-call | flops 2717908992 | bytes 9437184 | tf_op jit(solution)/shard_map/project_near/pallas_call | solution.py:269
  44.4 6.4 %project_far.1 = (bf16[2560,768]{1,0:T(8,128)(2,1)S(1)}, bf16[2560,1536]{1,0:T(8,128)(2,1)}, bf16[256,768]{1,0:T(8,128)(2,1)}) custom-call(s32[8]{0:T(128)S(1)} %pad_add_fusion.meta.refs_0_, f32[3,6,768]{2,1,0:T(8,128)S(1)} %bitcast.158, bf16[768,2304]{1,0:T(8,128)(2,1)S(1)} %copy-done.4, ...), custom_call_target="tpu_custom_call", output_to_operand_aliasing={{0}: (7, {}), {1}: (8, {})} | custom-call | flops 1811939328 | bytes 6291456 | tf_op jit(solution)/shard_map/project_far/pallas_call | solution.py:269
  50.9 14.6 %self_attend.1 = (f32[256,768]{1,0:T(8,128)S(1)}, bf16[256,768]{1,0:T(8,128)(2,1)S(1)}, bf16[256,128]{1,0:T(8,128)(2,1)S(1)}) custom-call(s32[8]{0:T(128)S(1)} %pad_add_fusion.meta.refs_0_, bf16[2560,768]{1,0:T(8,128)(2,1)S(1)} %get-tuple-element.76.q_ref, bf16[2560,1536]{1,0:T(8,128)(2,1)} %get-tuple-element.77.k_ref.v_ref, ...), custom_call_target="tpu_custom_call" | custom-call | flops 1006632960 | bytes 7864320 | tf_op jit(solution)/shard_map/self_attend/pallas_call | solution.py:375
  68.9 6.3 %cross_attend.1 = (f32[256,768]{1,0:T(8,128)S(1)}, bf16[256,768]{1,0:T(8,128)(2,1)S(1)}, bf16[256,128]{1,0:T(8,128)(2,1)S(1)}) custom-call(s32[8]{0:T(128)S(1)} %pad_add_fusion.meta.refs_0_, bf16[256,768]{1,0:T(8,128)(2,1)S(1)} %fusion.2.q_ref, bf16[768,1536]{1,0:T(8,128)(2,1)S(1)} %copy-done.3, bf16[768,1536]{1,0:T(8,128)(2,1)S(1)} %copy-done.3), custom_call_target="tpu_custom_call" | custom-call | flops 301989888 | bytes 2359296 | tf_op jit(solution)/shard_map/cross_attend/pallas_call | solution.py:375
  77.6 2.6 copy-done.46
  80.2 8.5 %mlp.1 = (bf16[5,2,256,768]{3,2,1,0:T(8,128)(2,1)S(1)}, f32[256,768]{1,0:T(8,128)S(1)}, f32[256,768]{1,0:T(8,128)S(1)}) custom-call(bf16[256,768]{1,0:T(8,128)(2,1)S(1)} %get-tuple-element.172.h_ref, bf16[256,768]{1,0:T(8,128)(2,1)S(1)} %get-tuple-element.209.d_ref, bf16[768,3072]{1,0:T(8,128)(2,1)S(1)} %copy-done.46, bf16[3072,768]{1,0:T(8,128)(2,1)} %down_ref.1), custom_call_target="tpu_custom_call" | custom-call | flops 4831838208 | bytes 12582912 | tf_op jit(solution)/shard_map/mlp/pallas_call | solution.py:680
  90.8 4.9 %collective-permute-done.10.refs_2_ = bf16[5,2,256,768]{3,2,1,0:T(8,128)(2,1)} collective-permute-done((bf16[5,2,256,768]{3,2,1,0:T(8,128)(2,1)S(1)}, bf16[5,2,256,768]{3,2,1,0:T(8,128)(2,1)}, u32[]{:S(2)}, u32[]{:S(2)}) %collective-permute-start.10) | collective-permute-done | bytes 3932192 | tf_op jit(solution)/shard_map/ppermute | solution.py:992
  95.7 7.8 %pack_mlp.1 = (bf16[2,4,192,384]{3,2,1,0:T(8,128)(2,1)S(1)}, bf16[2,4,192,384]{3,2,1,0:T(8,128)(2,1)S(1)}, bf16[2,4,192,384]{3,2,1,0:T(8,128)(2,1)S(1)}, bf16[2,4,192,384]{3,2,1,0:T(8,128)(2,1)S(1)}) custom-call(s32[8]{0:T(128)S(1)} %pad_add_fusion.meta.refs_0_, bf16[5,2,256,768]{3,2,1,0:T(8,128)(2,1)} %copy-done.47, ...), custom_call_target="tpu_custom_call" | custom-call | flops 2415919104 | bytes 12582912 | tf_op jit(solution)/shard_map/pack_mlp/pallas_call | solution.py:878
  107.8 9.3 %cross_grad.1 = (bf16[256,768]{1,0:T(8,128)(2,1)S(1)}, bf16[2,768,768]{2,1,0:T(8,128)(2,1)S(1)}) custom-call(s32[8]{0:T(128)S(1)} %pad_add_fusion.meta.refs_0_, bf16[256,768]{1,0:T(8,128)(2,1)S(1)} %fusion.2.q_ref, bf16[256,768]{1,0:T(8,128)(2,1)S(1)} %convolution_convert_fusion.2.do_ref, bf16[256,128]{1,0:T(8,128)(2,1)S(1)} %fusion.33.f_ref, ...), custom_call_target="tpu_custom_call" | custom-call | flops 704643072 | bytes 4718592 | tf_op jit(solution)/shard_map/cross_grad/pallas_call | solution.py:612
  134.0 2.7 collective-permute-start.33
  136.8 12.8 %self_query_grad.1 = bf16[256,768]{1,0:T(8,128)(2,1)S(1)} custom-call(s32[8]{0:T(128)S(1)} %pad_add_fusion.meta.refs_0_, bf16[2560,768]{1,0:T(8,128)(2,1)S(1)} %copy-done.2, bf16[256,768]{1,0:T(8,128)(2,1)S(1)} %convolution_convert_fusion.1.do_ref, bf16[256,128]{1,0:T(8,128)(2,1)S(1)} %copy-done.41, bf16[2560,1536]{1,0:T(8,128)(2,1)} %get-tuple-element.77.k_ref.v_ref, ...), custom_call_target="tpu_custom_call" | custom-call | flops 1509949440 | bytes 7864320 | tf_op jit(solution)/shard_map/self_query_grad/pallas_call | solution.py:464
  149.6 5.2 %collective-permute-done.31 = bf16[2,4,192,384]{3,2,1,0:T(8,128)(2,1)S(1)} collective-permute-done((bf16[2,4,192,384]{3,2,1,0:T(8,128)(2,1)}, bf16[2,4,192,384]{3,2,1,0:T(8,128)(2,1)S(1)}, u32[]{:S(2)}, u32[]{:S(2)}) %collective-permute-start.31) | collective-permute-done | bytes 1179680 | tf_op jit(solution)/shard_map/ppermute | solution.py:897
  157.5 6.3 %collective-permute-done.33 = bf16[2,4,192,384]{3,2,1,0:T(8,128)(2,1)S(1)} collective-permute-done((bf16[2,4,192,384]{3,2,1,0:T(8,128)(2,1)}, bf16[2,4,192,384]{3,2,1,0:T(8,128)(2,1)S(1)}, u32[]{:S(2)}, u32[]{:S(2)}) %collective-permute-start.33) | collective-permute-done | bytes 1179680 | tf_op jit(solution)/shard_map/ppermute | solution.py:897
  167.8 7.8 %pack_middle.1 = (bf16[2,4,144,384]{3,2,1,0:T(8,128)(2,1)}, bf16[2,4,144,384]{3,2,1,0:T(8,128)(2,1)S(1)}, bf16[2,4,128,384]{3,2,1,0:T(8,128)(2,1)S(1)}, bf16[2,4...) custom-call(s32[8]{0:T(128)S(1)} %pad_add_fusion.meta.refs_0_, ...), custom_call_target="tpu_custom_call" | custom-call | flops 1711276032 | bytes 14352384 | tf_op jit(solution)/shard_map/pack_middle/pallas_call | solution.py:878
  178.9 2.9 collective-permute-done.34
  186.4 2.1 copy.59
  190.6 2.3 slice_bitcast_fusion.5
  197.0 16.3 %self_key_grad.1 = (bf16[256,768]{1,0:T(8,128)(2,1)S(1)}, bf16[256,768]{1,0:T(8,128)(2,1)S(1)}) custom-call(s32[8]{0:T(128)S(1)} %pad_add_fusion.meta.refs_0_, bf16[2560,768]{1,0:T(8,128)(2,1)} %copy-done.1, bf16[2560,1536]{1,0:T(8,128)(2,1)} %get-tuple-element.77.k_ref.v_ref, bf16[2560,1536]{1,0:T(8,128)(2,1)} %get-tuple-element.77.k_ref.v_ref, ...), custom_call_target="tpu_custom_call" | custom-call | flops 2013265920 | bytes 7864320 | tf_op jit(solution)/shard_map/self_key_grad/pallas_call | solution.py:545
  215.6 12.8 %collective-permute-start.36 = (bf16[384,384]{0,1:T(8,128)(2,1)S(1)}, bf16[384,384]{0,1:T(8,128)(2,1)S(1)}, u32[]{:S(2)}, u32[]{:S(2)}) collective-permute-start(bf16[384,384]{0,1:T(8,128)(2,1)S(1)} %get-tuple-element.193), channel_id=1, source_target_pairs={{0,4},{1,5},{2,6},{3,7},{4,0},{5,1},{6,2},{7,3},{8,12},{9,13},{10,... | collective-permute-start | bytes 884744 | tf_op jit(solution)/shard_map/ppermute | solution.py:897
  236.8 2.9 pack_qkv.1
  256.2 4.8 %finish.1 = (f32[256,768]{1,0:T(8,128)}, f32[6,8,768]{2,1,0:T(8,128)S(1)}) custom-call(s32[8]{0:T(128)S(1)} %pad_add_fusion.meta.refs_0_, f32[3,6,768]{2,1,0:T(8,128)S(1)} %bitcast.159, bf16[768,2304]{1,0:T(8,128)(2,1)S(1)} %copy-done.5, bf16[256,2304]{1,0:T(8,128)(2,1)S(1)} %copy-done.10, bf16[256,768]{1,0:T(8,128)(2,1)S(1)} %bitcast.150, ...), custom_call_target="tpu_custom_call" | custom-call | flops 905969664 | bytes 9437184 | tf_op jit(solution)/shard_map/finish/pallas_call | solution.py:751
  266.7 3.5 %collective-permute-done.15 = f32[6,8,768]{2,1,0:T(8,128)S(1)} collective-permute-done((f32[6,8,768]{2,1,0:T(8,128)S(1)}, f32[6,8,768]{2,1,0:T(8,128)S(1)}, u32[]{:S(2)}, u32[]{:S(2)}) %collective-permute-start.15) | collective-permute-done | bytes 147488 | tf_op jit(solution)/shard_map/ppermute | solution.py:897
  270.3 2.4 collective-permute-start.16
  273.5 12.1 %collective-permute-done.16 = f32[6,8,768]{2,1,0:T(8,128)S(1)} collective-permute-done((f32[6,8,768]{2,1,0:T(8,128)S(1)}, f32[6,8,768]{2,1,0:T(8,128)S(1)}, u32[]{:S(2)}, u32[]{:S(2)}) %collective-permute-start.16) | collective-permute-done | bytes 147488 | tf_op jit(solution)/shard_map/ppermute | solution.py:897
  290.8 4.2 %collective-permute-done.20 = bf16[4,96,384]{2,1,0:T(8,128)(2,1)S(1)} collective-permute-done((bf16[4,96,384]{2,1,0:T(8,128)(2,1)S(1)}, bf16[4,96,384]{2,1,0:T(8,128)(2,1)S(1)}, u32[]{:S(2)}, u32[]{:S(2)}) %collective-permute-start.20) | collective-permute-done | bytes 294944 | tf_op jit(solution)/shard_map/ppermute | solution.py:897
  298.0 3.4 %collective-permute-done.23 = bf16[2,144,384]{2,1,0:T(8,128)(2,1)S(1)} collective-permute-done((bf16[2,144,384]{2,1,0:T(8,128)(2,1)S(1)}, bf16[2,144,384]{2,1,0:T(8,128)(2,1)S(1)}, u32[]{:S(2)}, u32[]{:S(2)}) %collective-permute-start.23) | collective-permute-done | bytes 221216 | tf_op jit(solution)/shard_map/ppermute | solution.py:897
  301.4 3.4 %collective-permute-start.24 = (bf16[144,384]{1,0:T(8,128)(2,1)S(1)}, bf16[144,384]{1,0:T(8,128)(2,1)S(1)}, u32[]{:S(2)}, u32[]{:S(2)}) collective-permute-start(bf16[144,384]{1,0:T(8,128)(2,1)S(1)} %slice_bitcast_fusion.26), channel_id=1, source_target_pairs={{0,4},{1,5},{2,6},{3,7},{4,0},{5,1},{6,2},{7,3},{8,12},{9,13},{10,... | collective-permute-start | bytes 331784 | tf_op jit(solution)/shard_map/ppermute | solution.py:897
  305.5 3.4 %collective-permute-done.24 = bf16[144,384]{1,0:T(8,128)(2,1)S(1)} collective-permute-done((bf16[144,384]{1,0:T(8,128)(2,1)S(1)}, bf16[144,384]{1,0:T(8,128)(2,1)S(1)}, u32[]{:S(2)}, u32[]{:S(2)}) %collective-permute-start.24) | collective-permute-done | bytes 110624 | tf_op jit(solution)/shard_map/ppermute | solution.py:897
  (329 shorter events, 102.3 us)
Async XLA Ops:
  7.2 187.7 %all-gather.2.cloned.1.call-start = ((), (), s32[]{:S(2)}) async-start(), calls=%async_computation | async-start | bytes 4128768 | tf_op jit(solution)/shard_map/all_gather | solution.py:1062
  7.2 13.9 %collective-permute-start = (bf16[256,768]{1,0:T(8,128)(2,1)}, bf16[256,768]{1,0:T(8,128)(2,1)}, u32[]{:S(2)}, u32[]{:S(2)}) collective-permute-start(bf16[256,768]{1,0:T(8,128)(2,1)} %bitcast.146), channel_id=1, source_target_pairs={{0,2},{1,3},{2,4},{3,5},{4,6},{5,7},{8,10},{9,11},{10,12},{11,13},... | collective-permute-start | bytes 1179656 | tf_op jit(solution)/shard_map/ppermute | solution.py:943
  13.2 12.8 %collective-permute-start.1 = (bf16[256,768]{1,0:T(8,128)(2,1)}, bf16[256,768]{1,0:T(8,128)(2,1)}, u32[]{:S(2)}, u32[]{:S(2)}) collective-permute-start(bf16[256,768]{1,0:T(8,128)(2,1)} %bitcast.147), channel_id=1, source_target_pairs={{2,0},{3,1},{4,2},{5,3},{6,4},{7,5},{10,8},{11,9},{12,10},{13,11},... | collective-permute-start | bytes 1179656 | tf_op jit(solution)/shard_map/ppermute | solution.py:943
  14.5 17.1 %collective-permute-start.4 = (bf16[256,768]{1,0:T(8,128)(2,1)}, bf16[256,768]{1,0:T(8,128)(2,1)}, u32[]{:S(2)}, u32[]{:S(2)}) collective-permute-start(bf16[256,768]{1,0:T(8,128)(2,1)} %bitcast.148), channel_id=1, source_target_pairs={{0,1},{1,0},{2,3},{3,2},{4,5},{5,4},{6,7},{7,6},{8,9},{9,8},{10,11... | collective-permute-start | bytes 1179656 | tf_op jit(solution)/shard_map/ppermute | solution.py:992
  26.5 15.6 %collective-permute-start.2 = (bf16[256,768]{1,0:T(8,128)(2,1)}, bf16[256,768]{1,0:T(8,128)(2,1)S(1)}, u32[]{:S(2)}, u32[]{:S(2)}) collective-permute-start(bf16[256,768]{1,0:T(8,128)(2,1)} %collective-permute-done.refs_2_), channel_id=1, source_target_pairs={{0,2},{1,3},{2,4},{3,5},{4,6},{5,7},{8,10},{9,11},{10,12},{11,13},... | collective-permute-start | bytes 1179656 | tf_op jit(solution)/shard_map/ppermute | solution.py:943
  29.2 12.8 %collective-permute-start.3 = (bf16[256,768]{1,0:T(8,128)(2,1)}, bf16[256,768]{1,0:T(8,128)(2,1)S(1)}, u32[]{:S(2)}, u32[]{:S(2)}) collective-permute-start(bf16[256,768]{1,0:T(8,128)(2,1)} %collective-permute-done.1.refs_4_), channel_id=1, source_target_pairs={{2,0},{3,1},{4,2},{5,3},{6,4},{7,5},{10,8},{11,9},{12,10},{13,11},... | collective-permute-start | bytes 1179656 | tf_op jit(solution)/shard_map/ppermute | solution.py:943
  42.7 22.8 %collective-permute-start.9 = (bf16[256,768]{1,0:T(8,128)(2,1)S(1)}, bf16[256,768]{1,0:T(8,128)(2,1)S(1)}, u32[]{:S(2)}, u32[]{:S(2)}) collective-permute-start(bf16[256,768]{1,0:T(8,128)(2,1)S(1)} %get-tuple-element.79.refs_1_), channel_id=1, source_target_pairs={{0,1},{1,0},{2,3},{3,2},{4,5},{5,4},{6,7},{7,6},{8,9},{9,8},{10,11... | collective-permute-start | bytes 1179656 | tf_op jit(solution)/shard_map/ppermute | solution.py:992
  88.7 7.0 %collective-permute-start.10 = (bf16[5,2,256,768]{3,2,1,0:T(8,128)(2,1)S(1)}, bf16[5,2,256,768]{3,2,1,0:T(8,128)(2,1)}, u32[]{:S(2)}, u32[]{:S(2)}) collective-permute-start(bf16[5,2,256,768]{3,2,1,0:T(8,128)(2,1)S(1)} %get-tuple-element.84.refs_1_), channel_id=1, source_target_pairs={{0,1},{1,0},{2,3},{3,2},{4,5},{5,4},{6,7},{7,6},{8,9},{9,8},{10,11... | collective-permute-start | bytes 11796488 | tf_op jit(solution)/shard_map/ppermute | solution.py:992
  126.5 28.2 %collective-permute-start.31 = (bf16[2,4,192,384]{3,2,1,0:T(8,128)(2,1)}, bf16[2,4,192,384]{3,2,1,0:T(8,128)(2,1)S(1)}, u32[]{:S(2)}, u32[]{:S(2)}) collective-permute-start(bf16[2,4,192,384]{3,2,1,0:T(8,128)(2,1)} %copy-done.49), channel_id=1, source_target_pairs={{0,16},{8,24},{16,0},{24,8},{1,17},{9,25},{17,1},{25,9},{2,18},{10... | collective-permute-start | bytes 3538952 | tf_op jit(solution)/shard_map/ppermute | solution.py:897
  133.9 32.5 %collective-permute-start.12 = (bf16[6,256,768]{2,1,0:T(8,128)(2,1)}, bf16[6,256,768]{2,1,0:T(8,128)(2,1)}, u32[]{:S(2)}, u32[]{:S(2)}) collective-permute-start(bf16[6,256,768]{2,1,0:T(8,128)(2,1)} %bitcast_dynamic-update-slice_fusion.refs_1_), channel_id=1, source_target_pairs={{0,1},{1,0},{2,3},{3,2},{4,5},{5,4},{6,7},{7,6},{8,9},{9,8},{10,11... | collective-permute-start | bytes 7077896 | tf_op jit(solution)/shard_map/ppermute | solution.py:992
  134.0 29.7 %collective-permute-start.33 = (bf16[2,4,192,384]{3,2,1,0:T(8,128)(2,1)}, bf16[2,4,192,384]{3,2,1,0:T(8,128)(2,1)S(1)}, u32[]{:S(2)}, u32[]{:S(2)}) collective-permute-start(bf16[2,4,192,384]{3,2,1,0:T(8,128)(2,1)} %copy-done.48), channel_id=1, source_target_pairs={{0,8},{8,0},{16,24},{24,16},{1,9},{9,1},{17,25},{25,17},{2,10},{10... | collective-permute-start | bytes 3538952 | tf_op jit(solution)/shard_map/ppermute | solution.py:897
  156.2 21.3 %collective-permute-start.32 = (bf16[4,192,384]{2,1,0:T(8,128)(2,1)}, bf16[4,192,384]{2,1,0:T(8,128)(2,1)}, u32[]{:S(2)}, u32[]{:S(2)}) collective-permute-start(bf16[4,192,384]{2,1,0:T(8,128)(2,1)} %get-tuple-element.179), channel_id=1, source_target_pairs={{0,8},{8,0},{16,24},{24,16},{1,9},{9,1},{17,25},{25,17},{2,10},{10... | collective-permute-start | bytes 1769480 | tf_op jit(solution)/shard_map/ppermute | solution.py:897
  165.3 16.6 %collective-permute-start.34 = (bf16[4,192,384]{2,1,0:T(8,128)(2,1)}, bf16[4,192,384]{2,1,0:T(8,128)(2,1)}, u32[]{:S(2)}, u32[]{:S(2)}) collective-permute-start(bf16[4,192,384]{2,1,0:T(8,128)(2,1)} %get-tuple-element.181), channel_id=1, source_target_pairs={{0,16},{8,24},{16,0},{24,8},{1,17},{9,25},{17,1},{25,9},{2,18},{10... | collective-permute-start | bytes 1769480 | tf_op jit(solution)/shard_map/ppermute | solution.py:897
  176.5 51.9 %collective-permute-start.25 = (bf16[2,4,144,384]{3,2,1,0:T(8,128)(2,1)}, bf16[2,4,144,384]{3,2,1,0:T(8,128)(2,1)}, u32[]{:S(2)}, u32[]{:S(2)}) collective-permute-start(bf16[2,4,144,384]{3,2,1,0:T(8,128)(2,1)} %get-tuple-element.97), channel_id=1, source_target_pairs={{0,16},{8,24},{16,0},{24,8},{1,17},{9,25},{17,1},{25,9},{2,18},{10... | collective-permute-start | bytes 2654216 | tf_op jit(solution)/shard_map/ppermute | solution.py:897
  188.6 24.9 %collective-permute-start.35 = (bf16[2,384,384]{1,2,0:T(8,128)(2,1)}, bf16[2,384,384]{1,2,0:T(8,128)(2,1)}, u32[]{:S(2)}, u32[]{:S(2)}) collective-permute-start(bf16[2,384,384]{1,2,0:T(8,128)(2,1)} %bitcast.166), channel_id=1, source_target_pairs={{0,2},{1,3},{2,0},{3,1},{4,6},{5,7},{6,4},{7,5},{8,10},{9,11},{10,... | collective-permute-start | bytes 1769480 | tf_op jit(solution)/shard_map/ppermute | solution.py:897
  188.6 41.4 %collective-permute-start.27 = (bf16[2,4,128,384]{3,2,1,0:T(8,128)(2,1)}, bf16[2,4,128,384]{3,2,1,0:T(8,128)(2,1)}, u32[]{:S(2)}, u32[]{:S(2)}) collective-permute-start(bf16[2,4,128,384]{3,2,1,0:T(8,128)(2,1)} %copy-done.50), channel_id=1, source_target_pairs={{0,8},{8,0},{16,24},{24,16},{1,9},{9,1},{17,25},{25,17},{2,10},{10... | collective-permute-start | bytes 2359304 | tf_op jit(solution)/shard_map/ppermute | solution.py:897
  192.9 39.5 %collective-permute-start.17 = (bf16[2,2,96,768]{3,2,1,0:T(8,128)(2,1)}, bf16[2,2,96,768]{3,2,1,0:T(8,128)(2,1)}, u32[]{:S(2)}, u32[]{:S(2)}) collective-permute-start(bf16[2,2,96,768]{3,2,1,0:T(8,128)(2,1)} %get-tuple-element.183), channel_id=1, source_target_pairs={{0,2},{1,3},{2,0},{3,1},{4,6},{5,7},{6,4},{7,5},{8,10},{9,11},{10,... | collective-permute-start | bytes 1769480 | tf_op jit(solution)/shard_map/ppermute | solution.py:897
  213.4 23.1 %collective-permute-start.13 = (bf16[3,256,768]{2,1,0:T(8,128)(2,1)S(1)}, bf16[3,256,768]{2,1,0:T(8,128)(2,1)S(1)}, u32[]{:S(2)}, u32[]{:S(2)}) collective-permute-start(bf16[3,256,768]{2,1,0:T(8,128)(2,1)S(1)} %pad_maximum_fusion.1.refs_3_), channel_id=1, source_target_pairs={{0,1},{1,0},{2,3},{3,2},{4,5},{5,4},{6,7},{7,6},{8,9},{9,8},{10,11... | collective-permute-start | bytes 3538952 | tf_op jit(solution)/shard_map/ppermute | solution.py:992
  215.6 26.5 %collective-permute-start.36 = (bf16[384,384]{0,1:T(8,128)(2,1)S(1)}, bf16[384,384]{0,1:T(8,128)(2,1)S(1)}, u32[]{:S(2)}, u32[]{:S(2)}) collective-permute-start(bf16[384,384]{0,1:T(8,128)(2,1)S(1)} %get-tuple-element.193), channel_id=1, source_target_pairs={{0,4},{1,5},{2,6},{3,7},{4,0},{5,1},{6,2},{7,3},{8,12},{9,13},{10,... | collective-permute-start | bytes 884744 | tf_op jit(solution)/shard_map/ppermute | solution.py:897
  229.9 12.5 %collective-permute-start.26 = (bf16[4,144,384]{2,1,0:T(8,128)(2,1)S(1)}, bf16[4,144,384]{2,1,0:T(8,128)(2,1)S(1)}, u32[]{:S(2)}, u32[]{:S(2)}) collective-permute-start(bf16[4,144,384]{2,1,0:T(8,128)(2,1)S(1)} %get-tuple-element.185), channel_id=1, source_target_pairs={{0,8},{8,0},{16,24},{24,16},{1,9},{9,1},{17,25},{25,17},{2,10},{10... | collective-permute-start | bytes 1327112 | tf_op jit(solution)/shard_map/ppermute | solution.py:897
  232.4 10.5 %collective-permute-start.28 = (bf16[4,128,384]{2,1,0:T(8,128)(2,1)S(1)}, bf16[4,128,384]{2,1,0:T(8,128)(2,1)S(1)}, u32[]{:S(2)}, u32[]{:S(2)}) collective-permute-start(bf16[4,128,384]{2,1,0:T(8,128)(2,1)S(1)} %get-tuple-element.187), channel_id=1, source_target_pairs={{0,16},{8,24},{16,0},{24,8},{1,17},{9,25},{17,1},{25,9},{2,18},{10... | collective-permute-start | bytes 1179656 | tf_op jit(solution)/shard_map/ppermute | solution.py:897
  235.4 12.9 %collective-permute-start.18 = (bf16[2,96,768]{2,1,0:T(8,128)(2,1)}, bf16[2,96,768]{2,1,0:T(8,128)(2,1)}, u32[]{:S(2)}, u32[]{:S(2)}) collective-permute-start(bf16[2,96,768]{2,1,0:T(8,128)(2,1)} %get-tuple-element.195), channel_id=1, source_target_pairs={{0,4},{1,5},{2,6},{3,7},{4,0},{5,1},{6,2},{7,3},{8,12},{9,13},{10,... | collective-permute-start | bytes 884744 | tf_op jit(solution)/shard_map/ppermute | solution.py:897
  239.8 47.1 %collective-permute-start.19 = (bf16[2,4,96,384]{3,2,1,0:T(8,128)(2,1)}, bf16[2,4,96,384]{3,2,1,0:T(8,128)(2,1)}, u32[]{:S(2)}, u32[]{:S(2)}) collective-permute-start(bf16[2,4,96,384]{3,2,1,0:T(8,128)(2,1)} %get-tuple-element.101), channel_id=1, source_target_pairs={{0,8},{8,0},{16,24},{24,16},{1,9},{9,1},{17,25},{25,17},{2,10},{10... | collective-permute-start | bytes 1769480 | tf_op jit(solution)/shard_map/ppermute | solution.py:897
  248.0 24.7 %collective-permute-start.29 = (bf16[2,272,384]{2,1,0:T(8,128)(2,1)S(1)}, bf16[2,272,384]{2,1,0:T(8,128)(2,1)S(1)}, u32[]{:S(2)}, u32[]{:S(2)}) collective-permute-start(bf16[2,272,384]{2,1,0:T(8,128)(2,1)S(1)} %slice_bitcast_fusion.8), channel_id=1, source_target_pairs={{0,2},{1,3},{2,0},{3,1},{4,6},{5,7},{6,4},{7,5},{8,10},{9,11},{10,... | collective-permute-start | bytes 1253384 | tf_op jit(solution)/shard_map/ppermute | solution.py:897
  248.0 17.7 %collective-permute-start.21 = (bf16[2,4,48,384]{3,2,1,0:T(8,128)(2,1)}, bf16[2,4,48,384]{3,2,1,0:T(8,128)(2,1)S(1)}, u32[]{:S(2)}, u32[]{:S(2)}) collective-permute-start(bf16[2,4,48,384]{3,2,1,0:T(8,128)(2,1)} %copy-done.55), channel_id=1, source_target_pairs={{0,16},{8,24},{16,0},{24,8},{1,17},{9,25},{17,1},{25,9},{2,18},{10... | collective-permute-start | bytes 884744 | tf_op jit(solution)/shard_map/ppermute | solution.py:897
  263.7 6.5 %collective-permute-start.15 = (f32[6,8,768]{2,1,0:T(8,128)S(1)}, f32[6,8,768]{2,1,0:T(8,128)S(1)}, u32[]{:S(2)}, u32[]{:S(2)}) collective-permute-start(f32[6,8,768]{2,1,0:T(8,128)S(1)} %add.181), channel_id=1, source_target_pairs={{0,2},{1,3},{2,0},{3,1},{4,6},{5,7},{6,4},{7,5},{8,10},{9,11},{10,... | collective-permute-start | bytes 442376 | tf_op jit(solution)/shard_map/ppermute | solution.py:897
  265.8 7.6 %collective-permute-start.22 = (bf16[4,48,384]{2,1,0:T(8,128)(2,1)S(1)}, bf16[4,48,384]{2,1,0:T(8,128)(2,1)S(1)}, u32[]{:S(2)}, u32[]{:S(2)}) collective-permute-start(bf16[4,48,384]{2,1,0:T(8,128)(2,1)S(1)} %slice_bitcast_fusion.22), channel_id=1, source_target_pairs={{0,8},{8,0},{16,24},{24,16},{1,9},{9,1},{17,25},{25,17},{2,10},{10... | collective-permute-start | bytes 442376 | tf_op jit(solution)/shard_map/ppermute | solution.py:897
  270.3 15.3 %collective-permute-start.16 = (f32[6,8,768]{2,1,0:T(8,128)S(1)}, f32[6,8,768]{2,1,0:T(8,128)S(1)}, u32[]{:S(2)}, u32[]{:S(2)}) collective-permute-start(f32[6,8,768]{2,1,0:T(8,128)S(1)} %add.182), channel_id=1, source_target_pairs={{0,4},{1,5},{2,6},{3,7},{4,0},{5,1},{6,2},{7,3},{8,12},{9,13},{10,... | collective-permute-start | bytes 442376 | tf_op jit(solution)/shard_map/ppermute | solution.py:897
  272.8 17.2 %collective-permute-start.30 = (bf16[272,384]{1,0:T(8,128)(2,1)S(1)}, bf16[272,384]{1,0:T(8,128)(2,1)S(1)}, u32[]{:S(2)}, u32[]{:S(2)}) collective-permute-start(bf16[272,384]{1,0:T(8,128)(2,1)S(1)} %slice_bitcast_fusion.20), channel_id=1, source_target_pairs={{0,4},{1,5},{2,6},{3,7},{4,0},{5,1},{6,2},{7,3},{8,12},{9,13},{10,... | collective-permute-start | bytes 626696 | tf_op jit(solution)/shard_map/ppermute | solution.py:897
  288.1 6.9 %collective-permute-start.20 = (bf16[4,96,384]{2,1,0:T(8,128)(2,1)S(1)}, bf16[4,96,384]{2,1,0:T(8,128)(2,1)S(1)}, u32[]{:S(2)}, u32[]{:S(2)}) collective-permute-start(bf16[4,96,384]{2,1,0:T(8,128)(2,1)S(1)} %slice_bitcast_fusion.14), channel_id=1, source_target_pairs={{0,16},{8,24},{16,0},{24,8},{1,17},{9,25},{17,1},{25,9},{2,18},{10... | collective-permute-start | bytes 884744 | tf_op jit(solution)/shard_map/ppermute | solution.py:897
  295.2 6.1 %collective-permute-start.23 = (bf16[2,144,384]{2,1,0:T(8,128)(2,1)S(1)}, bf16[2,144,384]{2,1,0:T(8,128)(2,1)S(1)}, u32[]{:S(2)}, u32[]{:S(2)}) collective-permute-start(bf16[2,144,384]{2,1,0:T(8,128)(2,1)S(1)} %slice_bitcast_fusion.18), channel_id=1, source_target_pairs={{0,2},{1,3},{2,0},{3,1},{4,6},{5,7},{6,4},{7,5},{8,10},{9,11},{10,... | collective-permute-start | bytes 663560 | tf_op jit(solution)/shard_map/ppermute | solution.py:897
  301.4 7.5 %collective-permute-start.24 = (bf16[144,384]{1,0:T(8,128)(2,1)S(1)}, bf16[144,384]{1,0:T(8,128)(2,1)S(1)}, u32[]{:S(2)}, u32[]{:S(2)}) collective-permute-start(bf16[144,384]{1,0:T(8,128)(2,1)S(1)} %slice_bitcast_fusion.26), channel_id=1, source_target_pairs={{0,4},{1,5},{2,6},{3,7},{4,0},{5,1},{6,2},{7,3},{8,12},{9,13},{10,... | collective-permute-start | bytes 331784 | tf_op jit(solution)/shard_map/ppermute | solution.py:897
  (91 other events, 586.7 us)
Sparse Core Ops, SparseCore 0:
  124.8 48.4 all-gather.1
